TPU v7x, 128 devices: a whole 4x4x4 slice. The times are simulated.
128 devices in a mesh: row: 4 (over y), col: 8 (over x, core), seq: 4 (over z).
Axes of the slice: x: 4, y: 4, z: 4, core: 2. Of those that a mesh axis runs over, the one named last changes fastest.
Arguments:
- hidden_in: bfloat16 [4, 48, 8192], P(None, None, 'row'), may hold values from -80 to 80, as said below
- norm_gain: bfloat16 [8192], replicated, may hold values from 0.099609375 to 1.8984375
- w_qkv: bfloat16 [8192, 10240], P('row', 'col'), may hold values from -0.0625 to 0.0625
- w_out: bfloat16 [8192, 8192], P('col', 'row'), may hold values from -0.0625 to 0.0625
- kv_pool: bfloat16 [4096, 2, 64, 1024], P(('row', 'seq'), None, None, 'col'), may hold values from -70 to 70, as said below
- page_owner: int32 [4096], replicated, may hold values from -1 to 51, as said below
- page_fill: int32 [4096], replicated, may hold values from 0 to 64, as said below
- lengths: int32 [48], replicated, may hold values from 65 to 16896, as said below
- group_of_request: int32 [48], replicated, may hold values from 0 to 3, as said below
- migrate_dest: int32 [4096], replicated, may hold values from 0 to 15, as said below
Outputs:
- layer_out: bfloat16 [4, 48, 8192], P(None, 'seq', ('row', 'col'))
- new_kv: bfloat16 [4, 48, 2, 1024], P(None, 'seq', None, 'col')
- new_pool: bfloat16 [4096, 2, 64, 1024], P(('row', 'seq'), None, None, 'col')
Inputs may be any that keep to these rules, and one draw needn't show every extreme that they name: `hidden_in`: drawn values. `kv_pool`: drawn values. `page_owner`: A shared prompt of a group owns up to 256 pages and a request up to 8 own pages; a page's valid tokens lead, only the last page of an owner is partly filled; within each block of 256 slots the non-empty slots come first, at most 128 of them, and some block holds exactly that many. `page_fill`: 0 exactly for empty slots. `lengths`: equals the valid tokens of the request's pages and of its group's prompt pages. `group_of_request`: each group has 1 to 16 requests, some group exactly 16. `migrate_dest`: each block of 256 slots names every destination exactly 16 times.
All inputs are finite; a program needn't handle non-finite values.
Results may differ from a plain program's by a relative error of at most 0.02.
Values may be sent and summed in bfloat16 or wider, within the bound.
No kernel may reach another device: no remote copies, remote signals or barrier semaphores. Data moves between devices by JAX's collectives and lax.ppermute only.
A program may use at most 192 MiB of HBM per device.

v0:
```python
import functools

import jax
import jax.numpy as jnp
from jax import lax
from jax.experimental import pallas as pl
from jax.experimental.pallas import tpu as pltpu
from jax.sharding import PartitionSpec as P

HEADS = 64
KV_HEADS = 8
HEAD = 128
GROUPS = 4
MEM = 16


EPS = 1e-06
THETA = 1000000.0
NEG = -1e30


def ring(axis, step):
    size = lax.axis_size(axis)
    return [(k, (k + step) % size) for k in range(size)]


def exchanged(parts, axis):
    size = lax.axis_size(axis)
    here = lax.axis_index(axis)
    return [
        lax.ppermute(
            lax.dynamic_index_in_dim(parts, (here + step) % size, 0, False), axis, ring(axis, step)
        )
        for step in range(1, size)
    ]


def collected(part, axis):
    size = lax.axis_size(axis)
    here = lax.axis_index(axis)
    ahead = [part] + [lax.ppermute(part, axis, ring(axis, size - step)) for step in range(1, size)]
    twice = jnp.stack(ahead + ahead[:-1])
    return lax.dynamic_slice_in_dim(twice, (size - here) % size, size, 0)


def pieces(value):
    high = lax.reduce_precision(value, 8, 7)
    middle = lax.reduce_precision(value - high, 8, 7)
    low = value - high - middle
    return [high.astype(jnp.bfloat16), middle.astype(jnp.bfloat16), low.astype(jnp.bfloat16)]


def packed_tail(lse_rows):
    count = len(lse_rows)
    row = lax.broadcasted_iota(jnp.int32, (16, HEAD), 0)
    tail = jnp.zeros((16, HEAD), jnp.float32)
    for index, lse in enumerate(lse_rows):
        high = lse.astype(jnp.bfloat16).astype(jnp.float32)
        middle = (lse - high).astype(jnp.bfloat16).astype(jnp.float32)
        low = lse - high - middle
        for k, term in enumerate((high, middle, low)):
            tail = jnp.where(row == k * count + index, jnp.broadcast_to(term, (16, HEAD)), tail)
    return tail.astype(jnp.bfloat16)


def attend_kernel(seqs, table, q_ref, pool_ref, out_ref, grouped, gathered, lse_rows, acc):
    page_len = pool_ref.shape[2]
    limit = pool_ref.shape[0]
    rows_each = q_ref.shape[1]
    requests = q_ref.shape[0]
    row_count = MEM * rows_each
    at_fill, at_code, at_start, at_slot = limit, 2 * limit, 3 * limit, 3 * limit + 8
    factor = HEAD ** (-0.5)
    grouped[...] = jnp.zeros_like(grouped)
    for r in range(requests):
        slot = table[at_slot + r]
        grouped[pl.ds(pl.multiple_of(slot * rows_each, rows_each), rows_each), :] = q_ref[r]
    lane_slot = lax.broadcasted_iota(jnp.int32, (1, row_count), 1) // rows_each
    token = lax.broadcasted_iota(jnp.int32, (page_len, row_count), 0)
    for g in range(GROUPS):
        first = table[at_start + g]
        last = table[at_start + g + 1]
        acc[...] = jnp.zeros_like(acc)

        def visit(number, carry):
            old_max, old_sum = carry
            base = first + number * TILE
            places = [jnp.minimum(base + i, limit - 1) for i in range(TILE)]
            keys = jnp.concatenate([pool_ref[table[p], 0] for p in places], 0)
            values = jnp.concatenate([pool_ref[table[p], 1] for p in places], 0)
            scores = lax.dot_general(
                keys,
                grouped[pl.ds(g * row_count, row_count), :],
                (((1,), (1,)), ((), ())),
                preferred_element_type=jnp.float32,
            )
            shown = []
            for i, p in enumerate(places):
                fill = jnp.where(base + i < last, table[at_fill + p], 0)
                code = table[at_code + p]
                rows_ok = jnp.where((lane_slot == code) | (code < 0), fill, 0)
                part = scores[i * page_len : (i + 1) * page_len]
                shown.append(jnp.where(token < rows_ok, part, NEG))
            new_max = old_max
            for part in shown:
                new_max = jnp.maximum(new_max, jnp.max(part, 0, keepdims=True))
            base_max = jnp.where(new_max > 0.5 * NEG, new_max, 0.0)
            fade = jnp.exp((old_max - base_max) * factor)
            expo = [jnp.exp((part - base_max) * factor) for part in shown]
            new_sum = old_sum * fade
            for part in expo:
                new_sum = new_sum + jnp.sum(part, 0, keepdims=True)
            weights = jnp.concatenate([part.astype(jnp.bfloat16) for part in expo], 0)
            acc[...] = acc[...] * fade + lax.dot_general(
                values, weights, (((0,), (0,)), ((), ())), preferred_element_type=jnp.float32
            )
            return new_max, new_sum

        start = (
            jnp.full((1, row_count), NEG, jnp.float32),
            jnp.zeros((1, row_count), jnp.float32),
        )
        run_max, run_sum = lax.fori_loop(0, (last - first + TILE - 1) // TILE, visit, start)
        held = run_sum > 0
        safe = jnp.where(held, run_sum, 1.0)
        lse = jnp.where(held, run_max * factor + jnp.log(safe), NEG)
        gathered[pl.ds(g * row_count, row_count), :] = (acc[...] * (1.0 / safe)).T
        for k in range(row_count // HEAD):
            lse_rows[pl.ds(g * (row_count // HEAD) + k, 1), :] = lse[:, k * HEAD : (k + 1) * HEAD]
    lane = lax.broadcasted_iota(jnp.int32, (8, HEAD), 1) // rows_each
    each = requests // seqs
    per_row = HEAD // rows_each
    for s in range(seqs):
        tails = []
        for k in range(each // per_row):
            line = jnp.zeros((8, HEAD), jnp.float32)
            for i in range(per_row):
                r = s * each + k * per_row + i
                slot = table[at_slot + r]
                out_ref[s, pl.ds((k * per_row + i) * rows_each, rows_each), :] = gathered[
                    pl.ds(pl.multiple_of(slot * rows_each, rows_each), rows_each), :
                ].astype(jnp.bfloat16)
                source = jnp.broadcast_to(lse_rows[pl.ds(slot // per_row, 1), :], (8, HEAD))
                shift = lax.rem(i - lax.rem(slot, per_row) + per_row, per_row) * rows_each
                line = jnp.where(lane == i, pltpu.roll(source, shift, 1), line)
            tails.append(line[0:1])
        out_ref[s, pl.ds(each * rows_each, 16), :] = packed_tail(tails)


TILE = 4


def attend(table, queries, pool, seqs):
    requests, rows_each, _ = queries.shape
    limit = pool.shape[0] // 2
    own = requests // seqs * rows_each
    return pl.pallas_call(
        functools.partial(attend_kernel, seqs),
        out_shape=jax.ShapeDtypeStruct((seqs, own + 16, HEAD), jnp.bfloat16),
        grid_spec=pltpu.PrefetchScalarGridSpec(
            num_scalar_prefetch=1,
            grid=(1,),
            in_specs=[
                pl.BlockSpec((requests, rows_each, HEAD), lambda i, t: (0, 0, 0)),
                pl.BlockSpec((limit,) + pool.shape[1:], lambda i, t: (0, 0, 0, 0)),
            ],
            out_specs=pl.BlockSpec((seqs, own + 16, HEAD), lambda i, t: (0, 0, 0)),
            scratch_shapes=[
                pltpu.VMEM((GROUPS * MEM * rows_each, HEAD), jnp.bfloat16),
                pltpu.VMEM((GROUPS * MEM * rows_each, HEAD), jnp.float32),
                pltpu.VMEM((GROUPS * MEM * rows_each // HEAD, HEAD), jnp.float32),
                pltpu.VMEM((HEAD, MEM * rows_each), jnp.float32),
            ],
        ),
        cost_estimate=pl.CostEstimate(
            flops=4 * limit * 64 * MEM * rows_each * HEAD,
            bytes_accessed=limit * 2 * 64 * HEAD * 2,
            transcendentals=limit * 64 * MEM * rows_each,
        ),
        name="attend",
    )(table, queries, pool)


def fresh_kernel(steps, q_ref, k_ref, v_ref, out_ref):
    rows = q_ref.shape[0]
    count = k_ref.shape[0] // steps
    rows_each = rows // count
    shape = (steps * count, rows)
    key = lax.broadcasted_iota(jnp.int32, shape, 0)
    lane = lax.broadcasted_iota(jnp.int32, shape, 1)
    seen = (lane // rows_each == lax.rem(key, count)) & (
        key // count <= lax.rem(lane, rows_each) // (rows_each // steps)
    )
    scores = lax.dot_general(
        k_ref[...], q_ref[...], (((1,), (1,)), ((), ())), preferred_element_type=jnp.float32
    ) * HEAD ** (-0.5)
    scores = jnp.where(seen, scores, NEG)
    peak = jnp.max(scores, 0, keepdims=True)
    expo = jnp.where(seen, jnp.exp(scores - peak), 0.0)
    total = jnp.sum(expo, 0, keepdims=True)
    value = lax.dot_general(
        v_ref[...],
        expo.astype(jnp.bfloat16),
        (((0,), (0,)), ((), ())),
        preferred_element_type=jnp.float32,
    )
    out_ref[pl.ds(0, rows), :] = (value * (1.0 / total)).T.astype(jnp.bfloat16)
    lse = peak + jnp.log(total)
    out_ref[pl.ds(rows, 16), :] = packed_tail(
        [lse[:, k * HEAD : (k + 1) * HEAD] for k in range(rows // HEAD)]
    )


def fresh_part(queries, keys, values, steps):
    rows = queries.shape[0]
    return pl.pallas_call(
        functools.partial(fresh_kernel, steps),
        out_shape=jax.ShapeDtypeStruct((rows + 16, HEAD), jnp.bfloat16),
        cost_estimate=pl.CostEstimate(
            flops=4 * rows * keys.shape[0] * HEAD, bytes_accessed=rows * HEAD * 4, transcendentals=0
        ),
        name="fresh",
    )(queries, keys, values)


def mix_refs(parts):
    rows = parts[0].shape[0] - 16
    blocks = rows // HEAD
    lses = []
    for part in parts:
        tail = part[pl.ds(rows, 16), :].astype(jnp.float32)
        lses.append(
            tail[0:blocks] + tail[blocks : 2 * blocks] + tail[2 * blocks : 3 * blocks]
        )
    peak = lses[0]
    for lse in lses[1:]:
        peak = jnp.maximum(peak, lse)
    fades = [jnp.exp(lse - peak) for lse in lses]
    total = sum(fades)
    inverse = 1.0 / total
    turned = [
        jnp.concatenate([fade * inverse, jnp.zeros((8 - blocks, HEAD), jnp.float32)], 0).T
        for fade in fades
    ]
    values = []
    for k in range(blocks):
        value = 0.0
        for part, weight in zip(parts, turned):
            value = value + part[pl.ds(k * HEAD, HEAD), :].astype(jnp.float32) * weight[:, k : k + 1]
        values.append(value)
    return values, peak + jnp.log(total)


def mix_kernel(*refs):
    out_ref = refs[-1]
    values, lse = mix_refs(refs[:-1])
    for k, value in enumerate(values):
        out_ref[pl.ds(k * HEAD, HEAD), :] = value.astype(jnp.bfloat16)
    out_ref[pl.ds(len(values) * HEAD, 16), :] = packed_tail(
        [lse[k : k + 1] for k in range(len(values))]
    )


def mix(parts):
    return pl.pallas_call(
        mix_kernel,
        out_shape=jax.ShapeDtypeStruct(parts[0].shape, jnp.bfloat16),
        cost_estimate=pl.CostEstimate(
            flops=2 * len(parts) * parts[0].size, bytes_accessed=parts[0].size * 10, transcendentals=0
        ),
        name="mix",
    )(*parts)


def final_kernel(ratio, *refs):
    parts, out_ref, scratch = refs[:-2], refs[-2], refs[-1]
    values, _ = mix_refs(parts)
    for k, value in enumerate(values):
        scratch[pl.ds(k * HEAD, HEAD), :] = value
    tokens = out_ref.shape[0]
    for h in range(ratio):
        out_ref[:, h * HEAD : (h + 1) * HEAD] = scratch[pl.ds(h, tokens, stride=ratio), :].astype(
            jnp.bfloat16
        )


def final(parts, ratio):
    rows = parts[0].shape[0] - 16
    return pl.pallas_call(
        functools.partial(final_kernel, ratio),
        out_shape=jax.ShapeDtypeStruct((rows // ratio, ratio * HEAD), jnp.bfloat16),
        scratch_shapes=[pltpu.VMEM((rows, HEAD), jnp.float32)],
        cost_estimate=pl.CostEstimate(
            flops=2 * len(parts) * parts[0].size, bytes_accessed=parts[0].size * 10, transcendentals=0
        ),
        name="final",
    )(*parts)


def page_table(owners, fills, group_of_request):
    requests = group_of_request.shape[0]
    count = owners.shape[0]
    index = jnp.arange(requests, dtype=jnp.int32)
    same = group_of_request[:, None] == group_of_request[None, :]
    rank = jnp.sum((same & (index[None, :] < index[:, None])).astype(jnp.int32), 1)
    slot = group_of_request * MEM + rank
    shared = owners >= requests
    own_slot = jnp.sum(jnp.where(owners[:, None] == index[None, :], slot[None, :], 0), 1)
    group = jnp.where(shared, owners - requests, own_slot // MEM)
    group = jnp.where(owners >= 0, group, GROUPS)
    code = jnp.where(shared, -1, own_slot % MEM)
    place = jnp.arange(count, dtype=jnp.int32)
    before = (group[None, :] < group[:, None]) | (
        (group[None, :] == group[:, None]) & (place[None, :] < place[:, None])
    )
    target = jnp.sum(before.astype(jnp.int32), 1)
    hit = target[None, :] == place[:, None]
    ordered = [
        jnp.sum(jnp.where(hit, row[None, :], 0), 1) for row in (place, fills, code)
    ]
    starts = jnp.sum(
        (group[None, :] < jnp.arange(8, dtype=jnp.int32)[:, None]).astype(jnp.int32), 1
    )
    return jnp.concatenate(ordered + [starts, slot])


CAP_SEQ = 44
CAP_ROW = 40


def earlier(count):
    index = jnp.arange(count, dtype=jnp.int32)
    return index[None, :] < index[:, None]


def counted(mask, axis):
    return jnp.sum(mask.astype(jnp.int32), axis)


def inverted(place, value, count):
    hit = place[None, :] == jnp.arange(count, dtype=jnp.int32)[:, None]
    return jnp.sum(jnp.where(hit, value[None, :], 0), 1)


def migration_tables(page_owner, migrate_dest, pool_size):
    rows, seqs = lax.axis_size("row"), lax.axis_size("seq")
    row, seq = lax.axis_index("row"), lax.axis_index("seq")
    limit = pool_size // 2
    cap = pool_size // (rows * seqs)
    dest = migrate_dest.reshape(rows, seqs, pool_size)[:, :, :limit]
    live = (page_owner >= 0).reshape(rows, seqs, pool_size)[:, :, :limit]
    dest = jnp.where(live, dest, -1)
    column = jnp.where(live, dest % seqs, -1)
    all_seq = jnp.arange(seqs, dtype=jnp.int32)
    in_column = counted(column[..., None, :] == all_seq[:, None], -1)
    everyone = jnp.arange(rows * seqs, dtype=jnp.int32)
    from_row = counted(dest.reshape(rows, 1, seqs * limit) == everyone[:, None], -1)
    fits = (jnp.max(in_column) <= CAP_SEQ) & (jnp.max(from_row) <= CAP_ROW)

    dest_row = lax.dynamic_index_in_dim(dest, row, 0, False)
    own = lax.dynamic_index_in_dim(dest_row, seq, 0, False)
    step = jnp.where(own >= 0, (own % seqs - seq + seqs) % seqs, -1)
    rank = counted((step[None, :] == step[:, None]) & earlier(limit), 1)
    place = jnp.where((step >= 0) & (rank < CAP_SEQ), step * CAP_SEQ + rank, -1)
    first = inverted(place, jnp.arange(limit, dtype=jnp.int32), seqs * CAP_SEQ)

    sender = (seq - all_seq + seqs) % seqs
    lists = jnp.sum(
        jnp.where((sender[:, None] == all_seq[None, :])[..., None], dest_row[None], 0), 1
    )
    lists = lists.reshape(seqs * limit)
    which = jnp.arange(seqs * limit, dtype=jnp.int32) // limit
    here = (lists >= 0) & (lists % seqs == seq)
    step = jnp.where(here, (lists // seqs - row + rows) % rows, -1)
    before = earlier(seqs * limit) & here[None, :]
    rank = counted(before & (which[None, :] == which[:, None]), 1)
    order = counted(before & (step[None, :] == step[:, None]), 1)
    place = jnp.where(here & (order < CAP_ROW), step * CAP_ROW + order, -1)
    second = inverted(place, which * CAP_SEQ + jnp.minimum(rank, CAP_SEQ - 1), rows * CAP_ROW)

    coming = counted(dest == row * seqs + seq, -1)
    ahead = (seq - all_seq + seqs) % seqs
    offset = jnp.sum(jnp.where(ahead[None, :] < ahead[:, None], coming[:, None, :], 0), -1)
    listed = (row - jnp.arange(rows, dtype=jnp.int32) + rows) % rows
    page = jnp.arange(cap, dtype=jnp.int32)
    third = (listed[:, None] * CAP_ROW + offset)[..., None] + page
    third = jnp.where(page < coming[..., None], jnp.minimum(third, rows * CAP_ROW - 1), -1)
    return fits, first, second, third.reshape(pool_size), coming.reshape(rows * seqs)


def split_kernel(table, pool_ref, *out_refs):
    lists = len(out_refs) // 2
    length = out_refs[0].shape[0]
    for k in range(lists):

        def move(i, _):
            page = table[k * length + i]
            out_refs[k][i] = pool_ref[page, 0]
            out_refs[lists + k][i] = pool_ref[page, 1]
            return 0

        lax.fori_loop(0, length, move, 0, unroll=4)


def split_pool(table, pool, lists):
    limit, _, page_len, width = (pool.shape[0] // 2,) + pool.shape[1:]
    length = table.shape[0] // lists
    shape = (length, page_len, width)
    return pl.pallas_call(
        split_kernel,
        out_shape=[jax.ShapeDtypeStruct(shape, pool.dtype)] * (2 * lists),
        grid_spec=pltpu.PrefetchScalarGridSpec(
            num_scalar_prefetch=1,
            grid=(1,),
            in_specs=[pl.BlockSpec((limit,) + pool.shape[1:], lambda i, t: (0, 0, 0, 0))],
            out_specs=[pl.BlockSpec(shape, lambda i, t: (0, 0, 0))] * (2 * lists),
        ),
        cost_estimate=pl.CostEstimate(
            flops=0, bytes_accessed=pool.size + 4 * lists * length * page_len * width, transcendentals=0
        ),
        name="split_pool",
    )(table, pool)


def resplit_kernel(count, table, *refs):
    sources, outs = refs[:count], refs[count : 2 * count]
    scratch, sems = refs[2 * count], refs[2 * count + 1]
    length = sources[0].shape[0]
    copies = [
        pltpu.make_async_copy(ref, scratch.at[pl.ds(k * length, length)], sems.at[k])
        for k, ref in enumerate(sources)
    ]
    for copy in copies:
        copy.start()
    for copy in copies:
        copy.wait()
    length_out = outs[0].shape[0]
    for k, out in enumerate(outs):

        def move(i, _):
            out[i] = scratch[table[k * length_out + i]]
            return 0

        lax.fori_loop(0, length_out, move, 0, unroll=4)


def resplit(table, lists):
    count = len(lists)
    length, page_len, width = lists[0].shape
    shape = (table.shape[0] // count, page_len, width)
    return pl.pallas_call(
        functools.partial(resplit_kernel, count),
        out_shape=[jax.ShapeDtypeStruct(shape, lists[0].dtype)] * count,
        grid_spec=pltpu.PrefetchScalarGridSpec(
            num_scalar_prefetch=1,
            grid=(1,),
            in_specs=[pl.BlockSpec(memory_space=pl.ANY)] * count,
            out_specs=[pl.BlockSpec(shape, lambda i, t: (0, 0, 0))] * count,
            scratch_shapes=[
                pltpu.VMEM((count * length, page_len, width), lists[0].dtype),
                pltpu.SemaphoreType.DMA((count,)),
            ],
        ),
        cost_estimate=pl.CostEstimate(
            flops=0, bytes_accessed=4 * count * length * page_len * width, transcendentals=0
        ),
        name="resplit",
    )(table, *lists)


def settle_kernel(count, table, *refs):
    sources, out, scratch, sems = refs[: 2 * count], refs[-3], refs[-2], refs[-1]
    length = sources[0].shape[0]
    block = out.shape[0]

    @pl.when(pl.program_id(0) == 0)
    def _():
        copies = [
            pltpu.make_async_copy(
                ref, scratch.at[k // count, pl.ds(k % count * length, length)], sems.at[k]
            )
            for k, ref in enumerate(sources)
        ]
        for copy in copies:
            copy.start()
        for copy in copies:
            copy.wait()

    for i in range(block):
        place = table[pl.program_id(0) * block + i]

        @pl.when(place >= 0)
        def _():
            for half in range(2):
                out[i, half] = scratch[half, place]

        @pl.when(place < 0)
        def _():
            out[i] = jnp.zeros(out.shape[1:], out.dtype)


def settle(table, keys, values, block):
    count = len(keys)
    length, page_len, width = keys[0].shape
    slots = table.shape[0]
    return pl.pallas_call(
        functools.partial(settle_kernel, count),
        out_shape=jax.ShapeDtypeStruct((slots, 2, page_len, width), keys[0].dtype),
        grid_spec=pltpu.PrefetchScalarGridSpec(
            num_scalar_prefetch=1,
            grid=(slots // block,),
            in_specs=[pl.BlockSpec(memory_space=pl.ANY)] * (2 * count),
            out_specs=pl.BlockSpec((block, 2, page_len, width), lambda i, t: (i, 0, 0, 0)),
            scratch_shapes=[
                pltpu.VMEM((2, count * length, page_len, width), keys[0].dtype),
                pltpu.SemaphoreType.DMA((2 * count,)),
            ],
        ),
        cost_estimate=pl.CostEstimate(
            flops=0, bytes_accessed=8 * slots * page_len * width, transcendentals=0
        ),
        name="settle",
    )(table, *keys, *values)


def passed(lists, axis):
    return [lists[0]] + [
        lax.ppermute(part, axis, ring(axis, k)) for k, part in enumerate(lists) if k
    ]


def rotate(values, cosine, sine):
    half = values.shape[-1] // 2
    first_half = values[..., :half]
    second_half = values[..., half:]
    return jnp.concatenate(
        [first_half * cosine - second_half * sine, second_half * cosine + first_half * sine], -1
    )


def migrate_whole(kv_pool, migrate_dest, coming, device):
    pool_size = kv_pool.shape[0]
    own_dest = lax.dynamic_slice_in_dim(migrate_dest, device * pool_size, pool_size)
    send_order = jnp.argsort(own_dest, stable=True)
    moved = lax.all_to_all(
        kv_pool[send_order], ("row", "seq"), split_axis=0, concat_axis=0, tiled=True
    )
    page = jnp.arange(pool_size // coming.shape[0], dtype=jnp.int32)
    full = (page[None, :] < coming[:, None]).reshape(pool_size)
    return jnp.where(full[:, None, None, None], moved, jnp.zeros_like(moved))


def block(
    hidden_in,
    norm_gain,
    w_qkv,
    w_out,
    kv_pool,
    page_owner,
    page_fill,
    lengths,
    group_of_request,
    migrate_dest,
):
    step_count, request_count, width_here = hidden_in.shape
    ratio = HEADS // KV_HEADS
    heads_here = w_qkv.shape[1] // ((ratio + 2) * HEAD)
    hidden_f = hidden_in.astype(jnp.float32)
    fits, first_table, second_table, third_table, coming = migration_tables(
        page_owner, migrate_dest, kv_pool.shape[0]
    )
    seqs = lax.axis_size("seq")
    lists = split_pool(first_table, kv_pool, seqs)
    key_lists = passed(lists[:seqs], "seq")
    value_lists = passed(lists[seqs:], "seq")
    row_start = lax.axis_index("row") * width_here
    gain_f = lax.dynamic_slice_in_dim(norm_gain, row_start, width_here).astype(jnp.float32)
    width = width_here * lax.axis_size("row")
    squares = jnp.sum(hidden_f * hidden_f, -1)
    partial_value = jnp.dot(
        (hidden_f * gain_f).astype(jnp.bfloat16).reshape(step_count * request_count, width_here),
        w_qkv,
        preferred_element_type=jnp.float32,
    ).astype(jnp.bfloat16)
    columns = partial_value.shape[1]
    extra = jnp.pad(jnp.stack(pieces(squares), -1), ((0, 0), (0, 0), (0, HEAD - 3)))
    partial_value = jnp.concatenate(
        [partial_value.reshape(step_count, request_count, columns), extra], 2
    )
    step_here = lax.axis_index("row")
    position = (lengths + step_here).astype(jnp.float32)
    half = HEAD // 2
    angle = position[:, None] * THETA ** (-(jnp.arange(half, dtype=jnp.float32) * 2.0 / HEAD))
    cosine, sine = lax.optimization_barrier((jnp.cos(angle), jnp.sin(angle)))
    summed = lax.dynamic_index_in_dim(partial_value, step_here, 0, False).astype(jnp.float32)
    arrived = exchanged(partial_value, "row")
    for part in arrived:
        summed = summed + part.astype(jnp.float32)
    scale = lax.rsqrt(jnp.sum(summed[:, columns : columns + 3], -1) / width + EPS)
    projected = (summed[:, :columns] * scale[:, None]).astype(jnp.bfloat16).astype(jnp.float32)
    projected = projected.reshape(request_count, heads_here * (ratio + 2), HEAD)
    rotated = rotate(projected, cosine[:, None], sine[:, None])
    is_value = jnp.arange(heads_here * (ratio + 2)) % (ratio + 2) == ratio + 1
    ready = jnp.where(is_value[None, :, None], projected, rotated).astype(jnp.bfloat16)
    ready = collected(ready, "row")
    ready = ready.reshape(step_count, request_count, heads_here, ratio + 2, HEAD)
    key_lists = resplit(second_table, key_lists)
    key_lists = passed(key_lists, "row")
    queries = ready[:, :, :, :ratio]
    keys_new = ready[:, :, :, ratio]
    values_new = ready[:, :, :, ratio + 1]
    local_req = request_count // lax.axis_size("seq")
    req_start = lax.axis_index("seq") * local_req
    new_kv = jnp.stack(
        [
            keys_new.reshape(step_count, request_count, heads_here * HEAD),
            values_new.reshape(step_count, request_count, heads_here * HEAD),
        ],
        2,
    )
    new_kv_local = lax.dynamic_slice_in_dim(new_kv, req_start, local_req, 1)
    device = lax.axis_index("row") * lax.axis_size("seq") + lax.axis_index("seq")
    pool_size = kv_pool.shape[0]
    owners_here = lax.dynamic_slice_in_dim(page_owner, device * pool_size, pool_size)
    fills = lax.dynamic_slice_in_dim(page_fill, device * pool_size, pool_size)
    live_limit = pool_size // 2
    table = page_table(owners_here[:live_limit], fills[:live_limit], group_of_request)
    rows_here = step_count * ratio
    rows_first = queries[:, :, 0].transpose(1, 0, 2, 3).reshape(request_count, rows_here, HEAD)
    seq_size = lax.axis_size("seq")
    own_rows = local_req * rows_here
    both = attend(table, rows_first, kv_pool, seq_size)
    parts = [lax.dynamic_index_in_dim(both, lax.axis_index("seq"), 0, False)]
    parts += exchanged(both, "seq")
    value_lists = resplit(second_table, value_lists)
    both = mix(parts)
    parts = [both] + [lax.ppermute(both, "row", ring("row", k)) for k in range(1, 4)]
    value_lists = passed(value_lists, "row")
    query_own = lax.dynamic_slice_in_dim(rows_first, req_start, local_req, 0)
    key_own = lax.dynamic_slice_in_dim(keys_new, req_start, local_req, 1)
    value_own = lax.dynamic_slice_in_dim(values_new, req_start, local_req, 1)
    own = fresh_part(
        query_own.reshape(own_rows, HEAD),
        key_own.reshape(step_count * local_req, HEAD),
        value_own.reshape(step_count * local_req, HEAD),
        step_count,
    )
    picked = final([own] + parts, ratio)
    partial_out = jnp.dot(picked, w_out, preferred_element_type=jnp.float32).astype(jnp.bfloat16)
    col_size = lax.axis_size("col")
    col_width = partial_out.shape[1] // col_size
    spread = partial_out.reshape(step_count * local_req, col_size, col_width).transpose(1, 0, 2)
    summed = jnp.sum(
        lax.all_to_all(spread, "col", 0, 0, tiled=True).astype(jnp.float32), 0
    )
    residual = lax.dynamic_slice_in_dim(
        lax.dynamic_slice_in_dim(hidden_f, req_start, local_req, 1),
        lax.axis_index("col") * col_width,
        col_width,
        2,
    )
    summed = summed.reshape(local_req, step_count, col_width).transpose(1, 0, 2)
    layer_out = (summed + residual).astype(jnp.bfloat16)
    moved = lax.cond(
        fits,
        lambda: settle(third_table, key_lists, value_lists, kv_pool.shape[0] // coming.shape[0]),
        lambda: migrate_whole(kv_pool, migrate_dest, coming, device),
    )
    return (layer_out, new_kv_local, moved)


def solution(mesh):
    in_specs = (
        P(None, None, "row"),
        P(),
        P("row", "col"),
        P("col", "row"),
        P(("row", "seq"), None, None, "col"),
        P(),
        P(),
        P(),
        P(),
        P(),
    )
    out_specs = (
        P(None, "seq", ("row", "col")),
        P(None, "seq", None, "col"),
        P(("row", "seq"), None, None, "col"),
    )
    return jax.shard_map(block, mesh=mesh, in_specs=in_specs, out_specs=out_specs, check_vma=False)
```

profile of v0, /device:TPU:0, one launch (start us, length us, event | category | flops | bytes accessed | tf_op | source)
XLA Modules:
  0.0 192.5 jit_solution(4026099075031977097)
XLA Ops:
  0.6 0.7 broadcast_compare_fusion.1
  1.4 0.8 dynamic_slice.75
  2.1 0.9 convert_reduce_fusion.7
  3.0 0.7 multiply_add_fusion.1
  3.7 0.7 reshape.599
  4.9 0.7 select_reduce_fusion.2.table
  5.6 6.1 %split_pool.1 = (bf16[44,64,128]{2,1,0:T(8,128)(2,1)}, bf16[44,64,128]{2,1,0:T(8,128)(2,1)}, bf16[44,64,128]{2,1,0:T(8,128)(2,1)}, bf16[44,64,128]{2,1,0:T(8,128...) custom-call(s32[176]{0:T(256)} %select_reduce_fusion.2.table, ...), custom_call_target="tpu_custom_call" | custom-call | bytes 9961472 | tf_op jit(solution)/shard_map/split_pool/pallas_call | solution.py:409
  11.7 2.0 %collective-permute-start.12 = (bf16[44,64,128]{2,1,0:T(8,128)(2,1)}, bf16[44,64,128]{2,1,0:T(8,128)(2,1)S(1)}, u32[]{:S(2)}, u32[]{:S(2)}) collective-permute-start(bf16[44,64,128]{2,1,0:T(8,128)(2,1)} %get-tuple-element.171), channel_id=1, source_target_pairs={{0,1},{1,2},{2,3},{3,0},{4,5},{5,6},{6,7},{7,4},{8,9},{9,10},{10,1... | collective-permute-start | bytes 2162696 | tf_op jit(solution)/shard_map/ppermute | solution.py:528
  13.8 3.6 %collective-permute-start.13 = (bf16[44,64,128]{2,1,0:T(8,128)(2,1)}, bf16[44,64,128]{2,1,0:T(8,128)(2,1)S(1)}, u32[]{:S(2)}, u32[]{:S(2)}) collective-permute-start(bf16[44,64,128]{2,1,0:T(8,128)(2,1)} %get-tuple-element.172), channel_id=1, source_target_pairs={{0,2},{1,3},{2,0},{3,1},{4,6},{5,7},{6,4},{7,5},{8,10},{9,11},{10,... | collective-permute-start | bytes 2162696 | tf_op jit(solution)/shard_map/ppermute | solution.py:528
  17.3 0.7 dynamic-slice_convert_fusion
  18.5 3.7 %convolution_convert_fusion = bf16[192,1280]{1,0:T(8,128)(2,1)S(1)} fusion(bf16[192,2048]{1,0:T(8,128)(2,1)S(1)} %bitcast.123, bf16[2048,1280]{1,0:T(8,128)(2,1)} %param.14), kind=kOutput, calls=%fused_computation.22 | convolution fusion | flops 1006878720 | bytes 6520832 | tf_op jit(solution)/shard_map/dot_general | solution.py:580
  22.3 0.7 dynamic-slice_bitcast_fusion.2
  23.0 1.6 collective-permute-start
  24.6 2.9 %collective-permute-start.1 = (bf16[48,1408]{1,0:T(8,128)(2,1)S(1)}, bf16[48,1408]{1,0:T(8,128)(2,1)S(1)}, u32[]{:S(2)}, u32[]{:S(2)}) collective-permute-start(bf16[48,1408]{1,0:T(8,128)(2,1)S(1)} %get-tuple-element.226), channel_id=1, source_target_pairs={{0,64},{32,96},{64,0},{96,32},{1,65},{33,97},{65,1},{97,33},{2,66}... | collective-permute-start | bytes 405512 | tf_op jit(solution)/shard_map/ppermute | solution.py:31
  27.5 1.3 collective-permute-start.2
  30.3 0.8 dynamic_slice.76
  31.5 0.7 concatenate.27.table
  32.2 1.0 collective-permute-start.14
  33.3 0.9 collective-permute-start.18
  34.2 1.0 fusion.13
  35.9 1.6 collective-permute-start.3
  37.6 4.0 %collective-permute-done.3 = bf16[48,10,128]{2,1,0:T(8,128)(2,1)S(1)} collective-permute-done((bf16[48,10,128]{2,1,0:T(8,128)(2,1)S(1)}, bf16[48,10,128]{2,1,0:T(8,128)(2,1)S(1)}, u32[]{:S(2)}, u32[]{:S(2)}) %collective-permute-start.3) | collective-permute-done | bytes 122912 | tf_op jit(solution)/shard_map/ppermute | solution.py:41
  41.6 2.1 %collective-permute-start.4 = (bf16[48,10,128]{2,1,0:T(8,128)(2,1)S(1)}, bf16[48,10,128]{2,1,0:T(8,128)(2,1)S(1)}, u32[]{:S(2)}, u32[]{:S(2)}) collective-permute-start(bf16[48,10,128]{2,1,0:T(8,128)(2,1)S(1)} %fusion.11), channel_id=1, source_target_pairs={{0,64},{32,96},{64,0},{96,32},{1,65},{33,97},{65,1},{97,33},{2,66}... | collective-permute-start | bytes 368648 | tf_op jit(solution)/shard_map/ppermute | solution.py:41
  43.8 5.0 %collective-permute-done.4 = bf16[48,10,128]{2,1,0:T(8,128)(2,1)S(1)} collective-permute-done((bf16[48,10,128]{2,1,0:T(8,128)(2,1)S(1)}, bf16[48,10,128]{2,1,0:T(8,128)(2,1)S(1)}, u32[]{:S(2)}, u32[]{:S(2)}) %collective-permute-start.4) | collective-permute-done | bytes 122912 | tf_op jit(solution)/shard_map/ppermute | solution.py:41
  48.8 0.7 collective-permute-start.5
  49.5 6.2 %collective-permute-done.5 = bf16[48,10,128]{2,1,0:T(8,128)(2,1)S(1)} collective-permute-done((bf16[48,10,128]{2,1,0:T(8,128)(2,1)S(1)}, bf16[48,10,128]{2,1,0:T(8,128)(2,1)S(1)}, u32[]{:S(2)}, u32[]{:S(2)}) %collective-permute-start.5) | collective-permute-done | bytes 122912 | tf_op jit(solution)/shard_map/ppermute | solution.py:41
  55.7 1.6 collective-permute-start.19
  57.7 0.9 copy.58
  58.6 23.4 %attend.1 = bf16[4,400,128]{2,1,0:T(8,128)(2,1)} custom-call(s32[440]{0:T(512)} %concatenate.27.table, bf16[48,32,128]{2,1,0:T(8,128)(2,1)} %bitcast.116, bf16[256,2,64,128]{3,2,1,0:T(8,128)(2,1)} %pool_ref.3), custom_call_target="tpu_custom_call" | custom-call | flops 2147483648 | bytes 4194304 | tf_op jit(solution)/shard_map/attend/pallas_call | solution.py:157
  82.0 1.7 dynamic-slice_bitcast_fusion.3
  83.7 2.0 %collective-permute-start.6 = (bf16[400,128]{1,0:T(8,128)(2,1)S(1)}, bf16[400,128]{1,0:T(8,128)(2,1)S(1)}, u32[]{:S(2)}, u32[]{:S(2)}) collective-permute-start(bf16[400,128]{1,0:T(8,128)(2,1)S(1)} %get-tuple-element.235), channel_id=1, source_target_pairs={{0,1},{1,2},{2,3},{3,0},{4,5},{5,6},{6,7},{7,4},{8,9},{9,10},{10,1... | collective-permute-start | bytes 307208 | tf_op jit(solution)/shard_map/ppermute | solution.py:31
  85.7 2.0 %collective-permute-start.7 = (bf16[400,128]{1,0:T(8,128)(2,1)S(1)}, bf16[400,128]{1,0:T(8,128)(2,1)}, u32[]{:S(2)}, u32[]{:S(2)}) collective-permute-start(bf16[400,128]{1,0:T(8,128)(2,1)S(1)} %get-tuple-element.234), channel_id=1, source_target_pairs={{0,2},{1,3},{2,0},{3,1},{4,6},{5,7},{6,4},{7,5},{8,10},{9,11},{10,... | collective-permute-start | bytes 307208 | tf_op jit(solution)/shard_map/ppermute | solution.py:31
  87.7 0.6 select_reduce_fusion.1.table
  88.3 4.4 %resplit.2 = (bf16[40,64,128]{2,1,0:T(8,128)(2,1)}, bf16[40,64,128]{2,1,0:T(8,128)(2,1)}, bf16[40,64,128]{2,1,0:T(8,128)(2,1)}, bf16[40,64,128]{2,1,0:T(8,128)(2,1)}) custom-call(s32[160]{0:T(256)} %select_reduce_fusion.1.table, bf16[44,64,128]{2,1,0:T(8,128)(2,1)} %get-tuple-element.170.refs_0_, bf16[44,64,128]{2,1,0:T(8,128)(2,1)} %copy-done.1, ...), custom_call_target="tpu_custom_call" | custom-call | bytes 5767168 | tf_op jit(solution)/shard_map/resplit/pallas_call | solution.py:451
  93.3 9.7 %collective-permute-start.8 = (bf16[400,128]{1,0:T(8,128)(2,1)S(1)}, bf16[400,128]{1,0:T(8,128)(2,1)S(1)}, u32[]{:S(2)}, u32[]{:S(2)}) collective-permute-start(bf16[400,128]{1,0:T(8,128)(2,1)S(1)} %get-tuple-element.233), channel_id=1, source_target_pairs={{0,3},{1,0},{2,1},{3,2},{4,7},{5,4},{6,5},{7,6},{8,11},{9,8},{10,9... | collective-permute-start | bytes 307208 | tf_op jit(solution)/shard_map/ppermute | solution.py:31
  103.3 0.7 reduce_max.18
  104.1 1.5 collective-permute-done.8.refs_3_
  105.6 0.6 copy-done.9
  106.3 2.1 %mix.1.refs_1_ = bf16[400,128]{1,0:T(8,128)(2,1)} custom-call(bf16[400,128]{1,0:T(8,128)(2,1)} %get-tuple-element.236.refs_0_, bf16[400,128]{1,0:T(8,128)(2,1)} %copy-done.8, bf16[400,128]{1,0:T(8,128)(2,1)} %collective-permute-done.7.refs_2_, bf16[400,128]{1,0:T(8,128)(2,1)} %copy-done.9), custom_call_target="tpu_custom_call" | custom-call | flops 409600 | bytes 512000 | tf_op jit(solution)/shard_map/mix/pallas_call | solution.py:265
  108.9 5.9 %collective-permute-done.10.refs_3_ = bf16[400,128]{1,0:T(8,128)(2,1)S(1)} collective-permute-done((bf16[400,128]{1,0:T(8,128)(2,1)}, bf16[400,128]{1,0:T(8,128)(2,1)S(1)}, u32[]{:S(2)}, u32[]{:S(2)}) %collective-permute-start.10) | collective-permute-done | bytes 102432 | tf_op jit(solution)/shard_map/ppermute | solution.py:637
  114.8 0.6 reshape.594.k_ref
  116.0 3.6 %collective-permute-done.11.refs_4_ = bf16[400,128]{1,0:T(8,128)(2,1)S(1)} collective-permute-done((bf16[400,128]{1,0:T(8,128)(2,1)}, bf16[400,128]{1,0:T(8,128)(2,1)S(1)}, u32[]{:S(2)}, u32[]{:S(2)}) %collective-permute-start.11) | collective-permute-done | bytes 102432 | tf_op jit(solution)/shard_map/ppermute | solution.py:637
  119.9 1.5 constant_dynamic-slice_fusion.4
  121.5 2.0 %fresh.1.refs_0_ = bf16[400,128]{1,0:T(8,128)(2,1)} custom-call(bf16[384,128]{1,0:T(8,128)(2,1)} %bitcast.125, bf16[48,128]{1,0:T(8,128)(2,1)} %reshape.594.k_ref, bf16[48,128]{1,0:T(8,128)(2,1)} %reshape.595.v_ref), custom_call_target="tpu_custom_call" | custom-call | flops 9437184 | bytes 196608 | tf_op jit(solution)/shard_map/fresh/pallas_call | solution.py:216
  123.4 9.7 %collective-permute-done.9.refs_2_ = bf16[400,128]{1,0:T(8,128)(2,1)S(1)} collective-permute-done((bf16[400,128]{1,0:T(8,128)(2,1)}, bf16[400,128]{1,0:T(8,128)(2,1)S(1)}, u32[]{:S(2)}, u32[]{:S(2)}) %collective-permute-start.9) | collective-permute-done | bytes 102432 | tf_op jit(solution)/shard_map/ppermute | solution.py:637
  133.2 0.7 copy-done.7
  133.8 2.3 %final.1 = bf16[48,1024]{1,0:T(8,128)(2,1)} custom-call(bf16[400,128]{1,0:T(8,128)(2,1)} %fresh.1.refs_0_, bf16[400,128]{1,0:T(8,128)(2,1)} %mix.1.refs_1_, bf16[400,128]{1,0:T(8,128)(2,1)} %copy-done.7, bf16[400,128]{1,0:T(8,128)(2,1)} %copy-done.5, bf16[400,128]{1,0:T(8,128)(2,1)} %copy-done.6), custom_call_target="tpu_custom_call" | custom-call | flops 512000 | bytes 512000 | tf_op jit(solution)/shard_map/final/pallas_call | solution.py:289
  136.2 4.4 %resplit.3 = (bf16[40,64,128]{2,1,0:T(8,128)(2,1)}, bf16[40,64,128]{2,1,0:T(8,128)(2,1)}, bf16[40,64,128]{2,1,0:T(8,128)(2,1)}, bf16[40,64,128]{2,1,0:T(8,128)(2,1)}) custom-call(s32[160]{0:T(256)} %select_reduce_fusion.1.table, bf16[44,64,128]{2,1,0:T(8,128)(2,1)} %get-tuple-element.178.refs_0_, bf16[44,64,128]{2,1,0:T(8,128)(2,1)} %collective-permute-done.18.refs_1_, ...), custom_call_target="tpu_custom_call" | custom-call | bytes 5767168 | tf_op jit(solution)/shard_map/resplit/pallas_call | solution.py:451
  140.6 2.1 %collective-permute-start.21 = (bf16[40,64,128]{2,1,0:T(8,128)(2,1)}, bf16[40,64,128]{2,1,0:T(8,128)(2,1)}, u32[]{:S(2)}, u32[]{:S(2)}) collective-permute-start(bf16[40,64,128]{2,1,0:T(8,128)(2,1)} %get-tuple-element.183), channel_id=1, source_target_pairs={{0,32},{32,64},{64,96},{96,0},{1,33},{33,65},{65,97},{97,1},{2,34}... | collective-permute-start | bytes 1966088 | tf_op jit(solution)/shard_map/ppermute | solution.py:528
  142.7 3.5 %collective-permute-start.22 = (bf16[40,64,128]{2,1,0:T(8,128)(2,1)}, bf16[40,64,128]{2,1,0:T(8,128)(2,1)}, u32[]{:S(2)}, u32[]{:S(2)}) collective-permute-start(bf16[40,64,128]{2,1,0:T(8,128)(2,1)} %get-tuple-element.184), channel_id=1, source_target_pairs={{0,64},{32,96},{64,0},{96,32},{1,65},{33,97},{65,1},{97,33},{2,66}... | collective-permute-start | bytes 1966088 | tf_op jit(solution)/shard_map/ppermute | solution.py:528
  146.1 0.6 collective-permute-start.23
  146.8 3.0 %convolution_convert_fusion.1 = bf16[48,2048]{1,0:T(8,128)(2,1)S(1)} fusion(bf16[48,1024]{1,0:T(8,128)(2,1)S(1)} %copy-done.4, bf16[1024,2048]{1,0:T(8,128)(2,1)} %param.15), kind=kOutput, calls=%fused_computation.23 | convolution fusion | flops 201424896 | bytes 4489216 | tf_op jit(solution)/shard_map/dot_general | solution.py:649
  149.8 0.7 copy.59
  150.5 4.3 %all-to-all-start.1 = ((bf16[8,48,256]{2,1,0:T(8,128)(2,1)}), bf16[8,48,256]{2,1,0:T(8,128)(2,1)S(1)}, u32[]{:S(2)}, u32[]{:S(2)}) async-start(bf16[8,48,256]{2,1,0:T(8,128)(2,1)} %bitcast.114), calls=%async_computation.1 | async-start | bytes 393216 | tf_op jit(solution)/shard_map/all_to_all | solution.py:654
  155.0 0.6 reduce_max.19
  157.0 0.6 copy.48
  157.6 4.0 %all-to-all-done.1 = bf16[8,48,256]{2,1,0:T(8,128)(2,1)S(1)} async-done(((bf16[8,48,256]{2,1,0:T(8,128)(2,1)}), bf16[8,48,256]{2,1,0:T(8,128)(2,1)S(1)}, u32[]{:S(2)}, u32[]{:S(2)}) %all-to-all-start.1) | async-done | bytes 196640 | tf_op jit(solution)/shard_map/all_to_all | solution.py:654
  161.8 0.6 copy.47
  162.4 3.4 %collective-permute-done.17 = bf16[40,64,128]{2,1,0:T(8,128)(2,1)} collective-permute-done((bf16[40,64,128]{2,1,0:T(8,128)(2,1)}, bf16[40,64,128]{2,1,0:T(8,128)(2,1)}, u32[]{:S(2)}, u32[]{:S(2)}) %collective-permute-start.17) | collective-permute-done | bytes 655392 | tf_op jit(solution)/shard_map/ppermute | solution.py:528
  165.8 2.1 %collective-permute-done.21 = bf16[40,64,128]{2,1,0:T(8,128)(2,1)} collective-permute-done((bf16[40,64,128]{2,1,0:T(8,128)(2,1)}, bf16[40,64,128]{2,1,0:T(8,128)(2,1)}, u32[]{:S(2)}, u32[]{:S(2)}) %collective-permute-start.21) | collective-permute-done | bytes 655392 | tf_op jit(solution)/shard_map/ppermute | solution.py:528
  167.9 12.0 %collective-permute-done.23 = bf16[40,64,128]{2,1,0:T(8,128)(2,1)} collective-permute-done((bf16[40,64,128]{2,1,0:T(8,128)(2,1)}, bf16[40,64,128]{2,1,0:T(8,128)(2,1)}, u32[]{:S(2)}, u32[]{:S(2)}) %collective-permute-start.23) | collective-permute-done | bytes 655392 | tf_op jit(solution)/shard_map/ppermute | solution.py:528
  179.9 12.4 %conditional.1 = (bf16[256,2,64,128]{3,2,1,0:T(8,128)(2,1)}) conditional(s32[]{:T(128)} %convert_element_type.144, (s32[4,4]{1,0:T(4,128)S(1)}, s32[]{:T(128)}, s32[4096]{0:T(1024)}, bf16[256,2,64,128]{3,2,1,0:T(8,128)(2,1)}) %tuple.49, (s32[4,4]{1,0:T(4,128)S(1)}, s32[4,4,16]{2,1,0:T(4,128)S(1)}, s32[]{:T(128)}, s32[]{:T(128)}, s32[]{:T(128)}, ...), branch_computations={%region_21.23_spmd, %region_23.25_spmd} | conditional | flops 4198404 | bytes 58736920 | solution.py:664
  180.3 0.7 select_n.300.table
  181.0 11.3 %settle.1 = bf16[256,2,64,128]{3,2,1,0:T(8,128)(2,1)} custom-call(s32[256]{0:T(256)} %select_n.300.table, bf16[40,64,128]{2,1,0:T(8,128)(2,1)S(1)} %get-tuple-element.139.refs_0_, bf16[40,64,128]{2,1,0:T(8,128)(2,1)} %get-tuple-element.140.refs_1_, bf16[40,64,128]{2,1,0:T(8,128)(2,1)S(1)} %get-tuple-element.141.refs_2_, ...), custom_call_target="tpu_custom_call" | custom-call | bytes 16777216 | tf_op jit(solution)/shard_map/cond/branch_1_fun/settle/pallas_call | solution.py:506
  (113 shorter events, 7.3 us)
Async XLA Ops:
  5.6 12.4 %copy-start = (bf16[4,48,2048]{2,1,0:T(8,128)(2,1)S(1)}, bf16[4,48,2048]{2,1,0:T(8,128)(2,1)}, u32[]{:S(2)}) copy-start(bf16[4,48,2048]{2,1,0:T(8,128)(2,1)} %param.12) | copy-start | bytes 2359300
  11.7 72.0 %collective-permute-start.12 = (bf16[44,64,128]{2,1,0:T(8,128)(2,1)}, bf16[44,64,128]{2,1,0:T(8,128)(2,1)S(1)}, u32[]{:S(2)}, u32[]{:S(2)}) collective-permute-start(bf16[44,64,128]{2,1,0:T(8,128)(2,1)} %get-tuple-element.171), channel_id=1, source_target_pairs={{0,1},{1,2},{2,3},{3,0},{4,5},{5,6},{6,7},{7,4},{8,9},{9,10},{10,1... | collective-permute-start | bytes 2162696 | tf_op jit(solution)/shard_map/ppermute | solution.py:528
  13.8 69.9 %collective-permute-start.13 = (bf16[44,64,128]{2,1,0:T(8,128)(2,1)}, bf16[44,64,128]{2,1,0:T(8,128)(2,1)S(1)}, u32[]{:S(2)}, u32[]{:S(2)}) collective-permute-start(bf16[44,64,128]{2,1,0:T(8,128)(2,1)} %get-tuple-element.172), channel_id=1, source_target_pairs={{0,2},{1,3},{2,0},{3,1},{4,6},{5,7},{6,4},{7,5},{8,10},{9,11},{10,... | collective-permute-start | bytes 2162696 | tf_op jit(solution)/shard_map/ppermute | solution.py:528
  22.2 7.8 %copy-start.11 = (s32[48]{0:T(128)S(1)}, s32[48]{0:T(128)}, u32[]{:S(2)}) copy-start(s32[48]{0:T(128)} %param.19) | copy-start | bytes 580
  23.0 9.2 %collective-permute-start = (bf16[48,1408]{1,0:T(8,128)(2,1)}, bf16[48,1408]{1,0:T(8,128)(2,1)S(1)}, u32[]{:S(2)}, u32[]{:S(2)}) collective-permute-start(bf16[48,1408]{1,0:T(8,128)(2,1)} %get-tuple-element.224), channel_id=1, source_target_pairs={{0,32},{32,64},{64,96},{96,0},{1,33},{33,65},{65,97},{97,1},{2,34}... | collective-permute-start | bytes 405512 | tf_op jit(solution)/shard_map/ppermute | solution.py:31
  24.6 8.7 %collective-permute-start.1 = (bf16[48,1408]{1,0:T(8,128)(2,1)S(1)}, bf16[48,1408]{1,0:T(8,128)(2,1)S(1)}, u32[]{:S(2)}, u32[]{:S(2)}) collective-permute-start(bf16[48,1408]{1,0:T(8,128)(2,1)S(1)} %get-tuple-element.226), channel_id=1, source_target_pairs={{0,64},{32,96},{64,0},{96,32},{1,65},{33,97},{65,1},{97,33},{2,66}... | collective-permute-start | bytes 405512 | tf_op jit(solution)/shard_map/ppermute | solution.py:31
  27.5 6.8 %collective-permute-start.2 = (bf16[48,1408]{1,0:T(8,128)(2,1)S(1)}, bf16[48,1408]{1,0:T(8,128)(2,1)}, u32[]{:S(2)}, u32[]{:S(2)}) collective-permute-start(bf16[48,1408]{1,0:T(8,128)(2,1)S(1)} %get-tuple-element.225), channel_id=1, source_target_pairs={{0,96},{32,0},{64,32},{96,64},{1,97},{33,1},{65,33},{97,65},{2,98}... | collective-permute-start | bytes 405512 | tf_op jit(solution)/shard_map/ppermute | solution.py:31
  28.8 1.4 copy-start.12
  32.2 53.5 %collective-permute-start.14 = (bf16[44,64,128]{2,1,0:T(8,128)(2,1)}, bf16[44,64,128]{2,1,0:T(8,128)(2,1)}, u32[]{:S(2)}, u32[]{:S(2)}) collective-permute-start(bf16[44,64,128]{2,1,0:T(8,128)(2,1)} %get-tuple-element.173), channel_id=1, source_target_pairs={{0,3},{1,0},{2,1},{3,2},{4,7},{5,4},{6,5},{7,6},{8,11},{9,8},{10,9... | collective-permute-start | bytes 2162696 | tf_op jit(solution)/shard_map/ppermute | solution.py:528
  33.3 102.8 %collective-permute-start.18 = (bf16[44,64,128]{2,1,0:T(8,128)(2,1)}, bf16[44,64,128]{2,1,0:T(8,128)(2,1)}, u32[]{:S(2)}, u32[]{:S(2)}) collective-permute-start(bf16[44,64,128]{2,1,0:T(8,128)(2,1)} %get-tuple-element.179), channel_id=1, source_target_pairs={{0,1},{1,2},{2,3},{3,0},{4,5},{5,6},{6,7},{7,4},{8,9},{9,10},{10,1... | collective-permute-start | bytes 2162696 | tf_op jit(solution)/shard_map/ppermute | solution.py:528
  35.9 5.7 %collective-permute-start.3 = (bf16[48,10,128]{2,1,0:T(8,128)(2,1)S(1)}, bf16[48,10,128]{2,1,0:T(8,128)(2,1)S(1)}, u32[]{:S(2)}, u32[]{:S(2)}) collective-permute-start(bf16[48,10,128]{2,1,0:T(8,128)(2,1)S(1)} %fusion.11), channel_id=1, source_target_pairs={{0,96},{32,0},{64,32},{96,64},{1,97},{33,1},{65,33},{97,65},{2,98}... | collective-permute-start | bytes 368648 | tf_op jit(solution)/shard_map/ppermute | solution.py:41
  41.6 7.2 %collective-permute-start.4 = (bf16[48,10,128]{2,1,0:T(8,128)(2,1)S(1)}, bf16[48,10,128]{2,1,0:T(8,128)(2,1)S(1)}, u32[]{:S(2)}, u32[]{:S(2)}) collective-permute-start(bf16[48,10,128]{2,1,0:T(8,128)(2,1)S(1)} %fusion.11), channel_id=1, source_target_pairs={{0,64},{32,96},{64,0},{96,32},{1,65},{33,97},{65,1},{97,33},{2,66}... | collective-permute-start | bytes 368648 | tf_op jit(solution)/shard_map/ppermute | solution.py:41
  48.8 6.9 %collective-permute-start.5 = (bf16[48,10,128]{2,1,0:T(8,128)(2,1)S(1)}, bf16[48,10,128]{2,1,0:T(8,128)(2,1)S(1)}, u32[]{:S(2)}, u32[]{:S(2)}) collective-permute-start(bf16[48,10,128]{2,1,0:T(8,128)(2,1)S(1)} %fusion.11), channel_id=1, source_target_pairs={{0,32},{32,64},{64,96},{96,0},{1,33},{33,65},{65,97},{97,1},{2,34}... | collective-permute-start | bytes 368648 | tf_op jit(solution)/shard_map/ppermute | solution.py:41
  55.7 80.5 %collective-permute-start.19 = (bf16[44,64,128]{2,1,0:T(8,128)(2,1)}, bf16[44,64,128]{2,1,0:T(8,128)(2,1)}, u32[]{:S(2)}, u32[]{:S(2)}) collective-permute-start(bf16[44,64,128]{2,1,0:T(8,128)(2,1)} %get-tuple-element.180), channel_id=1, source_target_pairs={{0,2},{1,3},{2,0},{3,1},{4,6},{5,7},{6,4},{7,5},{8,10},{9,11},{10,... | collective-permute-start | bytes 2162696 | tf_op jit(solution)/shard_map/ppermute | solution.py:528
  83.7 4.7 %copy-start.1 = (bf16[44,64,128]{2,1,0:T(8,128)(2,1)}, bf16[44,64,128]{2,1,0:T(8,128)(2,1)S(1)}, u32[]{:S(2)}) copy-start(bf16[44,64,128]{2,1,0:T(8,128)(2,1)S(1)} %collective-permute-done.12.refs_1_) | copy-start | bytes 2162692
  83.7 52.5 %collective-permute-start.20 = (bf16[44,64,128]{2,1,0:T(8,128)(2,1)}, bf16[44,64,128]{2,1,0:T(8,128)(2,1)}, u32[]{:S(2)}, u32[]{:S(2)}) collective-permute-start(bf16[44,64,128]{2,1,0:T(8,128)(2,1)} %get-tuple-element.181), channel_id=1, source_target_pairs={{0,3},{1,0},{2,1},{3,2},{4,7},{5,4},{6,5},{7,6},{8,11},{9,8},{10,9... | collective-permute-start | bytes 2162696 | tf_op jit(solution)/shard_map/ppermute | solution.py:528
  83.7 4.6 %copy-start.2 = (bf16[44,64,128]{2,1,0:T(8,128)(2,1)}, bf16[44,64,128]{2,1,0:T(8,128)(2,1)S(1)}, u32[]{:S(2)}) copy-start(bf16[44,64,128]{2,1,0:T(8,128)(2,1)S(1)} %collective-permute-done.13.refs_2_) | copy-start | bytes 2162692
  83.7 9.1 %collective-permute-start.6 = (bf16[400,128]{1,0:T(8,128)(2,1)S(1)}, bf16[400,128]{1,0:T(8,128)(2,1)S(1)}, u32[]{:S(2)}, u32[]{:S(2)}) collective-permute-start(bf16[400,128]{1,0:T(8,128)(2,1)S(1)} %get-tuple-element.235), channel_id=1, source_target_pairs={{0,1},{1,2},{2,3},{3,0},{4,5},{5,6},{6,7},{7,4},{8,9},{9,10},{10,1... | collective-permute-start | bytes 307208 | tf_op jit(solution)/shard_map/ppermute | solution.py:31
  85.7 7.5 %collective-permute-start.7 = (bf16[400,128]{1,0:T(8,128)(2,1)S(1)}, bf16[400,128]{1,0:T(8,128)(2,1)}, u32[]{:S(2)}, u32[]{:S(2)}) collective-permute-start(bf16[400,128]{1,0:T(8,128)(2,1)S(1)} %get-tuple-element.234), channel_id=1, source_target_pairs={{0,2},{1,3},{2,0},{3,1},{4,6},{5,7},{6,4},{7,5},{8,10},{9,11},{10,... | collective-permute-start | bytes 307208 | tf_op jit(solution)/shard_map/ppermute | solution.py:31
  92.8 10.2 %copy-start.10 = (s32[4,4,128]{2,1,0:T(4,128)S(1)}, s32[4,4,128]{2,1,0:T(4,128)}, u32[]{:S(2)}) copy-start(s32[4,4,128]{2,1,0:T(4,128)} %get-tuple-element.244) | copy-start | bytes 24580
  92.8 12.8 %copy-start.8 = (bf16[400,128]{1,0:T(8,128)(2,1)}, bf16[400,128]{1,0:T(8,128)(2,1)S(1)}, u32[]{:S(2)}) copy-start(bf16[400,128]{1,0:T(8,128)(2,1)S(1)} %collective-permute-done.6.refs_1_) | copy-start | bytes 307204
  92.8 53.3 %collective-permute-start.15 = (bf16[40,64,128]{2,1,0:T(8,128)(2,1)}, bf16[40,64,128]{2,1,0:T(8,128)(2,1)}, u32[]{:S(2)}, u32[]{:S(2)}) collective-permute-start(bf16[40,64,128]{2,1,0:T(8,128)(2,1)} %get-tuple-element.175), channel_id=1, source_target_pairs={{0,32},{32,64},{64,96},{96,0},{1,33},{33,65},{65,97},{97,1},{2,34}... | collective-permute-start | bytes 1966088 | tf_op jit(solution)/shard_map/ppermute | solution.py:528
  93.3 12.3 %collective-permute-start.8 = (bf16[400,128]{1,0:T(8,128)(2,1)S(1)}, bf16[400,128]{1,0:T(8,128)(2,1)S(1)}, u32[]{:S(2)}, u32[]{:S(2)}) collective-permute-start(bf16[400,128]{1,0:T(8,128)(2,1)S(1)} %get-tuple-element.233), channel_id=1, source_target_pairs={{0,3},{1,0},{2,1},{3,2},{4,7},{5,4},{6,5},{7,6},{8,11},{9,8},{10,9... | collective-permute-start | bytes 307208 | tf_op jit(solution)/shard_map/ppermute | solution.py:31
  105.6 0.7 copy-start.9
  108.4 6.4 %collective-permute-start.10 = (bf16[400,128]{1,0:T(8,128)(2,1)}, bf16[400,128]{1,0:T(8,128)(2,1)S(1)}, u32[]{:S(2)}, u32[]{:S(2)}) collective-permute-start(bf16[400,128]{1,0:T(8,128)(2,1)} %mix.1.refs_1_), channel_id=1, source_target_pairs={{0,64},{32,96},{64,0},{96,32},{1,65},{33,97},{65,1},{97,33},{2,66}... | collective-permute-start | bytes 307208 | tf_op jit(solution)/shard_map/ppermute | solution.py:637
  114.7 18.4 %copy-start.5 = (bf16[400,128]{1,0:T(8,128)(2,1)}, bf16[400,128]{1,0:T(8,128)(2,1)S(1)}, u32[]{:S(2)}) copy-start(bf16[400,128]{1,0:T(8,128)(2,1)S(1)} %collective-permute-done.10.refs_3_) | copy-start | bytes 307204
  114.7 4.9 %collective-permute-start.11 = (bf16[400,128]{1,0:T(8,128)(2,1)}, bf16[400,128]{1,0:T(8,128)(2,1)S(1)}, u32[]{:S(2)}, u32[]{:S(2)}) collective-permute-start(bf16[400,128]{1,0:T(8,128)(2,1)} %mix.1.refs_1_), channel_id=1, source_target_pairs={{0,96},{32,0},{64,32},{96,64},{1,97},{33,1},{65,33},{97,65},{2,98}... | collective-permute-start | bytes 307208 | tf_op jit(solution)/shard_map/ppermute | solution.py:637
  119.6 13.6 %copy-start.6 = (bf16[400,128]{1,0:T(8,128)(2,1)}, bf16[400,128]{1,0:T(8,128)(2,1)S(1)}, u32[]{:S(2)}) copy-start(bf16[400,128]{1,0:T(8,128)(2,1)S(1)} %collective-permute-done.11.refs_4_) | copy-start | bytes 307204
  119.6 13.6 %collective-permute-start.9 = (bf16[400,128]{1,0:T(8,128)(2,1)}, bf16[400,128]{1,0:T(8,128)(2,1)S(1)}, u32[]{:S(2)}, u32[]{:S(2)}) collective-permute-start(bf16[400,128]{1,0:T(8,128)(2,1)} %mix.1.refs_1_), channel_id=1, source_target_pairs={{0,32},{32,64},{64,96},{96,0},{1,33},{33,65},{65,97},{97,1},{2,34}... | collective-permute-start | bytes 307208 | tf_op jit(solution)/shard_map/ppermute | solution.py:637
  133.2 0.7 copy-start.7
  136.1 10.7 %copy-start.4 = (bf16[48,1024]{1,0:T(8,128)(2,1)S(1)}, bf16[48,1024]{1,0:T(8,128)(2,1)}, u32[]{:S(2)}) copy-start(bf16[48,1024]{1,0:T(8,128)(2,1)} %final.1) | copy-start | bytes 294916
  136.1 26.3 %collective-permute-start.16 = (bf16[40,64,128]{2,1,0:T(8,128)(2,1)}, bf16[40,64,128]{2,1,0:T(8,128)(2,1)S(1)}, u32[]{:S(2)}, u32[]{:S(2)}) collective-permute-start(bf16[40,64,128]{2,1,0:T(8,128)(2,1)} %get-tuple-element.176), channel_id=1, source_target_pairs={{0,64},{32,96},{64,0},{96,32},{1,65},{33,97},{65,1},{97,33},{2,66}... | collective-permute-start | bytes 1966088 | tf_op jit(solution)/shard_map/ppermute | solution.py:528
  136.1 29.7 %collective-permute-start.17 = (bf16[40,64,128]{2,1,0:T(8,128)(2,1)}, bf16[40,64,128]{2,1,0:T(8,128)(2,1)}, u32[]{:S(2)}, u32[]{:S(2)}) collective-permute-start(bf16[40,64,128]{2,1,0:T(8,128)(2,1)} %get-tuple-element.177), channel_id=1, source_target_pairs={{0,96},{32,0},{64,32},{96,64},{1,97},{33,1},{65,33},{97,65},{2,98}... | collective-permute-start | bytes 1966088 | tf_op jit(solution)/shard_map/ppermute | solution.py:528
  140.6 27.3 %collective-permute-start.21 = (bf16[40,64,128]{2,1,0:T(8,128)(2,1)}, bf16[40,64,128]{2,1,0:T(8,128)(2,1)}, u32[]{:S(2)}, u32[]{:S(2)}) collective-permute-start(bf16[40,64,128]{2,1,0:T(8,128)(2,1)} %get-tuple-element.183), channel_id=1, source_target_pairs={{0,32},{32,64},{64,96},{96,0},{1,33},{33,65},{65,97},{97,1},{2,34}... | collective-permute-start | bytes 1966088 | tf_op jit(solution)/shard_map/ppermute | solution.py:528
  142.7 25.3 %collective-permute-start.22 = (bf16[40,64,128]{2,1,0:T(8,128)(2,1)}, bf16[40,64,128]{2,1,0:T(8,128)(2,1)}, u32[]{:S(2)}, u32[]{:S(2)}) collective-permute-start(bf16[40,64,128]{2,1,0:T(8,128)(2,1)} %get-tuple-element.184), channel_id=1, source_target_pairs={{0,64},{32,96},{64,0},{96,32},{1,65},{33,97},{65,1},{97,33},{2,66}... | collective-permute-start | bytes 1966088 | tf_op jit(solution)/shard_map/ppermute | solution.py:528
  146.1 33.8 %collective-permute-start.23 = (bf16[40,64,128]{2,1,0:T(8,128)(2,1)}, bf16[40,64,128]{2,1,0:T(8,128)(2,1)}, u32[]{:S(2)}, u32[]{:S(2)}) collective-permute-start(bf16[40,64,128]{2,1,0:T(8,128)(2,1)} %get-tuple-element.185), channel_id=1, source_target_pairs={{0,96},{32,0},{64,32},{96,64},{1,97},{33,1},{65,33},{97,65},{2,98}... | collective-permute-start | bytes 1966088 | tf_op jit(solution)/shard_map/ppermute | solution.py:528
  149.8 30.1 %copy-start.3 = (bf16[40,64,128]{2,1,0:T(8,128)(2,1)S(1)}, bf16[40,64,128]{2,1,0:T(8,128)(2,1)}, u32[]{:S(2)}) copy-start(bf16[40,64,128]{2,1,0:T(8,128)(2,1)} %get-tuple-element.174) | copy-start | bytes 1966084
  149.8 30.1 %copy-start.13 = (s32[4]{0:T(128)S(1)}, s32[4]{0:T(128)}, u32[]{:S(2)}) copy-start(s32[4]{0:T(128)} %copy-done.12) | copy-start | bytes 52
  150.5 11.1 %all-to-all-start.1 = ((bf16[8,48,256]{2,1,0:T(8,128)(2,1)}), bf16[8,48,256]{2,1,0:T(8,128)(2,1)S(1)}, u32[]{:S(2)}, u32[]{:S(2)}) async-start(bf16[8,48,256]{2,1,0:T(8,128)(2,1)} %bitcast.114), calls=%async_computation.1 | async-start | bytes 393216 | tf_op jit(solution)/shard_map/all_to_all | solution.py:654
where the time goes:
time: 193 us; the launch traced here: 192 us
  waiting for transfers between devices  57.6 us (30%)
  Pallas kernels  55.9 us (29%)
  starting transfers between devices  44.5 us (23%)
  local copies, waits for them, and re-layouts  13.8 us (7%)
  other arithmetic  11.2 us (6%)
  matrix products  6.7 us (3%)
  between operations  2.68 us (1%)
    pallas_call x1, Pallas kernels, attend(): pl.pallas_call(functools.partial(attend_kernel, seqs), out_shape=jax.Shap...  23.4 us
    ppermute x6, starting transfers between devices, exchanged(): lax.ppermute(lax.dynamic_index_in_dim(parts, (here + step) % size, 0, Fal...  19.5 us
    ppermute x3, waiting for transfers between devices, block(): lax.ppermute(both, 'row', ring('row', k))  19.2 us
    ppermute x12, waiting for transfers between devices, passed(): lax.ppermute(part, axis, ring(axis, k))  17.5 us
    ppermute x12, starting transfers between devices, passed(): lax.ppermute(part, axis, ring(axis, k))  15.6 us
    ppermute x3, waiting for transfers between devices, collected(): lax.ppermute(part, axis, ring(axis, size - step))  15.2 us
    pallas_call x1, Pallas kernels, settle(): pl.pallas_call(functools.partial(settle_kernel, count), out_shape=jax.Sha...  11.3 us
    pallas_call x2, Pallas kernels, resplit(): pl.pallas_call(functools.partial(resplit_kernel, count), out_shape=[jax.S...  8.81 us
  transfers between devices with their start and end apart: 25, of which 12 were waited for; matrix products, arithmetic and copies ran while one was open for 13% of the time, Pallas kernels for 20%

commit v1 on v0

--- a/solution.py
+++ b/solution.py
@@ -1,4 +1,5 @@
 import functools
+import math
 
 import jax
 import jax.numpy as jnp
@@ -70,7 +71,7 @@
     requests = q_ref.shape[0]
     row_count = MEM * rows_each
     at_fill, at_code, at_start, at_slot = limit, 2 * limit, 3 * limit, 3 * limit + 8
-    factor = HEAD ** (-0.5)
+    factor = HEAD ** (-0.5) * math.log2(math.e)
     grouped[...] = jnp.zeros_like(grouped)
     for r in range(requests):
         slot = table[at_slot + r]
@@ -105,8 +106,8 @@
             for part in shown:
                 new_max = jnp.maximum(new_max, jnp.max(part, 0, keepdims=True))
             base_max = jnp.where(new_max > 0.5 * NEG, new_max, 0.0)
-            fade = jnp.exp((old_max - base_max) * factor)
-            expo = [jnp.exp((part - base_max) * factor) for part in shown]
+            fade = jnp.exp2((old_max - base_max) * factor)
+            expo = [jnp.exp2((part - base_max) * factor) for part in shown]
             new_sum = old_sum * fade
             for part in expo:
                 new_sum = new_sum + jnp.sum(part, 0, keepdims=True)
@@ -123,7 +124,7 @@
         run_max, run_sum = lax.fori_loop(0, (last - first + TILE - 1) // TILE, visit, start)
         held = run_sum > 0
         safe = jnp.where(held, run_sum, 1.0)
-        lse = jnp.where(held, run_max * factor + jnp.log(safe), NEG)
+        lse = jnp.where(held, run_max * HEAD ** (-0.5) + jnp.log(safe), NEG)
         gathered[pl.ds(g * row_count, row_count), :] = (acc[...] * (1.0 / safe)).T
         for k in range(row_count // HEAD):
             lse_rows[pl.ds(g * (row_count // HEAD) + k, 1), :] = lse[:, k * HEAD : (k + 1) * HEAD]
@@ -147,7 +148,7 @@
         out_ref[s, pl.ds(each * rows_each, 16), :] = packed_tail(tails)
 
 
-TILE = 4
+TILE = 8
 
 
 def attend(table, queries, pool, seqs):
@@ -388,18 +389,26 @@
     return fits, first, second, third.reshape(pool_size), coming.reshape(rows * seqs)
 
 
-def split_kernel(table, pool_ref, *out_refs):
+def split_kernel(table, pool_ref, *refs):
+    out_refs, scratch, arrived, sems = refs[:-3], refs[-3], refs[-2], refs[-1]
     lists = len(out_refs) // 2
     length = out_refs[0].shape[0]
+    copy = pltpu.make_async_copy(pool_ref.at[pl.ds(0, scratch.shape[0])], scratch, arrived)
+    copy.start()
+    copy.wait()
     for k in range(lists):
 
         def move(i, _):
             page = table[k * length + i]
-            out_refs[k][i] = pool_ref[page, 0]
-            out_refs[lists + k][i] = pool_ref[page, 1]
+            for half in range(2):
+                pltpu.make_async_copy(
+                    scratch.at[page, half], out_refs[half * lists + k].at[i], sems.at[half * lists + k]
+                ).start()
             return 0
 
         lax.fori_loop(0, length, move, 0, unroll=4)
+    for k, out in enumerate(out_refs):
+        pltpu.make_async_copy(out, out, sems.at[k]).wait()
 
 
 def split_pool(table, pool, lists):
@@ -412,8 +421,13 @@
         grid_spec=pltpu.PrefetchScalarGridSpec(
             num_scalar_prefetch=1,
             grid=(1,),
-            in_specs=[pl.BlockSpec((limit,) + pool.shape[1:], lambda i, t: (0, 0, 0, 0))],
-            out_specs=[pl.BlockSpec(shape, lambda i, t: (0, 0, 0))] * (2 * lists),
+            in_specs=[pl.BlockSpec(memory_space=pl.ANY)],
+            out_specs=[pl.BlockSpec(memory_space=pl.ANY)] * (2 * lists),
+            scratch_shapes=[
+                pltpu.VMEM((limit,) + pool.shape[1:], pool.dtype),
+                pltpu.SemaphoreType.DMA,
+                pltpu.SemaphoreType.DMA((2 * lists,)),
+            ],
         ),
         cost_estimate=pl.CostEstimate(
             flops=0, bytes_accessed=pool.size + 4 * lists * length * page_len * width, transcendentals=0
@@ -424,10 +438,10 @@
 
 def resplit_kernel(count, table, *refs):
     sources, outs = refs[:count], refs[count : 2 * count]
-    scratch, sems = refs[2 * count], refs[2 * count + 1]
+    scratch, arrived, sems = refs[2 * count :]
     length = sources[0].shape[0]
     copies = [
-        pltpu.make_async_copy(ref, scratch.at[pl.ds(k * length, length)], sems.at[k])
+        pltpu.make_async_copy(ref, scratch.at[pl.ds(k * length, length)], arrived.at[k])
         for k, ref in enumerate(sources)
     ]
     for copy in copies:
@@ -438,10 +452,14 @@
     for k, out in enumerate(outs):
 
         def move(i, _):
-            out[i] = scratch[table[k * length_out + i]]
+            pltpu.make_async_copy(
+                scratch.at[table[k * length_out + i]], out.at[i], sems.at[k]
+            ).start()
             return 0
 
         lax.fori_loop(0, length_out, move, 0, unroll=4)
+    for k, out in enumerate(outs):
+        pltpu.make_async_copy(out, out, sems.at[k]).wait()
 
 
 def resplit(table, lists):
@@ -455,10 +473,11 @@
             num_scalar_prefetch=1,
             grid=(1,),
             in_specs=[pl.BlockSpec(memory_space=pl.ANY)] * count,
-            out_specs=[pl.BlockSpec(shape, lambda i, t: (0, 0, 0))] * count,
+            out_specs=[pl.BlockSpec(memory_space=pl.ANY)] * count,
             scratch_shapes=[
                 pltpu.VMEM((count * length, page_len, width), lists[0].dtype),
                 pltpu.SemaphoreType.DMA((count,)),
+                pltpu.SemaphoreType.DMA((count,)),
             ],
         ),
         cost_estimate=pl.CostEstimate(
@@ -469,51 +488,56 @@
 
 
 def settle_kernel(count, table, *refs):
-    sources, out, scratch, sems = refs[: 2 * count], refs[-3], refs[-2], refs[-1]
+    sources, out, scratch, zero, sems, done = refs[: 2 * count], refs[-5], refs[-4], refs[-3], refs[-2], refs[-1]
     length = sources[0].shape[0]
-    block = out.shape[0]
-
-    @pl.when(pl.program_id(0) == 0)
-    def _():
-        copies = [
-            pltpu.make_async_copy(
-                ref, scratch.at[k // count, pl.ds(k % count * length, length)], sems.at[k]
-            )
-            for k, ref in enumerate(sources)
-        ]
-        for copy in copies:
-            copy.start()
-        for copy in copies:
-            copy.wait()
-
-    for i in range(block):
-        place = table[pl.program_id(0) * block + i]
+    copies = [
+        pltpu.make_async_copy(
+            ref, scratch.at[k // count, pl.ds(k % count * length, length)], sems.at[k]
+        )
+        for k, ref in enumerate(sources)
+    ]
+    for copy in copies:
+        copy.start()
+    zero[...] = jnp.zeros_like(zero)
+    for copy in copies:
+        copy.wait()
+
+    def place_page(i, _):
+        place = table[i]
 
         @pl.when(place >= 0)
         def _():
             for half in range(2):
-                out[i, half] = scratch[half, place]
+                pltpu.make_async_copy(scratch.at[half, place], out.at[i, half], done).start()
 
         @pl.when(place < 0)
         def _():
-            out[i] = jnp.zeros(out.shape[1:], out.dtype)
-
-
-def settle(table, keys, values, block):
+            pltpu.make_async_copy(zero, out.at[i], done).start()
+
+        return 0
+
+    lax.fori_loop(0, out.shape[0], place_page, 0, unroll=4)
+    pltpu.make_async_copy(out, out, done).wait()
+
+
+def settle(table, keys, values):
     count = len(keys)
     length, page_len, width = keys[0].shape
     slots = table.shape[0]
+    kind = keys[0].dtype
     return pl.pallas_call(
         functools.partial(settle_kernel, count),
-        out_shape=jax.ShapeDtypeStruct((slots, 2, page_len, width), keys[0].dtype),
+        out_shape=jax.ShapeDtypeStruct((slots, 2, page_len, width), kind),
         grid_spec=pltpu.PrefetchScalarGridSpec(
             num_scalar_prefetch=1,
-            grid=(slots // block,),
+            grid=(1,),
             in_specs=[pl.BlockSpec(memory_space=pl.ANY)] * (2 * count),
-            out_specs=pl.BlockSpec((block, 2, page_len, width), lambda i, t: (i, 0, 0, 0)),
+            out_specs=pl.BlockSpec(memory_space=pl.ANY),
             scratch_shapes=[
-                pltpu.VMEM((2, count * length, page_len, width), keys[0].dtype),
+                pltpu.VMEM((2, count * length, page_len, width), kind),
+                pltpu.VMEM((2, page_len, width), kind),
                 pltpu.SemaphoreType.DMA((2 * count,)),
+                pltpu.SemaphoreType.DMA,
             ],
         ),
         cost_estimate=pl.CostEstimate(
@@ -632,10 +656,6 @@
     both = attend(table, rows_first, kv_pool, seq_size)
     parts = [lax.dynamic_index_in_dim(both, lax.axis_index("seq"), 0, False)]
     parts += exchanged(both, "seq")
-    value_lists = resplit(second_table, value_lists)
-    both = mix(parts)
-    parts = [both] + [lax.ppermute(both, "row", ring("row", k)) for k in range(1, 4)]
-    value_lists = passed(value_lists, "row")
     query_own = lax.dynamic_slice_in_dim(rows_first, req_start, local_req, 0)
     key_own = lax.dynamic_slice_in_dim(keys_new, req_start, local_req, 1)
     value_own = lax.dynamic_slice_in_dim(values_new, req_start, local_req, 1)
@@ -645,6 +665,10 @@
         value_own.reshape(step_count * local_req, HEAD),
         step_count,
     )
+    value_lists = resplit(second_table, value_lists)
+    both = mix(parts)
+    parts = [both] + [lax.ppermute(both, "row", ring("row", k)) for k in range(1, 4)]
+    value_lists = passed(value_lists, "row")
     picked = final([own] + parts, ratio)
     partial_out = jnp.dot(picked, w_out, preferred_element_type=jnp.float32).astype(jnp.bfloat16)
     col_size = lax.axis_size("col")
@@ -663,7 +687,7 @@
     layer_out = (summed + residual).astype(jnp.bfloat16)
     moved = lax.cond(
         fits,
-        lambda: settle(third_table, key_lists, value_lists, kv_pool.shape[0] // coming.shape[0]),
+        lambda: settle(third_table, key_lists, value_lists),
         lambda: migrate_whole(kv_pool, migrate_dest, coming, device),
     )
     return (layer_out, new_kv_local, moved)

time: 193 us -> 183 us (0.948)
  Pallas kernels: 55.9 us -> 44.2 us
    pallas_call x1, Pallas kernels: 23.4 us -> 18.2 us  [attend(): pl.pallas_call(functools.partial(attend_kernel, seqs), out_shape=jax.Shap...]
    pallas_call x1, Pallas kernels: 11.3 us -> 6.26 us  [settle(): pl.pallas_call(functools.partial(settle_kernel, count), out_shape=jax.Sha...]
  transfers between devices with their start and end apart: 25 -> 25, of which waited for: 12 -> 12; matrix products, arithmetic and copies ran while one was open for 13% -> 13% of each run, Pallas kernels for 20% -> 18%
where the time goes in v1:
time: 183 us; the launch traced here: 182 us
  waiting for transfers between devices  58.2 us (32%)
  starting transfers between devices  44.8 us (24%)
  Pallas kernels  44.2 us (24%)
  local copies, waits for them, and re-layouts  13.8 us (8%)
  other arithmetic  11.2 us (6%)
  matrix products  6.7 us (4%)
  between operations  2.68 us (1%)
    ppermute x6, starting transfers between devices, exchanged(): lax.ppermute(lax.dynamic_index_in_dim(parts, (here + step) % size, 0, Fal...  20.1 us
    ppermute x3, waiting for transfers between devices, block(): lax.ppermute(both, 'row', ring('row', k))  19.4 us
    pallas_call x1, Pallas kernels, attend(): pl.pallas_call(functools.partial(attend_kernel, seqs), out_shape=jax.Shap...  18.2 us
    ppermute x12, waiting for transfers between devices, passed(): lax.ppermute(part, axis, ring(axis, k))  18 us
    ppermute x12, starting transfers between devices, passed(): lax.ppermute(part, axis, ring(axis, k))  15.5 us
    ppermute x3, waiting for transfers between devices, collected(): lax.ppermute(part, axis, ring(axis, size - step))  15.2 us
    pallas_call x2, Pallas kernels, resplit(): pl.pallas_call(functools.partial(resplit_kernel, count), out_shape=[jax.S...  8 us
    pallas_call x1, Pallas kernels, settle(): pl.pallas_call(functools.partial(settle_kernel, count), out_shape=jax.Sha...  6.26 us
  transfers between devices with their start and end apart: 25, of which 12 were waited for; matrix products, arithmetic and copies ran while one was open for 13% of the time, Pallas kernels for 18%

profile of v1, /device:TPU:0, one launch (start us, length us, event | category | flops | bytes accessed | tf_op | source)
XLA Modules:
  0.0 181.6 jit_solution(17546267319331359260)
XLA Ops:
  0.6 0.7 broadcast_compare_fusion.1
  1.4 0.8 dynamic_slice.75
  2.1 0.9 convert_reduce_fusion.7
  3.0 0.7 multiply_add_fusion.1
  3.7 0.7 reshape.599
  4.9 0.7 select_reduce_fusion.2.table
  5.6 5.5 %split_pool.1 = (bf16[44,64,128]{2,1,0:T(8,128)(2,1)}, bf16[44,64,128]{2,1,0:T(8,128)(2,1)}, bf16[44,64,128]{2,1,0:T(8,128)(2,1)}, bf16[44,64,128]{2,1,0:T(8,128...) custom-call(s32[176]{0:T(256)} %select_reduce_fusion.2.table, ...), custom_call_target="tpu_custom_call" | custom-call | bytes 9961472 | tf_op jit(solution)/shard_map/split_pool/pallas_call | solution.py:418
  11.1 2.1 %collective-permute-start.12 = (bf16[44,64,128]{2,1,0:T(8,128)(2,1)}, bf16[44,64,128]{2,1,0:T(8,128)(2,1)S(1)}, u32[]{:S(2)}, u32[]{:S(2)}) collective-permute-start(bf16[44,64,128]{2,1,0:T(8,128)(2,1)} %get-tuple-element.171), channel_id=1, source_target_pairs={{0,1},{1,2},{2,3},{3,0},{4,5},{5,6},{6,7},{7,4},{8,9},{9,10},{10,1... | collective-permute-start | bytes 2162696 | tf_op jit(solution)/shard_map/ppermute | solution.py:552
  13.2 3.6 %collective-permute-start.13 = (bf16[44,64,128]{2,1,0:T(8,128)(2,1)}, bf16[44,64,128]{2,1,0:T(8,128)(2,1)S(1)}, u32[]{:S(2)}, u32[]{:S(2)}) collective-permute-start(bf16[44,64,128]{2,1,0:T(8,128)(2,1)} %get-tuple-element.172), channel_id=1, source_target_pairs={{0,2},{1,3},{2,0},{3,1},{4,6},{5,7},{6,4},{7,5},{8,10},{9,11},{10,... | collective-permute-start | bytes 2162696 | tf_op jit(solution)/shard_map/ppermute | solution.py:552
  16.8 0.7 dynamic-slice_convert_fusion
  18.0 3.7 %convolution_convert_fusion = bf16[192,1280]{1,0:T(8,128)(2,1)S(1)} fusion(bf16[192,2048]{1,0:T(8,128)(2,1)S(1)} %bitcast.123, bf16[2048,1280]{1,0:T(8,128)(2,1)} %param.14), kind=kOutput, calls=%fused_computation.22 | convolution fusion | flops 1006878720 | bytes 6520832 | tf_op jit(solution)/shard_map/dot_general | solution.py:604
  21.7 0.7 dynamic-slice_bitcast_fusion.2
  22.4 1.6 collective-permute-start
  24.0 2.9 %collective-permute-start.1 = (bf16[48,1408]{1,0:T(8,128)(2,1)S(1)}, bf16[48,1408]{1,0:T(8,128)(2,1)S(1)}, u32[]{:S(2)}, u32[]{:S(2)}) collective-permute-start(bf16[48,1408]{1,0:T(8,128)(2,1)S(1)} %get-tuple-element.226), channel_id=1, source_target_pairs={{0,64},{32,96},{64,0},{96,32},{1,65},{33,97},{65,1},{97,33},{2,66}... | collective-permute-start | bytes 405512 | tf_op jit(solution)/shard_map/ppermute | solution.py:32
  26.9 1.3 collective-permute-start.2
  29.7 0.8 dynamic_slice.76
  30.9 0.7 concatenate.27.table
  31.6 1.0 collective-permute-start.14
  32.7 0.9 collective-permute-start.18
  33.7 1.0 fusion.13
  35.3 1.6 collective-permute-start.3
  37.1 4.0 %collective-permute-done.3 = bf16[48,10,128]{2,1,0:T(8,128)(2,1)S(1)} collective-permute-done((bf16[48,10,128]{2,1,0:T(8,128)(2,1)S(1)}, bf16[48,10,128]{2,1,0:T(8,128)(2,1)S(1)}, u32[]{:S(2)}, u32[]{:S(2)}) %collective-permute-start.3) | collective-permute-done | bytes 122912 | tf_op jit(solution)/shard_map/ppermute | solution.py:42
  41.1 2.1 %collective-permute-start.4 = (bf16[48,10,128]{2,1,0:T(8,128)(2,1)S(1)}, bf16[48,10,128]{2,1,0:T(8,128)(2,1)S(1)}, u32[]{:S(2)}, u32[]{:S(2)}) collective-permute-start(bf16[48,10,128]{2,1,0:T(8,128)(2,1)S(1)} %fusion.11), channel_id=1, source_target_pairs={{0,64},{32,96},{64,0},{96,32},{1,65},{33,97},{65,1},{97,33},{2,66}... | collective-permute-start | bytes 368648 | tf_op jit(solution)/shard_map/ppermute | solution.py:42
  43.2 5.0 %collective-permute-done.4 = bf16[48,10,128]{2,1,0:T(8,128)(2,1)S(1)} collective-permute-done((bf16[48,10,128]{2,1,0:T(8,128)(2,1)S(1)}, bf16[48,10,128]{2,1,0:T(8,128)(2,1)S(1)}, u32[]{:S(2)}, u32[]{:S(2)}) %collective-permute-start.4) | collective-permute-done | bytes 122912 | tf_op jit(solution)/shard_map/ppermute | solution.py:42
  48.3 0.7 collective-permute-start.5
  49.0 6.2 %collective-permute-done.5 = bf16[48,10,128]{2,1,0:T(8,128)(2,1)S(1)} collective-permute-done((bf16[48,10,128]{2,1,0:T(8,128)(2,1)S(1)}, bf16[48,10,128]{2,1,0:T(8,128)(2,1)S(1)}, u32[]{:S(2)}, u32[]{:S(2)}) %collective-permute-start.5) | collective-permute-done | bytes 122912 | tf_op jit(solution)/shard_map/ppermute | solution.py:42
  55.1 1.6 collective-permute-start.19
  57.1 0.9 copy.58
  58.0 18.2 %attend.1 = bf16[4,400,128]{2,1,0:T(8,128)(2,1)} custom-call(s32[440]{0:T(512)} %concatenate.27.table, bf16[48,32,128]{2,1,0:T(8,128)(2,1)} %bitcast.116, bf16[256,2,64,128]{3,2,1,0:T(8,128)(2,1)} %pool_ref.3), custom_call_target="tpu_custom_call" | custom-call | flops 2147483648 | bytes 4194304 | tf_op jit(solution)/shard_map/attend/pallas_call | solution.py:158
  76.2 1.7 dynamic-slice_bitcast_fusion.3
  77.9 2.0 %collective-permute-start.6 = (bf16[400,128]{1,0:T(8,128)(2,1)S(1)}, bf16[400,128]{1,0:T(8,128)(2,1)S(1)}, u32[]{:S(2)}, u32[]{:S(2)}) collective-permute-start(bf16[400,128]{1,0:T(8,128)(2,1)S(1)} %get-tuple-element.235), channel_id=1, source_target_pairs={{0,1},{1,2},{2,3},{3,0},{4,5},{5,6},{6,7},{7,4},{8,9},{9,10},{10,1... | collective-permute-start | bytes 307208 | tf_op jit(solution)/shard_map/ppermute | solution.py:32
  79.9 2.0 %collective-permute-start.7 = (bf16[400,128]{1,0:T(8,128)(2,1)S(1)}, bf16[400,128]{1,0:T(8,128)(2,1)}, u32[]{:S(2)}, u32[]{:S(2)}) collective-permute-start(bf16[400,128]{1,0:T(8,128)(2,1)S(1)} %get-tuple-element.234), channel_id=1, source_target_pairs={{0,2},{1,3},{2,0},{3,1},{4,6},{5,7},{6,4},{7,5},{8,10},{9,11},{10,... | collective-permute-start | bytes 307208 | tf_op jit(solution)/shard_map/ppermute | solution.py:32
  81.9 0.6 select_reduce_fusion.1.table
  82.5 4.1 %resplit.2 = (bf16[40,64,128]{2,1,0:T(8,128)(2,1)}, bf16[40,64,128]{2,1,0:T(8,128)(2,1)}, bf16[40,64,128]{2,1,0:T(8,128)(2,1)}, bf16[40,64,128]{2,1,0:T(8,128)(2,1)}) custom-call(s32[160]{0:T(256)} %select_reduce_fusion.1.table, bf16[44,64,128]{2,1,0:T(8,128)(2,1)} %get-tuple-element.170.refs_0_, bf16[44,64,128]{2,1,0:T(8,128)(2,1)} %copy-done.1, ...), custom_call_target="tpu_custom_call" | custom-call | bytes 5767168 | tf_op jit(solution)/shard_map/resplit/pallas_call | solution.py:469
  86.9 10.3 %collective-permute-start.8 = (bf16[400,128]{1,0:T(8,128)(2,1)S(1)}, bf16[400,128]{1,0:T(8,128)(2,1)S(1)}, u32[]{:S(2)}, u32[]{:S(2)}) collective-permute-start(bf16[400,128]{1,0:T(8,128)(2,1)S(1)} %get-tuple-element.233), channel_id=1, source_target_pairs={{0,3},{1,0},{2,1},{3,2},{4,7},{5,4},{6,5},{7,6},{8,11},{9,8},{10,9... | collective-permute-start | bytes 307208 | tf_op jit(solution)/shard_map/ppermute | solution.py:32
  97.5 0.7 reduce_max.18
  98.3 1.5 collective-permute-done.8.refs_3_
  99.8 0.6 copy-done.9
  100.4 2.1 %mix.1.refs_1_ = bf16[400,128]{1,0:T(8,128)(2,1)} custom-call(bf16[400,128]{1,0:T(8,128)(2,1)} %get-tuple-element.236.refs_0_, bf16[400,128]{1,0:T(8,128)(2,1)} %copy-done.8, bf16[400,128]{1,0:T(8,128)(2,1)} %collective-permute-done.7.refs_2_, bf16[400,128]{1,0:T(8,128)(2,1)} %copy-done.9), custom_call_target="tpu_custom_call" | custom-call | flops 409600 | bytes 512000 | tf_op jit(solution)/shard_map/mix/pallas_call | solution.py:266
  102.8 6.1 %collective-permute-done.10.refs_3_ = bf16[400,128]{1,0:T(8,128)(2,1)S(1)} collective-permute-done((bf16[400,128]{1,0:T(8,128)(2,1)}, bf16[400,128]{1,0:T(8,128)(2,1)S(1)}, u32[]{:S(2)}, u32[]{:S(2)}) %collective-permute-start.10) | collective-permute-done | bytes 102432 | tf_op jit(solution)/shard_map/ppermute | solution.py:670
  108.9 0.6 reshape.594.k_ref
  110.2 3.6 %collective-permute-done.11.refs_4_ = bf16[400,128]{1,0:T(8,128)(2,1)S(1)} collective-permute-done((bf16[400,128]{1,0:T(8,128)(2,1)}, bf16[400,128]{1,0:T(8,128)(2,1)S(1)}, u32[]{:S(2)}, u32[]{:S(2)}) %collective-permute-start.11) | collective-permute-done | bytes 102432 | tf_op jit(solution)/shard_map/ppermute | solution.py:670
  114.1 1.5 constant_dynamic-slice_fusion.4
  115.6 2.0 %fresh.1.refs_0_ = bf16[400,128]{1,0:T(8,128)(2,1)} custom-call(bf16[384,128]{1,0:T(8,128)(2,1)} %bitcast.125, bf16[48,128]{1,0:T(8,128)(2,1)} %reshape.594.k_ref, bf16[48,128]{1,0:T(8,128)(2,1)} %reshape.595.v_ref), custom_call_target="tpu_custom_call" | custom-call | flops 9437184 | bytes 196608 | tf_op jit(solution)/shard_map/fresh/pallas_call | solution.py:217
  117.6 9.7 %collective-permute-done.9.refs_2_ = bf16[400,128]{1,0:T(8,128)(2,1)S(1)} collective-permute-done((bf16[400,128]{1,0:T(8,128)(2,1)}, bf16[400,128]{1,0:T(8,128)(2,1)S(1)}, u32[]{:S(2)}, u32[]{:S(2)}) %collective-permute-start.9) | collective-permute-done | bytes 102432 | tf_op jit(solution)/shard_map/ppermute | solution.py:670
  127.4 0.7 copy-done.7
  128.0 2.3 %final.1 = bf16[48,1024]{1,0:T(8,128)(2,1)} custom-call(bf16[400,128]{1,0:T(8,128)(2,1)} %fresh.1.refs_0_, bf16[400,128]{1,0:T(8,128)(2,1)} %mix.1.refs_1_, bf16[400,128]{1,0:T(8,128)(2,1)} %copy-done.7, bf16[400,128]{1,0:T(8,128)(2,1)} %copy-done.5, bf16[400,128]{1,0:T(8,128)(2,1)} %copy-done.6), custom_call_target="tpu_custom_call" | custom-call | flops 512000 | bytes 512000 | tf_op jit(solution)/shard_map/final/pallas_call | solution.py:290
  130.4 4.0 %resplit.3 = (bf16[40,64,128]{2,1,0:T(8,128)(2,1)}, bf16[40,64,128]{2,1,0:T(8,128)(2,1)}, bf16[40,64,128]{2,1,0:T(8,128)(2,1)}, bf16[40,64,128]{2,1,0:T(8,128)(2,1)}) custom-call(s32[160]{0:T(256)} %select_reduce_fusion.1.table, bf16[44,64,128]{2,1,0:T(8,128)(2,1)} %get-tuple-element.178.refs_0_, bf16[44,64,128]{2,1,0:T(8,128)(2,1)} %collective-permute-done.18.refs_1_, ...), custom_call_target="tpu_custom_call" | custom-call | bytes 5767168 | tf_op jit(solution)/shard_map/resplit/pallas_call | solution.py:469
  134.4 2.1 %collective-permute-start.21 = (bf16[40,64,128]{2,1,0:T(8,128)(2,1)}, bf16[40,64,128]{2,1,0:T(8,128)(2,1)}, u32[]{:S(2)}, u32[]{:S(2)}) collective-permute-start(bf16[40,64,128]{2,1,0:T(8,128)(2,1)} %get-tuple-element.183), channel_id=1, source_target_pairs={{0,32},{32,64},{64,96},{96,0},{1,33},{33,65},{65,97},{97,1},{2,34}... | collective-permute-start | bytes 1966088 | tf_op jit(solution)/shard_map/ppermute | solution.py:552
  136.4 3.5 %collective-permute-start.22 = (bf16[40,64,128]{2,1,0:T(8,128)(2,1)}, bf16[40,64,128]{2,1,0:T(8,128)(2,1)}, u32[]{:S(2)}, u32[]{:S(2)}) collective-permute-start(bf16[40,64,128]{2,1,0:T(8,128)(2,1)} %get-tuple-element.184), channel_id=1, source_target_pairs={{0,64},{32,96},{64,0},{96,32},{1,65},{33,97},{65,1},{97,33},{2,66}... | collective-permute-start | bytes 1966088 | tf_op jit(solution)/shard_map/ppermute | solution.py:552
  139.9 0.6 collective-permute-start.23
  140.5 3.0 %convolution_convert_fusion.1 = bf16[48,2048]{1,0:T(8,128)(2,1)S(1)} fusion(bf16[48,1024]{1,0:T(8,128)(2,1)S(1)} %copy-done.4, bf16[1024,2048]{1,0:T(8,128)(2,1)} %param.15), kind=kOutput, calls=%fused_computation.23 | convolution fusion | flops 201424896 | bytes 4489216 | tf_op jit(solution)/shard_map/dot_general | solution.py:673
  143.6 0.7 copy.59
  144.2 4.3 %all-to-all-start.1 = ((bf16[8,48,256]{2,1,0:T(8,128)(2,1)}), bf16[8,48,256]{2,1,0:T(8,128)(2,1)S(1)}, u32[]{:S(2)}, u32[]{:S(2)}) async-start(bf16[8,48,256]{2,1,0:T(8,128)(2,1)} %bitcast.114), calls=%async_computation.1 | async-start | bytes 393216 | tf_op jit(solution)/shard_map/all_to_all | solution.py:678
  148.7 0.6 reduce_max.19
  150.7 0.6 copy.48
  151.3 4.0 %all-to-all-done.1 = bf16[8,48,256]{2,1,0:T(8,128)(2,1)S(1)} async-done(((bf16[8,48,256]{2,1,0:T(8,128)(2,1)}), bf16[8,48,256]{2,1,0:T(8,128)(2,1)S(1)}, u32[]{:S(2)}, u32[]{:S(2)}) %all-to-all-start.1) | async-done | bytes 196640 | tf_op jit(solution)/shard_map/all_to_all | solution.py:678
  155.5 0.6 copy.47
  156.1 3.8 %collective-permute-done.17 = bf16[40,64,128]{2,1,0:T(8,128)(2,1)} collective-permute-done((bf16[40,64,128]{2,1,0:T(8,128)(2,1)}, bf16[40,64,128]{2,1,0:T(8,128)(2,1)}, u32[]{:S(2)}, u32[]{:S(2)}) %collective-permute-start.17) | collective-permute-done | bytes 655392 | tf_op jit(solution)/shard_map/ppermute | solution.py:552
  160.0 2.1 %collective-permute-done.21 = bf16[40,64,128]{2,1,0:T(8,128)(2,1)} collective-permute-done((bf16[40,64,128]{2,1,0:T(8,128)(2,1)}, bf16[40,64,128]{2,1,0:T(8,128)(2,1)}, u32[]{:S(2)}, u32[]{:S(2)}) %collective-permute-start.21) | collective-permute-done | bytes 655392 | tf_op jit(solution)/shard_map/ppermute | solution.py:552
  162.1 12.0 %collective-permute-done.23 = bf16[40,64,128]{2,1,0:T(8,128)(2,1)} collective-permute-done((bf16[40,64,128]{2,1,0:T(8,128)(2,1)}, bf16[40,64,128]{2,1,0:T(8,128)(2,1)}, u32[]{:S(2)}, u32[]{:S(2)}) %collective-permute-start.23) | collective-permute-done | bytes 655392 | tf_op jit(solution)/shard_map/ppermute | solution.py:552
  174.1 7.4 %conditional.1 = (bf16[256,2,64,128]{3,2,1,0:T(8,128)(2,1)}) conditional(s32[]{:T(128)} %convert_element_type.144, (s32[4,4]{1,0:T(4,128)S(1)}, s32[]{:T(128)}, s32[4096]{0:T(1024)}, bf16[256,2,64,128]{3,2,1,0:T(8,128)(2,1)}) %tuple.49, (s32[4,4]{1,0:T(4,128)S(1)}, s32[4,4,16]{2,1,0:T(4,128)S(1)}, s32[]{:T(128)}, s32[]{:T(128)}, s32[]{:T(128)}, ...), branch_computations={%region_21.23_spmd, %region_23.25_spmd} | conditional | flops 4198404 | bytes 58736920 | solution.py:688
  174.5 0.7 select_n.300.table
  175.2 6.3 %settle.1 = bf16[256,2,64,128]{3,2,1,0:T(8,128)(2,1)} custom-call(s32[256]{0:T(256)} %select_n.300.table, bf16[40,64,128]{2,1,0:T(8,128)(2,1)S(1)} %get-tuple-element.139.refs_0_, bf16[40,64,128]{2,1,0:T(8,128)(2,1)} %get-tuple-element.140.refs_1_, bf16[40,64,128]{2,1,0:T(8,128)(2,1)S(1)} %get-tuple-element.141.refs_2_, ...), custom_call_target="tpu_custom_call" | custom-call | bytes 16777216 | tf_op jit(solution)/shard_map/cond/branch_1_fun/settle/pallas_call | solution.py:528
  (113 shorter events, 6.9 us)
Async XLA Ops:
  5.6 11.9 %copy-start = (bf16[4,48,2048]{2,1,0:T(8,128)(2,1)S(1)}, bf16[4,48,2048]{2,1,0:T(8,128)(2,1)}, u32[]{:S(2)}) copy-start(bf16[4,48,2048]{2,1,0:T(8,128)(2,1)} %param.12) | copy-start | bytes 2359300
  11.1 66.8 %collective-permute-start.12 = (bf16[44,64,128]{2,1,0:T(8,128)(2,1)}, bf16[44,64,128]{2,1,0:T(8,128)(2,1)S(1)}, u32[]{:S(2)}, u32[]{:S(2)}) collective-permute-start(bf16[44,64,128]{2,1,0:T(8,128)(2,1)} %get-tuple-element.171), channel_id=1, source_target_pairs={{0,1},{1,2},{2,3},{3,0},{4,5},{5,6},{6,7},{7,4},{8,9},{9,10},{10,1... | collective-permute-start | bytes 2162696 | tf_op jit(solution)/shard_map/ppermute | solution.py:552
  13.2 64.7 %collective-permute-start.13 = (bf16[44,64,128]{2,1,0:T(8,128)(2,1)}, bf16[44,64,128]{2,1,0:T(8,128)(2,1)S(1)}, u32[]{:S(2)}, u32[]{:S(2)}) collective-permute-start(bf16[44,64,128]{2,1,0:T(8,128)(2,1)} %get-tuple-element.172), channel_id=1, source_target_pairs={{0,2},{1,3},{2,0},{3,1},{4,6},{5,7},{6,4},{7,5},{8,10},{9,11},{10,... | collective-permute-start | bytes 2162696 | tf_op jit(solution)/shard_map/ppermute | solution.py:552
  21.6 7.8 %copy-start.11 = (s32[48]{0:T(128)S(1)}, s32[48]{0:T(128)}, u32[]{:S(2)}) copy-start(s32[48]{0:T(128)} %param.19) | copy-start | bytes 580
  22.4 9.2 %collective-permute-start = (bf16[48,1408]{1,0:T(8,128)(2,1)}, bf16[48,1408]{1,0:T(8,128)(2,1)S(1)}, u32[]{:S(2)}, u32[]{:S(2)}) collective-permute-start(bf16[48,1408]{1,0:T(8,128)(2,1)} %get-tuple-element.224), channel_id=1, source_target_pairs={{0,32},{32,64},{64,96},{96,0},{1,33},{33,65},{65,97},{97,1},{2,34}... | collective-permute-start | bytes 405512 | tf_op jit(solution)/shard_map/ppermute | solution.py:32
  24.0 8.7 %collective-permute-start.1 = (bf16[48,1408]{1,0:T(8,128)(2,1)S(1)}, bf16[48,1408]{1,0:T(8,128)(2,1)S(1)}, u32[]{:S(2)}, u32[]{:S(2)}) collective-permute-start(bf16[48,1408]{1,0:T(8,128)(2,1)S(1)} %get-tuple-element.226), channel_id=1, source_target_pairs={{0,64},{32,96},{64,0},{96,32},{1,65},{33,97},{65,1},{97,33},{2,66}... | collective-permute-start | bytes 405512 | tf_op jit(solution)/shard_map/ppermute | solution.py:32
  26.9 6.8 %collective-permute-start.2 = (bf16[48,1408]{1,0:T(8,128)(2,1)S(1)}, bf16[48,1408]{1,0:T(8,128)(2,1)}, u32[]{:S(2)}, u32[]{:S(2)}) collective-permute-start(bf16[48,1408]{1,0:T(8,128)(2,1)S(1)} %get-tuple-element.225), channel_id=1, source_target_pairs={{0,96},{32,0},{64,32},{96,64},{1,97},{33,1},{65,33},{97,65},{2,98}... | collective-permute-start | bytes 405512 | tf_op jit(solution)/shard_map/ppermute | solution.py:32
  28.3 1.4 copy-start.12
  31.6 48.3 %collective-permute-start.14 = (bf16[44,64,128]{2,1,0:T(8,128)(2,1)}, bf16[44,64,128]{2,1,0:T(8,128)(2,1)}, u32[]{:S(2)}, u32[]{:S(2)}) collective-permute-start(bf16[44,64,128]{2,1,0:T(8,128)(2,1)} %get-tuple-element.173), channel_id=1, source_target_pairs={{0,3},{1,0},{2,1},{3,2},{4,7},{5,4},{6,5},{7,6},{8,11},{9,8},{10,9... | collective-permute-start | bytes 2162696 | tf_op jit(solution)/shard_map/ppermute | solution.py:552
  32.7 97.5 %collective-permute-start.18 = (bf16[44,64,128]{2,1,0:T(8,128)(2,1)}, bf16[44,64,128]{2,1,0:T(8,128)(2,1)}, u32[]{:S(2)}, u32[]{:S(2)}) collective-permute-start(bf16[44,64,128]{2,1,0:T(8,128)(2,1)} %get-tuple-element.179), channel_id=1, source_target_pairs={{0,1},{1,2},{2,3},{3,0},{4,5},{5,6},{6,7},{7,4},{8,9},{9,10},{10,1... | collective-permute-start | bytes 2162696 | tf_op jit(solution)/shard_map/ppermute | solution.py:552
  35.3 5.7 %collective-permute-start.3 = (bf16[48,10,128]{2,1,0:T(8,128)(2,1)S(1)}, bf16[48,10,128]{2,1,0:T(8,128)(2,1)S(1)}, u32[]{:S(2)}, u32[]{:S(2)}) collective-permute-start(bf16[48,10,128]{2,1,0:T(8,128)(2,1)S(1)} %fusion.11), channel_id=1, source_target_pairs={{0,96},{32,0},{64,32},{96,64},{1,97},{33,1},{65,33},{97,65},{2,98}... | collective-permute-start | bytes 368648 | tf_op jit(solution)/shard_map/ppermute | solution.py:42
  41.1 7.2 %collective-permute-start.4 = (bf16[48,10,128]{2,1,0:T(8,128)(2,1)S(1)}, bf16[48,10,128]{2,1,0:T(8,128)(2,1)S(1)}, u32[]{:S(2)}, u32[]{:S(2)}) collective-permute-start(bf16[48,10,128]{2,1,0:T(8,128)(2,1)S(1)} %fusion.11), channel_id=1, source_target_pairs={{0,64},{32,96},{64,0},{96,32},{1,65},{33,97},{65,1},{97,33},{2,66}... | collective-permute-start | bytes 368648 | tf_op jit(solution)/shard_map/ppermute | solution.py:42
  48.3 6.9 %collective-permute-start.5 = (bf16[48,10,128]{2,1,0:T(8,128)(2,1)S(1)}, bf16[48,10,128]{2,1,0:T(8,128)(2,1)S(1)}, u32[]{:S(2)}, u32[]{:S(2)}) collective-permute-start(bf16[48,10,128]{2,1,0:T(8,128)(2,1)S(1)} %fusion.11), channel_id=1, source_target_pairs={{0,32},{32,64},{64,96},{96,0},{1,33},{33,65},{65,97},{97,1},{2,34}... | collective-permute-start | bytes 368648 | tf_op jit(solution)/shard_map/ppermute | solution.py:42
  55.1 75.2 %collective-permute-start.19 = (bf16[44,64,128]{2,1,0:T(8,128)(2,1)}, bf16[44,64,128]{2,1,0:T(8,128)(2,1)}, u32[]{:S(2)}, u32[]{:S(2)}) collective-permute-start(bf16[44,64,128]{2,1,0:T(8,128)(2,1)} %get-tuple-element.180), channel_id=1, source_target_pairs={{0,2},{1,3},{2,0},{3,1},{4,6},{5,7},{6,4},{7,5},{8,10},{9,11},{10,... | collective-permute-start | bytes 2162696 | tf_op jit(solution)/shard_map/ppermute | solution.py:552
  77.9 4.7 %copy-start.1 = (bf16[44,64,128]{2,1,0:T(8,128)(2,1)}, bf16[44,64,128]{2,1,0:T(8,128)(2,1)S(1)}, u32[]{:S(2)}) copy-start(bf16[44,64,128]{2,1,0:T(8,128)(2,1)S(1)} %collective-permute-done.12.refs_1_) | copy-start | bytes 2162692
  77.9 52.5 %collective-permute-start.20 = (bf16[44,64,128]{2,1,0:T(8,128)(2,1)}, bf16[44,64,128]{2,1,0:T(8,128)(2,1)}, u32[]{:S(2)}, u32[]{:S(2)}) collective-permute-start(bf16[44,64,128]{2,1,0:T(8,128)(2,1)} %get-tuple-element.181), channel_id=1, source_target_pairs={{0,3},{1,0},{2,1},{3,2},{4,7},{5,4},{6,5},{7,6},{8,11},{9,8},{10,9... | collective-permute-start | bytes 2162696 | tf_op jit(solution)/shard_map/ppermute | solution.py:552
  77.9 4.6 %copy-start.2 = (bf16[44,64,128]{2,1,0:T(8,128)(2,1)}, bf16[44,64,128]{2,1,0:T(8,128)(2,1)S(1)}, u32[]{:S(2)}) copy-start(bf16[44,64,128]{2,1,0:T(8,128)(2,1)S(1)} %collective-permute-done.13.refs_2_) | copy-start | bytes 2162692
  77.9 8.7 %collective-permute-start.6 = (bf16[400,128]{1,0:T(8,128)(2,1)S(1)}, bf16[400,128]{1,0:T(8,128)(2,1)S(1)}, u32[]{:S(2)}, u32[]{:S(2)}) collective-permute-start(bf16[400,128]{1,0:T(8,128)(2,1)S(1)} %get-tuple-element.235), channel_id=1, source_target_pairs={{0,1},{1,2},{2,3},{3,0},{4,5},{5,6},{6,7},{7,4},{8,9},{9,10},{10,1... | collective-permute-start | bytes 307208 | tf_op jit(solution)/shard_map/ppermute | solution.py:32
  79.9 7.0 %collective-permute-start.7 = (bf16[400,128]{1,0:T(8,128)(2,1)S(1)}, bf16[400,128]{1,0:T(8,128)(2,1)}, u32[]{:S(2)}, u32[]{:S(2)}) collective-permute-start(bf16[400,128]{1,0:T(8,128)(2,1)S(1)} %get-tuple-element.234), channel_id=1, source_target_pairs={{0,2},{1,3},{2,0},{3,1},{4,6},{5,7},{6,4},{7,5},{8,10},{9,11},{10,... | collective-permute-start | bytes 307208 | tf_op jit(solution)/shard_map/ppermute | solution.py:32
  86.6 10.6 %copy-start.10 = (s32[4,4,128]{2,1,0:T(4,128)S(1)}, s32[4,4,128]{2,1,0:T(4,128)}, u32[]{:S(2)}) copy-start(s32[4,4,128]{2,1,0:T(4,128)} %get-tuple-element.244) | copy-start | bytes 24580
  86.6 13.2 %copy-start.8 = (bf16[400,128]{1,0:T(8,128)(2,1)}, bf16[400,128]{1,0:T(8,128)(2,1)S(1)}, u32[]{:S(2)}) copy-start(bf16[400,128]{1,0:T(8,128)(2,1)S(1)} %collective-permute-done.6.refs_1_) | copy-start | bytes 307204
  86.6 53.3 %collective-permute-start.15 = (bf16[40,64,128]{2,1,0:T(8,128)(2,1)}, bf16[40,64,128]{2,1,0:T(8,128)(2,1)}, u32[]{:S(2)}, u32[]{:S(2)}) collective-permute-start(bf16[40,64,128]{2,1,0:T(8,128)(2,1)} %get-tuple-element.175), channel_id=1, source_target_pairs={{0,32},{32,64},{64,96},{96,0},{1,33},{33,65},{65,97},{97,1},{2,34}... | collective-permute-start | bytes 1966088 | tf_op jit(solution)/shard_map/ppermute | solution.py:552
  86.9 12.9 %collective-permute-start.8 = (bf16[400,128]{1,0:T(8,128)(2,1)S(1)}, bf16[400,128]{1,0:T(8,128)(2,1)S(1)}, u32[]{:S(2)}, u32[]{:S(2)}) collective-permute-start(bf16[400,128]{1,0:T(8,128)(2,1)S(1)} %get-tuple-element.233), channel_id=1, source_target_pairs={{0,3},{1,0},{2,1},{3,2},{4,7},{5,4},{6,5},{7,6},{8,11},{9,8},{10,9... | collective-permute-start | bytes 307208 | tf_op jit(solution)/shard_map/ppermute | solution.py:32
  99.8 0.7 copy-start.9
  102.5 6.4 %collective-permute-start.10 = (bf16[400,128]{1,0:T(8,128)(2,1)}, bf16[400,128]{1,0:T(8,128)(2,1)S(1)}, u32[]{:S(2)}, u32[]{:S(2)}) collective-permute-start(bf16[400,128]{1,0:T(8,128)(2,1)} %mix.1.refs_1_), channel_id=1, source_target_pairs={{0,64},{32,96},{64,0},{96,32},{1,65},{33,97},{65,1},{97,33},{2,66}... | collective-permute-start | bytes 307208 | tf_op jit(solution)/shard_map/ppermute | solution.py:670
  108.9 18.4 %copy-start.5 = (bf16[400,128]{1,0:T(8,128)(2,1)}, bf16[400,128]{1,0:T(8,128)(2,1)S(1)}, u32[]{:S(2)}) copy-start(bf16[400,128]{1,0:T(8,128)(2,1)S(1)} %collective-permute-done.10.refs_3_) | copy-start | bytes 307204
  108.9 4.9 %collective-permute-start.11 = (bf16[400,128]{1,0:T(8,128)(2,1)}, bf16[400,128]{1,0:T(8,128)(2,1)S(1)}, u32[]{:S(2)}, u32[]{:S(2)}) collective-permute-start(bf16[400,128]{1,0:T(8,128)(2,1)} %mix.1.refs_1_), channel_id=1, source_target_pairs={{0,96},{32,0},{64,32},{96,64},{1,97},{33,1},{65,33},{97,65},{2,98}... | collective-permute-start | bytes 307208 | tf_op jit(solution)/shard_map/ppermute | solution.py:670
  113.8 13.6 %copy-start.6 = (bf16[400,128]{1,0:T(8,128)(2,1)}, bf16[400,128]{1,0:T(8,128)(2,1)S(1)}, u32[]{:S(2)}) copy-start(bf16[400,128]{1,0:T(8,128)(2,1)S(1)} %collective-permute-done.11.refs_4_) | copy-start | bytes 307204
  113.8 13.6 %collective-permute-start.9 = (bf16[400,128]{1,0:T(8,128)(2,1)}, bf16[400,128]{1,0:T(8,128)(2,1)S(1)}, u32[]{:S(2)}, u32[]{:S(2)}) collective-permute-start(bf16[400,128]{1,0:T(8,128)(2,1)} %mix.1.refs_1_), channel_id=1, source_target_pairs={{0,32},{32,64},{64,96},{96,0},{1,33},{33,65},{65,97},{97,1},{2,34}... | collective-permute-start | bytes 307208 | tf_op jit(solution)/shard_map/ppermute | solution.py:670
  127.4 0.7 copy-start.7
  130.3 10.2 %copy-start.4 = (bf16[48,1024]{1,0:T(8,128)(2,1)S(1)}, bf16[48,1024]{1,0:T(8,128)(2,1)}, u32[]{:S(2)}) copy-start(bf16[48,1024]{1,0:T(8,128)(2,1)} %final.1) | copy-start | bytes 294916
  130.3 25.9 %collective-permute-start.16 = (bf16[40,64,128]{2,1,0:T(8,128)(2,1)}, bf16[40,64,128]{2,1,0:T(8,128)(2,1)S(1)}, u32[]{:S(2)}, u32[]{:S(2)}) collective-permute-start(bf16[40,64,128]{2,1,0:T(8,128)(2,1)} %get-tuple-element.176), channel_id=1, source_target_pairs={{0,64},{32,96},{64,0},{96,32},{1,65},{33,97},{65,1},{97,33},{2,66}... | collective-permute-start | bytes 1966088 | tf_op jit(solution)/shard_map/ppermute | solution.py:552
  130.3 29.7 %collective-permute-start.17 = (bf16[40,64,128]{2,1,0:T(8,128)(2,1)}, bf16[40,64,128]{2,1,0:T(8,128)(2,1)}, u32[]{:S(2)}, u32[]{:S(2)}) collective-permute-start(bf16[40,64,128]{2,1,0:T(8,128)(2,1)} %get-tuple-element.177), channel_id=1, source_target_pairs={{0,96},{32,0},{64,32},{96,64},{1,97},{33,1},{65,33},{97,65},{2,98}... | collective-permute-start | bytes 1966088 | tf_op jit(solution)/shard_map/ppermute | solution.py:552
  134.4 27.8 %collective-permute-start.21 = (bf16[40,64,128]{2,1,0:T(8,128)(2,1)}, bf16[40,64,128]{2,1,0:T(8,128)(2,1)}, u32[]{:S(2)}, u32[]{:S(2)}) collective-permute-start(bf16[40,64,128]{2,1,0:T(8,128)(2,1)} %get-tuple-element.183), channel_id=1, source_target_pairs={{0,32},{32,64},{64,96},{96,0},{1,33},{33,65},{65,97},{97,1},{2,34}... | collective-permute-start | bytes 1966088 | tf_op jit(solution)/shard_map/ppermute | solution.py:552
  136.4 25.7 %collective-permute-start.22 = (bf16[40,64,128]{2,1,0:T(8,128)(2,1)}, bf16[40,64,128]{2,1,0:T(8,128)(2,1)}, u32[]{:S(2)}, u32[]{:S(2)}) collective-permute-start(bf16[40,64,128]{2,1,0:T(8,128)(2,1)} %get-tuple-element.184), channel_id=1, source_target_pairs={{0,64},{32,96},{64,0},{96,32},{1,65},{33,97},{65,1},{97,33},{2,66}... | collective-permute-start | bytes 1966088 | tf_op jit(solution)/shard_map/ppermute | solution.py:552
  139.9 34.2 %collective-permute-start.23 = (bf16[40,64,128]{2,1,0:T(8,128)(2,1)}, bf16[40,64,128]{2,1,0:T(8,128)(2,1)}, u32[]{:S(2)}, u32[]{:S(2)}) collective-permute-start(bf16[40,64,128]{2,1,0:T(8,128)(2,1)} %get-tuple-element.185), channel_id=1, source_target_pairs={{0,96},{32,0},{64,32},{96,64},{1,97},{33,1},{65,33},{97,65},{2,98}... | collective-permute-start | bytes 1966088 | tf_op jit(solution)/shard_map/ppermute | solution.py:552
  143.5 30.5 %copy-start.3 = (bf16[40,64,128]{2,1,0:T(8,128)(2,1)S(1)}, bf16[40,64,128]{2,1,0:T(8,128)(2,1)}, u32[]{:S(2)}) copy-start(bf16[40,64,128]{2,1,0:T(8,128)(2,1)} %get-tuple-element.174) | copy-start | bytes 1966084
  143.5 30.5 %copy-start.13 = (s32[4]{0:T(128)S(1)}, s32[4]{0:T(128)}, u32[]{:S(2)}) copy-start(s32[4]{0:T(128)} %copy-done.12) | copy-start | bytes 52
  144.2 11.1 %all-to-all-start.1 = ((bf16[8,48,256]{2,1,0:T(8,128)(2,1)}), bf16[8,48,256]{2,1,0:T(8,128)(2,1)S(1)}, u32[]{:S(2)}, u32[]{:S(2)}) async-start(bf16[8,48,256]{2,1,0:T(8,128)(2,1)} %bitcast.114), calls=%async_computation.1 | async-start | bytes 393216 | tf_op jit(solution)/shard_map/all_to_all | solution.py:678

commit v2 on v1

--- a/solution.py
+++ b/solution.py
@@ -64,7 +64,9 @@
     return tail.astype(jnp.bfloat16)
 
 
-def attend_kernel(seqs, table, q_ref, pool_ref, out_ref, grouped, gathered, lse_rows, acc):
+def attend_kernel(seqs, table, q_ref, pool_ref, *refs):
+    outs = refs[:seqs]
+    grouped, gathered, lse_rows, acc = refs[seqs:]
     page_len = pool_ref.shape[2]
     limit = pool_ref.shape[0]
     rows_each = q_ref.shape[1]
@@ -131,21 +133,22 @@
     lane = lax.broadcasted_iota(jnp.int32, (8, HEAD), 1) // rows_each
     each = requests // seqs
     per_row = HEAD // rows_each
-    for s in range(seqs):
+    for k_out, out_ref in enumerate(outs):
+        s = lax.rem(table[at_slot + requests] + k_out, seqs)
         tails = []
         for k in range(each // per_row):
             line = jnp.zeros((8, HEAD), jnp.float32)
             for i in range(per_row):
                 r = s * each + k * per_row + i
                 slot = table[at_slot + r]
-                out_ref[s, pl.ds((k * per_row + i) * rows_each, rows_each), :] = gathered[
+                out_ref[pl.ds((k * per_row + i) * rows_each, rows_each), :] = gathered[
                     pl.ds(pl.multiple_of(slot * rows_each, rows_each), rows_each), :
                 ].astype(jnp.bfloat16)
                 source = jnp.broadcast_to(lse_rows[pl.ds(slot // per_row, 1), :], (8, HEAD))
                 shift = lax.rem(i - lax.rem(slot, per_row) + per_row, per_row) * rows_each
                 line = jnp.where(lane == i, pltpu.roll(source, shift, 1), line)
             tails.append(line[0:1])
-        out_ref[s, pl.ds(each * rows_each, 16), :] = packed_tail(tails)
+        out_ref[pl.ds(each * rows_each, 16), :] = packed_tail(tails)
 
 
 TILE = 8
@@ -157,7 +160,7 @@
     own = requests // seqs * rows_each
     return pl.pallas_call(
         functools.partial(attend_kernel, seqs),
-        out_shape=jax.ShapeDtypeStruct((seqs, own + 16, HEAD), jnp.bfloat16),
+        out_shape=[jax.ShapeDtypeStruct((own + 16, HEAD), jnp.bfloat16)] * seqs,
         grid_spec=pltpu.PrefetchScalarGridSpec(
             num_scalar_prefetch=1,
             grid=(1,),
@@ -165,7 +168,7 @@
                 pl.BlockSpec((requests, rows_each, HEAD), lambda i, t: (0, 0, 0)),
                 pl.BlockSpec((limit,) + pool.shape[1:], lambda i, t: (0, 0, 0, 0)),
             ],
-            out_specs=pl.BlockSpec((seqs, own + 16, HEAD), lambda i, t: (0, 0, 0)),
+            out_specs=[pl.BlockSpec((own + 16, HEAD), lambda i, t: (0, 0))] * seqs,
             scratch_shapes=[
                 pltpu.VMEM((GROUPS * MEM * rows_each, HEAD), jnp.bfloat16),
                 pltpu.VMEM((GROUPS * MEM * rows_each, HEAD), jnp.float32),
@@ -322,7 +325,7 @@
     starts = jnp.sum(
         (group[None, :] < jnp.arange(8, dtype=jnp.int32)[:, None]).astype(jnp.int32), 1
     )
-    return jnp.concatenate(ordered + [starts, slot])
+    return jnp.concatenate(ordered + [starts, slot, lax.axis_index("seq").astype(jnp.int32)[None]])
 
 
 CAP_SEQ = 44
@@ -589,10 +592,11 @@
     step_count, request_count, width_here = hidden_in.shape
     ratio = HEADS // KV_HEADS
     heads_here = w_qkv.shape[1] // ((ratio + 2) * HEAD)
-    hidden_f = hidden_in.astype(jnp.float32)
     fits, first_table, second_table, third_table, coming = migration_tables(
         page_owner, migrate_dest, kv_pool.shape[0]
     )
+    first_table, hidden_in = lax.optimization_barrier((first_table, hidden_in))
+    hidden_f = hidden_in.astype(jnp.float32)
     seqs = lax.axis_size("seq")
     lists = split_pool(first_table, kv_pool, seqs)
     key_lists = passed(lists[:seqs], "seq")
@@ -606,6 +610,9 @@
         w_qkv,
         preferred_element_type=jnp.float32,
     ).astype(jnp.bfloat16)
+    partial_value, page_fill, group_of_request = lax.optimization_barrier(
+        (partial_value, page_fill, group_of_request)
+    )
     columns = partial_value.shape[1]
     extra = jnp.pad(jnp.stack(pieces(squares), -1), ((0, 0), (0, 0), (0, HEAD - 3)))
     partial_value = jnp.concatenate(
@@ -654,8 +661,7 @@
     seq_size = lax.axis_size("seq")
     own_rows = local_req * rows_here
     both = attend(table, rows_first, kv_pool, seq_size)
-    parts = [lax.dynamic_index_in_dim(both, lax.axis_index("seq"), 0, False)]
-    parts += exchanged(both, "seq")
+    parts = passed(both, "seq")
     query_own = lax.dynamic_slice_in_dim(rows_first, req_start, local_req, 0)
     key_own = lax.dynamic_slice_in_dim(keys_new, req_start, local_req, 1)
     value_own = lax.dynamic_slice_in_dim(values_new, req_start, local_req, 1)

time: 183 us -> 194 us (1.060)
  waiting for transfers between devices: 58.2 us -> 67.9 us
  starting transfers between devices: 44.8 us -> 50.6 us
    ppermute x12 -> x15, starting transfers between devices: 15.5 us -> 37.1 us  [passed(): lax.ppermute(part, axis, ring(axis, k))]
    ppermute x6 -> x3, starting transfers between devices: 20.1 us -> 5.82 us  [exchanged(): lax.ppermute(lax.dynamic_index_in_dim(parts, (here + step) % size, 0, Fal...]
    ppermute x12 -> x15, waiting for transfers between devices: 18 us -> 29.2 us  [passed(): lax.ppermute(part, axis, ring(axis, k))]
  transfers between devices with their start and end apart: 25 -> 25, of which waited for: 12 -> 12; matrix products, arithmetic and copies ran while one was open for 13% -> 12% of each run, Pallas kernels for 18% -> 17%
where the time goes in v2:
time: 194 us
  waiting for transfers between devices  67.9 us (35%)
  starting transfers between devices  50.6 us (26%)
  Pallas kernels  44.2 us (23%)
  local copies, waits for them, and re-layouts  12.1 us (6%)
  other arithmetic  9.33 us (5%)
  matrix products  6.7 us (3%)
  between operations  2.56 us (1%)
    ppermute x15, starting transfers between devices, passed(): lax.ppermute(part, axis, ring(axis, k))  37.1 us
    ppermute x15, waiting for transfers between devices, passed(): lax.ppermute(part, axis, ring(axis, k))  29.2 us
    ppermute x3, waiting for transfers between devices, block(): lax.ppermute(both, 'row', ring('row', k))  18.4 us
    pallas_call x1, Pallas kernels, attend(): pl.pallas_call(functools.partial(attend_kernel, seqs), out_shape=[jax.Sha...  18.1 us
    ppermute x3, waiting for transfers between devices, collected(): lax.ppermute(part, axis, ring(axis, size - step))  16.2 us
    pallas_call x2, Pallas kernels, resplit(): pl.pallas_call(functools.partial(resplit_kernel, count), out_shape=[jax.S...  8 us
    pallas_call x1, Pallas kernels, settle(): pl.pallas_call(functools.partial(settle_kernel, count), out_shape=jax.Sha...  6.26 us
    ppermute x3, starting transfers between devices, exchanged(): lax.ppermute(lax.dynamic_index_in_dim(parts, (here + step) % size, 0, Fal...  5.82 us
  transfers between devices with their start and end apart: 25, of which 12 were waited for; matrix products, arithmetic and copies ran while one was open for 12% of the time, Pallas kernels for 17%

profile of v2, /device:TPU:0, one launch (start us, length us, event | category | flops | bytes accessed | tf_op | source)
XLA Modules:
  0.0 193.5 jit_solution(15265792624420121439)
XLA Ops:
  0.6 0.7 broadcast_compare_fusion.1
  1.4 0.7 reshape.588
  2.5 0.7 select_reduce_fusion.2.table
  3.2 5.5 %split_pool.1 = (bf16[44,64,128]{2,1,0:T(8,128)(2,1)}, bf16[44,64,128]{2,1,0:T(8,128)(2,1)}, bf16[44,64,128]{2,1,0:T(8,128)(2,1)}, bf16[44,64,128]{2,1,0:T(8,128...) custom-call(s32[176]{0:T(256)} %select_reduce_fusion.2.table, ...), custom_call_target="tpu_custom_call" | custom-call | bytes 9961472 | tf_op jit(solution)/shard_map/split_pool/pallas_call | solution.py:421
  8.7 2.1 %collective-permute-start.12 = (bf16[44,64,128]{2,1,0:T(8,128)(2,1)}, bf16[44,64,128]{2,1,0:T(8,128)(2,1)S(1)}, u32[]{:S(2)}, u32[]{:S(2)}) collective-permute-start(bf16[44,64,128]{2,1,0:T(8,128)(2,1)} %get-tuple-element.189), channel_id=1, source_target_pairs={{0,1},{1,2},{2,3},{3,0},{4,5},{5,6},{6,7},{7,4},{8,9},{9,10},{10,1... | collective-permute-start | bytes 2162696 | tf_op jit(solution)/shard_map/ppermute | solution.py:555
  10.8 3.6 %collective-permute-start.13 = (bf16[44,64,128]{2,1,0:T(8,128)(2,1)}, bf16[44,64,128]{2,1,0:T(8,128)(2,1)S(1)}, u32[]{:S(2)}, u32[]{:S(2)}) collective-permute-start(bf16[44,64,128]{2,1,0:T(8,128)(2,1)} %get-tuple-element.190), channel_id=1, source_target_pairs={{0,2},{1,3},{2,0},{3,1},{4,6},{5,7},{6,4},{7,5},{8,10},{9,11},{10,... | collective-permute-start | bytes 2162696 | tf_op jit(solution)/shard_map/ppermute | solution.py:555
  14.4 0.7 dynamic-slice_convert_fusion
  15.6 3.7 %convolution_convert_fusion = bf16[192,1280]{1,0:T(8,128)(2,1)S(1)} fusion(bf16[192,2048]{1,0:T(8,128)(2,1)S(1)} %bitcast.118, bf16[2048,1280]{1,0:T(8,128)(2,1)} %param.14), kind=kOutput, calls=%fused_computation.22 | convolution fusion | flops 1006878720 | bytes 6520832 | tf_op jit(solution)/shard_map/dot_general | solution.py:608
  19.3 0.7 dynamic-slice_bitcast_fusion.2
  20.1 1.6 collective-permute-start
  21.6 2.9 %collective-permute-start.1 = (bf16[48,1408]{1,0:T(8,128)(2,1)S(1)}, bf16[48,1408]{1,0:T(8,128)(2,1)S(1)}, u32[]{:S(2)}, u32[]{:S(2)}) collective-permute-start(bf16[48,1408]{1,0:T(8,128)(2,1)S(1)} %get-tuple-element.244), channel_id=1, source_target_pairs={{0,64},{32,96},{64,0},{96,32},{1,65},{33,97},{65,1},{97,33},{2,66}... | collective-permute-start | bytes 405512 | tf_op jit(solution)/shard_map/ppermute | solution.py:32
  24.5 1.3 collective-permute-start.2
  26.1 0.5 convert_reduce_fusion.1
  26.8 0.8 dynamic_slice.63
  27.9 0.8 dynamic_slice.64
  29.1 0.7 concatenate.27.table
  29.8 1.0 collective-permute-start.14
  30.8 1.0 collective-permute-start.18
  31.8 1.0 fusion.13
  33.5 1.1 collective-permute-start.3
  34.7 4.5 %collective-permute-done.3 = bf16[48,10,128]{2,1,0:T(8,128)(2,1)S(1)} collective-permute-done((bf16[48,10,128]{2,1,0:T(8,128)(2,1)S(1)}, bf16[48,10,128]{2,1,0:T(8,128)(2,1)S(1)}, u32[]{:S(2)}, u32[]{:S(2)}) %collective-permute-start.3) | collective-permute-done | bytes 122912 | tf_op jit(solution)/shard_map/ppermute | solution.py:42
  39.2 1.6 collective-permute-start.4
  40.9 5.5 %collective-permute-done.4 = bf16[48,10,128]{2,1,0:T(8,128)(2,1)S(1)} collective-permute-done((bf16[48,10,128]{2,1,0:T(8,128)(2,1)S(1)}, bf16[48,10,128]{2,1,0:T(8,128)(2,1)S(1)}, u32[]{:S(2)}, u32[]{:S(2)}) %collective-permute-start.4) | collective-permute-done | bytes 122912 | tf_op jit(solution)/shard_map/ppermute | solution.py:42
  46.4 0.7 collective-permute-start.5
  47.1 6.2 %collective-permute-done.5 = bf16[48,10,128]{2,1,0:T(8,128)(2,1)S(1)} collective-permute-done((bf16[48,10,128]{2,1,0:T(8,128)(2,1)S(1)}, bf16[48,10,128]{2,1,0:T(8,128)(2,1)S(1)}, u32[]{:S(2)}, u32[]{:S(2)}) %collective-permute-start.5) | collective-permute-done | bytes 122912 | tf_op jit(solution)/shard_map/ppermute | solution.py:42
  53.7 0.9 copy.58
  54.6 18.1 %attend.1 = (bf16[400,128]{1,0:T(8,128)(2,1)}, bf16[400,128]{1,0:T(8,128)(2,1)}, bf16[400,128]{1,0:T(8,128)(2,1)}, bf16[400,128]{1,0:T(8,128)(2,1)}) custom-call(s32[441]{0:T(512)} %concatenate.27.table, bf16[48,32,128]{2,1,0:T(8,128)(2,1)} %bitcast.111, bf16[256,2,64,128]{3,2,1,0:T(8,128)(2,1)} %pool_ref.3), custom_call_target="tpu_custom_call" | custom-call | flops 2147483648 | bytes 4194304 | tf_op jit(solution)/shard_map/attend/pallas_call | solution.py:161
  72.7 0.7 select_reduce_fusion.1.table
  73.5 1.0 collective-permute-start.19
  74.5 2.6 %collective-permute-start.20 = (bf16[44,64,128]{2,1,0:T(8,128)(2,1)}, bf16[44,64,128]{2,1,0:T(8,128)(2,1)}, u32[]{:S(2)}, u32[]{:S(2)}) collective-permute-start(bf16[44,64,128]{2,1,0:T(8,128)(2,1)} %get-tuple-element.199), channel_id=1, source_target_pairs={{0,3},{1,0},{2,1},{3,2},{4,7},{5,4},{6,5},{7,6},{8,11},{9,8},{10,9... | collective-permute-start | bytes 2162696 | tf_op jit(solution)/shard_map/ppermute | solution.py:555
  77.1 2.5 %collective-permute-start.7 = (bf16[400,128]{1,0:T(8,128)(2,1)}, bf16[400,128]{1,0:T(8,128)(2,1)S(1)}, u32[]{:S(2)}, u32[]{:S(2)}) collective-permute-start(bf16[400,128]{1,0:T(8,128)(2,1)} %get-tuple-element.185), channel_id=1, source_target_pairs={{0,2},{1,3},{2,0},{3,1},{4,6},{5,7},{6,4},{7,5},{8,10},{9,11},{10,... | collective-permute-start | bytes 307208 | tf_op jit(solution)/shard_map/ppermute | solution.py:555
  79.6 4.1 %resplit.2 = (bf16[40,64,128]{2,1,0:T(8,128)(2,1)}, bf16[40,64,128]{2,1,0:T(8,128)(2,1)}, bf16[40,64,128]{2,1,0:T(8,128)(2,1)}, bf16[40,64,128]{2,1,0:T(8,128)(2,1)}) custom-call(s32[160]{0:T(256)} %select_reduce_fusion.1.table, bf16[44,64,128]{2,1,0:T(8,128)(2,1)} %get-tuple-element.188.refs_0_, bf16[44,64,128]{2,1,0:T(8,128)(2,1)} %copy-done.1, ...), custom_call_target="tpu_custom_call" | custom-call | bytes 5767168 | tf_op jit(solution)/shard_map/resplit/pallas_call | solution.py:472
  83.7 10.0 %collective-permute-done.6.refs_1_ = bf16[400,128]{1,0:T(8,128)(2,1)S(1)} collective-permute-done((bf16[400,128]{1,0:T(8,128)(2,1)}, bf16[400,128]{1,0:T(8,128)(2,1)S(1)}, u32[]{:S(2)}, u32[]{:S(2)}) %collective-permute-start.6) | collective-permute-done | bytes 102432 | tf_op jit(solution)/shard_map/ppermute | solution.py:555
  93.9 17.1 %collective-permute-start.8 = (bf16[400,128]{1,0:T(8,128)(2,1)S(1)}, bf16[400,128]{1,0:T(8,128)(2,1)S(1)}, u32[]{:S(2)}, u32[]{:S(2)}) collective-permute-start(bf16[400,128]{1,0:T(8,128)(2,1)S(1)} %copy-done.13), channel_id=1, source_target_pairs={{0,3},{1,0},{2,1},{3,2},{4,7},{5,4},{6,5},{7,6},{8,11},{9,8},{10,9... | collective-permute-start | bytes 307208 | tf_op jit(solution)/shard_map/ppermute | solution.py:555
  111.3 0.6 reduce_max.18
  112.0 1.2 collective-permute-done.8.refs_3_
  113.2 0.6 copy-done.10
  113.9 2.1 %mix.1.refs_1_ = bf16[400,128]{1,0:T(8,128)(2,1)} custom-call(bf16[400,128]{1,0:T(8,128)(2,1)} %get-tuple-element.183.refs_0_, bf16[400,128]{1,0:T(8,128)(2,1)} %copy-done.8, bf16[400,128]{1,0:T(8,128)(2,1)} %copy-done.9, bf16[400,128]{1,0:T(8,128)(2,1)} %copy-done.10), custom_call_target="tpu_custom_call" | custom-call | flops 409600 | bytes 512000 | tf_op jit(solution)/shard_map/mix/pallas_call | solution.py:269
  116.0 6.3 %collective-permute-done.10.refs_3_ = bf16[400,128]{1,0:T(8,128)(2,1)S(1)} collective-permute-done((bf16[400,128]{1,0:T(8,128)(2,1)}, bf16[400,128]{1,0:T(8,128)(2,1)S(1)}, u32[]{:S(2)}, u32[]{:S(2)}) %collective-permute-start.10) | collective-permute-done | bytes 102432 | tf_op jit(solution)/shard_map/ppermute | solution.py:676
  122.4 0.6 reshape.596.k_ref
  123.0 0.6 reshape.597.v_ref
  123.6 3.6 %collective-permute-done.11.refs_4_ = bf16[400,128]{1,0:T(8,128)(2,1)S(1)} collective-permute-done((bf16[400,128]{1,0:T(8,128)(2,1)}, bf16[400,128]{1,0:T(8,128)(2,1)S(1)}, u32[]{:S(2)}, u32[]{:S(2)}) %collective-permute-start.11) | collective-permute-done | bytes 102432 | tf_op jit(solution)/shard_map/ppermute | solution.py:676
  127.2 1.6 constant_dynamic-slice_fusion.3
  128.8 2.0 %fresh.1.refs_0_ = bf16[400,128]{1,0:T(8,128)(2,1)} custom-call(bf16[384,128]{1,0:T(8,128)(2,1)} %bitcast.120, bf16[48,128]{1,0:T(8,128)(2,1)} %reshape.596.k_ref, bf16[48,128]{1,0:T(8,128)(2,1)} %reshape.597.v_ref), custom_call_target="tpu_custom_call" | custom-call | flops 9437184 | bytes 196608 | tf_op jit(solution)/shard_map/fresh/pallas_call | solution.py:220
  130.8 8.5 %collective-permute-done.9.refs_2_ = bf16[400,128]{1,0:T(8,128)(2,1)S(1)} collective-permute-done((bf16[400,128]{1,0:T(8,128)(2,1)}, bf16[400,128]{1,0:T(8,128)(2,1)S(1)}, u32[]{:S(2)}, u32[]{:S(2)}) %collective-permute-start.9) | collective-permute-done | bytes 102432 | tf_op jit(solution)/shard_map/ppermute | solution.py:676
  139.3 0.7 copy-done.7
  139.9 2.3 %final.1 = bf16[48,1024]{1,0:T(8,128)(2,1)} custom-call(bf16[400,128]{1,0:T(8,128)(2,1)} %fresh.1.refs_0_, bf16[400,128]{1,0:T(8,128)(2,1)} %mix.1.refs_1_, bf16[400,128]{1,0:T(8,128)(2,1)} %copy-done.7, bf16[400,128]{1,0:T(8,128)(2,1)} %copy-done.5, bf16[400,128]{1,0:T(8,128)(2,1)} %copy-done.6), custom_call_target="tpu_custom_call" | custom-call | flops 512000 | bytes 512000 | tf_op jit(solution)/shard_map/final/pallas_call | solution.py:293
  142.3 4.0 %resplit.3 = (bf16[40,64,128]{2,1,0:T(8,128)(2,1)}, bf16[40,64,128]{2,1,0:T(8,128)(2,1)}, bf16[40,64,128]{2,1,0:T(8,128)(2,1)}, bf16[40,64,128]{2,1,0:T(8,128)(2,1)}) custom-call(s32[160]{0:T(256)} %select_reduce_fusion.1.table, bf16[44,64,128]{2,1,0:T(8,128)(2,1)} %get-tuple-element.196.refs_0_, bf16[44,64,128]{2,1,0:T(8,128)(2,1)} %collective-permute-done.18.refs_1_, ...), custom_call_target="tpu_custom_call" | custom-call | bytes 5767168 | tf_op jit(solution)/shard_map/resplit/pallas_call | solution.py:472
  146.3 2.1 %collective-permute-start.21 = (bf16[40,64,128]{2,1,0:T(8,128)(2,1)}, bf16[40,64,128]{2,1,0:T(8,128)(2,1)}, u32[]{:S(2)}, u32[]{:S(2)}) collective-permute-start(bf16[40,64,128]{2,1,0:T(8,128)(2,1)} %get-tuple-element.201), channel_id=1, source_target_pairs={{0,32},{32,64},{64,96},{96,0},{1,33},{33,65},{65,97},{97,1},{2,34}... | collective-permute-start | bytes 1966088 | tf_op jit(solution)/shard_map/ppermute | solution.py:555
  148.3 3.5 %collective-permute-start.22 = (bf16[40,64,128]{2,1,0:T(8,128)(2,1)}, bf16[40,64,128]{2,1,0:T(8,128)(2,1)}, u32[]{:S(2)}, u32[]{:S(2)}) collective-permute-start(bf16[40,64,128]{2,1,0:T(8,128)(2,1)} %get-tuple-element.202), channel_id=1, source_target_pairs={{0,64},{32,96},{64,0},{96,32},{1,65},{33,97},{65,1},{97,33},{2,66}... | collective-permute-start | bytes 1966088 | tf_op jit(solution)/shard_map/ppermute | solution.py:555
  151.8 0.6 collective-permute-start.23
  152.4 3.0 %convolution_convert_fusion.1 = bf16[48,2048]{1,0:T(8,128)(2,1)S(1)} fusion(bf16[48,1024]{1,0:T(8,128)(2,1)S(1)} %copy-done.4, bf16[1024,2048]{1,0:T(8,128)(2,1)} %param.15), kind=kOutput, calls=%fused_computation.23 | convolution fusion | flops 201424896 | bytes 4489216 | tf_op jit(solution)/shard_map/dot_general | solution.py:679
  155.5 0.7 copy.59
  156.1 4.3 %all-to-all-start.1 = ((bf16[8,48,256]{2,1,0:T(8,128)(2,1)}), bf16[8,48,256]{2,1,0:T(8,128)(2,1)S(1)}, u32[]{:S(2)}, u32[]{:S(2)}) async-start(bf16[8,48,256]{2,1,0:T(8,128)(2,1)} %bitcast.109), calls=%async_computation.1 | async-start | bytes 393216 | tf_op jit(solution)/shard_map/all_to_all | solution.py:684
  160.6 0.6 reduce_max.19
  162.5 0.6 copy.48
  163.2 4.1 %all-to-all-done.1 = bf16[8,48,256]{2,1,0:T(8,128)(2,1)S(1)} async-done(((bf16[8,48,256]{2,1,0:T(8,128)(2,1)}), bf16[8,48,256]{2,1,0:T(8,128)(2,1)S(1)}, u32[]{:S(2)}, u32[]{:S(2)}) %all-to-all-start.1) | async-done | bytes 196640 | tf_op jit(solution)/shard_map/all_to_all | solution.py:684
  167.4 0.6 copy.47
  168.0 3.8 %collective-permute-done.17 = bf16[40,64,128]{2,1,0:T(8,128)(2,1)} collective-permute-done((bf16[40,64,128]{2,1,0:T(8,128)(2,1)}, bf16[40,64,128]{2,1,0:T(8,128)(2,1)}, u32[]{:S(2)}, u32[]{:S(2)}) %collective-permute-start.17) | collective-permute-done | bytes 655392 | tf_op jit(solution)/shard_map/ppermute | solution.py:555
  171.9 2.4 %collective-permute-done.21 = bf16[40,64,128]{2,1,0:T(8,128)(2,1)} collective-permute-done((bf16[40,64,128]{2,1,0:T(8,128)(2,1)}, bf16[40,64,128]{2,1,0:T(8,128)(2,1)}, u32[]{:S(2)}, u32[]{:S(2)}) %collective-permute-start.21) | collective-permute-done | bytes 655392 | tf_op jit(solution)/shard_map/ppermute | solution.py:555
  174.3 11.7 %collective-permute-done.23 = bf16[40,64,128]{2,1,0:T(8,128)(2,1)} collective-permute-done((bf16[40,64,128]{2,1,0:T(8,128)(2,1)}, bf16[40,64,128]{2,1,0:T(8,128)(2,1)}, u32[]{:S(2)}, u32[]{:S(2)}) %collective-permute-start.23) | collective-permute-done | bytes 655392 | tf_op jit(solution)/shard_map/ppermute | solution.py:555
  186.0 7.4 %conditional.1 = (bf16[256,2,64,128]{3,2,1,0:T(8,128)(2,1)}) conditional(s32[]{:T(128)} %convert_element_type.145, (s32[4,4]{1,0:T(4,128)S(1)}, s32[]{:T(128)}, s32[4096]{0:T(1024)}, bf16[256,2,64,128]{3,2,1,0:T(8,128)(2,1)}) %tuple.53, (s32[4,4]{1,0:T(4,128)S(1)}, s32[4,4,16]{2,1,0:T(4,128)S(1)}, s32[]{:T(128)}, s32[]{:T(128)}, s32[]{:T(128)}, ...), branch_computations={%region_21.23_spmd, %region_23.25_spmd} | conditional | flops 4198404 | bytes 58736920 | solution.py:694
  186.4 0.7 select_n.283.table
  187.1 6.3 %settle.1 = bf16[256,2,64,128]{3,2,1,0:T(8,128)(2,1)} custom-call(s32[256]{0:T(256)} %select_n.283.table, bf16[40,64,128]{2,1,0:T(8,128)(2,1)S(1)} %get-tuple-element.139.refs_0_, bf16[40,64,128]{2,1,0:T(8,128)(2,1)} %get-tuple-element.140.refs_1_, bf16[40,64,128]{2,1,0:T(8,128)(2,1)S(1)} %get-tuple-element.141.refs_2_, ...), custom_call_target="tpu_custom_call" | custom-call | bytes 16777216 | tf_op jit(solution)/shard_map/cond/branch_1_fun/settle/pallas_call | solution.py:531
  (121 shorter events, 4.8 us)
Async XLA Ops:
  1.4 7.3 %copy-start.11 = (pred[4,4,256]{2,1,0:T(4,128)(4,1)}, pred[4,4,256]{2,1,0:T(4,128)(4,1)S(1)}, u32[]{:S(2)}) copy-start(pred[4,4,256]{2,1,0:T(4,128)(4,1)S(1)} %reshape.587) | copy-start | bytes 12292
  3.2 11.9 %copy-start = (bf16[4,48,2048]{2,1,0:T(8,128)(2,1)S(1)}, bf16[4,48,2048]{2,1,0:T(8,128)(2,1)}, u32[]{:S(2)}) copy-start(bf16[4,48,2048]{2,1,0:T(8,128)(2,1)} %param.12) | copy-start | bytes 2359300
  8.7 64.7 %collective-permute-start.12 = (bf16[44,64,128]{2,1,0:T(8,128)(2,1)}, bf16[44,64,128]{2,1,0:T(8,128)(2,1)S(1)}, u32[]{:S(2)}, u32[]{:S(2)}) collective-permute-start(bf16[44,64,128]{2,1,0:T(8,128)(2,1)} %get-tuple-element.189), channel_id=1, source_target_pairs={{0,1},{1,2},{2,3},{3,0},{4,5},{5,6},{6,7},{7,4},{8,9},{9,10},{10,1... | collective-permute-start | bytes 2162696 | tf_op jit(solution)/shard_map/ppermute | solution.py:555
  10.8 63.7 %collective-permute-start.13 = (bf16[44,64,128]{2,1,0:T(8,128)(2,1)}, bf16[44,64,128]{2,1,0:T(8,128)(2,1)S(1)}, u32[]{:S(2)}, u32[]{:S(2)}) collective-permute-start(bf16[44,64,128]{2,1,0:T(8,128)(2,1)} %get-tuple-element.190), channel_id=1, source_target_pairs={{0,2},{1,3},{2,0},{3,1},{4,6},{5,7},{6,4},{7,5},{8,10},{9,11},{10,... | collective-permute-start | bytes 2162696 | tf_op jit(solution)/shard_map/ppermute | solution.py:555
  19.2 7.3 %copy-start.14 = (s32[48]{0:T(128)S(1)}, s32[48]{0:T(128)}, u32[]{:S(2)}) copy-start(s32[48]{0:T(128)} %param.19) | copy-start | bytes 580
  19.3 7.4 %copy-start.15 = (s32[48]{0:T(128)S(1)}, s32[48]{0:T(128)}, u32[]{:S(2)}) copy-start(s32[48]{0:T(128)} %param.20) | copy-start | bytes 580
  20.1 9.7 %collective-permute-start = (bf16[48,1408]{1,0:T(8,128)(2,1)}, bf16[48,1408]{1,0:T(8,128)(2,1)S(1)}, u32[]{:S(2)}, u32[]{:S(2)}) collective-permute-start(bf16[48,1408]{1,0:T(8,128)(2,1)} %get-tuple-element.242), channel_id=1, source_target_pairs={{0,32},{32,64},{64,96},{96,0},{1,33},{33,65},{65,97},{97,1},{2,34}... | collective-permute-start | bytes 405512 | tf_op jit(solution)/shard_map/ppermute | solution.py:32
  21.6 9.2 %collective-permute-start.1 = (bf16[48,1408]{1,0:T(8,128)(2,1)S(1)}, bf16[48,1408]{1,0:T(8,128)(2,1)S(1)}, u32[]{:S(2)}, u32[]{:S(2)}) collective-permute-start(bf16[48,1408]{1,0:T(8,128)(2,1)S(1)} %get-tuple-element.244), channel_id=1, source_target_pairs={{0,64},{32,96},{64,0},{96,32},{1,65},{33,97},{65,1},{97,33},{2,66}... | collective-permute-start | bytes 405512 | tf_op jit(solution)/shard_map/ppermute | solution.py:32
  24.5 7.3 %collective-permute-start.2 = (bf16[48,1408]{1,0:T(8,128)(2,1)S(1)}, bf16[48,1408]{1,0:T(8,128)(2,1)}, u32[]{:S(2)}, u32[]{:S(2)}) collective-permute-start(bf16[48,1408]{1,0:T(8,128)(2,1)S(1)} %get-tuple-element.243), channel_id=1, source_target_pairs={{0,96},{32,0},{64,32},{96,64},{1,97},{33,1},{65,33},{97,65},{2,98}... | collective-permute-start | bytes 405512 | tf_op jit(solution)/shard_map/ppermute | solution.py:32
  25.9 0.7 copy-start.16
  29.8 47.4 %collective-permute-start.14 = (bf16[44,64,128]{2,1,0:T(8,128)(2,1)}, bf16[44,64,128]{2,1,0:T(8,128)(2,1)}, u32[]{:S(2)}, u32[]{:S(2)}) collective-permute-start(bf16[44,64,128]{2,1,0:T(8,128)(2,1)} %get-tuple-element.191), channel_id=1, source_target_pairs={{0,3},{1,0},{2,1},{3,2},{4,7},{5,4},{6,5},{7,6},{8,11},{9,8},{10,9... | collective-permute-start | bytes 2162696 | tf_op jit(solution)/shard_map/ppermute | solution.py:555
  30.8 111.4 %collective-permute-start.18 = (bf16[44,64,128]{2,1,0:T(8,128)(2,1)}, bf16[44,64,128]{2,1,0:T(8,128)(2,1)}, u32[]{:S(2)}, u32[]{:S(2)}) collective-permute-start(bf16[44,64,128]{2,1,0:T(8,128)(2,1)} %get-tuple-element.197), channel_id=1, source_target_pairs={{0,1},{1,2},{2,3},{3,0},{4,5},{5,6},{6,7},{7,4},{8,9},{9,10},{10,1... | collective-permute-start | bytes 2162696 | tf_op jit(solution)/shard_map/ppermute | solution.py:555
  33.5 5.7 %collective-permute-start.3 = (bf16[48,10,128]{2,1,0:T(8,128)(2,1)S(1)}, bf16[48,10,128]{2,1,0:T(8,128)(2,1)S(1)}, u32[]{:S(2)}, u32[]{:S(2)}) collective-permute-start(bf16[48,10,128]{2,1,0:T(8,128)(2,1)S(1)} %fusion.11), channel_id=1, source_target_pairs={{0,96},{32,0},{64,32},{96,64},{1,97},{33,1},{65,33},{97,65},{2,98}... | collective-permute-start | bytes 368648 | tf_op jit(solution)/shard_map/ppermute | solution.py:42
  39.2 7.2 %collective-permute-start.4 = (bf16[48,10,128]{2,1,0:T(8,128)(2,1)S(1)}, bf16[48,10,128]{2,1,0:T(8,128)(2,1)S(1)}, u32[]{:S(2)}, u32[]{:S(2)}) collective-permute-start(bf16[48,10,128]{2,1,0:T(8,128)(2,1)S(1)} %fusion.11), channel_id=1, source_target_pairs={{0,64},{32,96},{64,0},{96,32},{1,65},{33,97},{65,1},{97,33},{2,66}... | collective-permute-start | bytes 368648 | tf_op jit(solution)/shard_map/ppermute | solution.py:42
  46.4 6.9 %collective-permute-start.5 = (bf16[48,10,128]{2,1,0:T(8,128)(2,1)S(1)}, bf16[48,10,128]{2,1,0:T(8,128)(2,1)S(1)}, u32[]{:S(2)}, u32[]{:S(2)}) collective-permute-start(bf16[48,10,128]{2,1,0:T(8,128)(2,1)S(1)} %fusion.11), channel_id=1, source_target_pairs={{0,32},{32,64},{64,96},{96,0},{1,33},{33,65},{65,97},{97,1},{2,34}... | collective-permute-start | bytes 368648 | tf_op jit(solution)/shard_map/ppermute | solution.py:42
  72.7 20.9 %copy-start.12 = (pred[4,4,256]{2,1,0:T(4,128)(4,1)S(1)}, pred[4,4,256]{2,1,0:T(4,128)(4,1)}, u32[]{:S(2)}) copy-start(pred[4,4,256]{2,1,0:T(4,128)(4,1)} %copy-done.11) | copy-start | bytes 12292
  72.7 20.9 %collective-permute-start.6 = (bf16[400,128]{1,0:T(8,128)(2,1)}, bf16[400,128]{1,0:T(8,128)(2,1)S(1)}, u32[]{:S(2)}, u32[]{:S(2)}) collective-permute-start(bf16[400,128]{1,0:T(8,128)(2,1)} %get-tuple-element.184), channel_id=1, source_target_pairs={{0,1},{1,2},{2,3},{3,0},{4,5},{5,6},{6,7},{7,4},{8,9},{9,10},{10,1... | collective-permute-start | bytes 307208 | tf_op jit(solution)/shard_map/ppermute | solution.py:555
  73.5 6.2 %copy-start.1 = (bf16[44,64,128]{2,1,0:T(8,128)(2,1)}, bf16[44,64,128]{2,1,0:T(8,128)(2,1)S(1)}, u32[]{:S(2)}) copy-start(bf16[44,64,128]{2,1,0:T(8,128)(2,1)S(1)} %collective-permute-done.12.refs_1_) | copy-start | bytes 2162692
  73.5 68.8 %collective-permute-start.19 = (bf16[44,64,128]{2,1,0:T(8,128)(2,1)}, bf16[44,64,128]{2,1,0:T(8,128)(2,1)}, u32[]{:S(2)}, u32[]{:S(2)}) collective-permute-start(bf16[44,64,128]{2,1,0:T(8,128)(2,1)} %get-tuple-element.198), channel_id=1, source_target_pairs={{0,2},{1,3},{2,0},{3,1},{4,6},{5,7},{6,4},{7,5},{8,10},{9,11},{10,... | collective-permute-start | bytes 2162696 | tf_op jit(solution)/shard_map/ppermute | solution.py:555
  74.5 5.1 %copy-start.2 = (bf16[44,64,128]{2,1,0:T(8,128)(2,1)}, bf16[44,64,128]{2,1,0:T(8,128)(2,1)S(1)}, u32[]{:S(2)}) copy-start(bf16[44,64,128]{2,1,0:T(8,128)(2,1)S(1)} %collective-permute-done.13.refs_2_) | copy-start | bytes 2162692
  74.5 67.8 %collective-permute-start.20 = (bf16[44,64,128]{2,1,0:T(8,128)(2,1)}, bf16[44,64,128]{2,1,0:T(8,128)(2,1)}, u32[]{:S(2)}, u32[]{:S(2)}) collective-permute-start(bf16[44,64,128]{2,1,0:T(8,128)(2,1)} %get-tuple-element.199), channel_id=1, source_target_pairs={{0,3},{1,0},{2,1},{3,2},{4,7},{5,4},{6,5},{7,6},{8,11},{9,8},{10,9... | collective-permute-start | bytes 2162696 | tf_op jit(solution)/shard_map/ppermute | solution.py:555
  77.1 16.8 %collective-permute-start.7 = (bf16[400,128]{1,0:T(8,128)(2,1)}, bf16[400,128]{1,0:T(8,128)(2,1)S(1)}, u32[]{:S(2)}, u32[]{:S(2)}) collective-permute-start(bf16[400,128]{1,0:T(8,128)(2,1)} %get-tuple-element.185), channel_id=1, source_target_pairs={{0,2},{1,3},{2,0},{3,1},{4,6},{5,7},{6,4},{7,5},{8,10},{9,11},{10,... | collective-permute-start | bytes 307208 | tf_op jit(solution)/shard_map/ppermute | solution.py:555
  83.7 10.2 %copy-start.13 = (bf16[400,128]{1,0:T(8,128)(2,1)S(1)}, bf16[400,128]{1,0:T(8,128)(2,1)}, u32[]{:S(2)}) copy-start(bf16[400,128]{1,0:T(8,128)(2,1)} %get-tuple-element.186) | copy-start | bytes 307204
  93.7 19.6 %copy-start.8 = (bf16[400,128]{1,0:T(8,128)(2,1)}, bf16[400,128]{1,0:T(8,128)(2,1)S(1)}, u32[]{:S(2)}) copy-start(bf16[400,128]{1,0:T(8,128)(2,1)S(1)} %collective-permute-done.6.refs_1_) | copy-start | bytes 307204
  93.7 58.1 %collective-permute-start.15 = (bf16[40,64,128]{2,1,0:T(8,128)(2,1)}, bf16[40,64,128]{2,1,0:T(8,128)(2,1)}, u32[]{:S(2)}, u32[]{:S(2)}) collective-permute-start(bf16[40,64,128]{2,1,0:T(8,128)(2,1)} %get-tuple-element.193), channel_id=1, source_target_pairs={{0,32},{32,64},{64,96},{96,0},{1,33},{33,65},{65,97},{97,1},{2,34}... | collective-permute-start | bytes 1966088 | tf_op jit(solution)/shard_map/ppermute | solution.py:555
  93.9 19.3 %copy-start.9 = (bf16[400,128]{1,0:T(8,128)(2,1)}, bf16[400,128]{1,0:T(8,128)(2,1)S(1)}, u32[]{:S(2)}) copy-start(bf16[400,128]{1,0:T(8,128)(2,1)S(1)} %collective-permute-done.7.refs_2_) | copy-start | bytes 307204
  93.9 19.3 %collective-permute-start.8 = (bf16[400,128]{1,0:T(8,128)(2,1)S(1)}, bf16[400,128]{1,0:T(8,128)(2,1)S(1)}, u32[]{:S(2)}, u32[]{:S(2)}) collective-permute-start(bf16[400,128]{1,0:T(8,128)(2,1)S(1)} %copy-done.13), channel_id=1, source_target_pairs={{0,3},{1,0},{2,1},{3,2},{4,7},{5,4},{6,5},{7,6},{8,11},{9,8},{10,9... | collective-permute-start | bytes 307208 | tf_op jit(solution)/shard_map/ppermute | solution.py:555
  113.2 0.7 copy-start.10
  116.0 6.4 %collective-permute-start.10 = (bf16[400,128]{1,0:T(8,128)(2,1)}, bf16[400,128]{1,0:T(8,128)(2,1)S(1)}, u32[]{:S(2)}, u32[]{:S(2)}) collective-permute-start(bf16[400,128]{1,0:T(8,128)(2,1)} %mix.1.refs_1_), channel_id=1, source_target_pairs={{0,64},{32,96},{64,0},{96,32},{1,65},{33,97},{65,1},{97,33},{2,66}... | collective-permute-start | bytes 307208 | tf_op jit(solution)/shard_map/ppermute | solution.py:676
  122.4 16.9 %copy-start.5 = (bf16[400,128]{1,0:T(8,128)(2,1)}, bf16[400,128]{1,0:T(8,128)(2,1)S(1)}, u32[]{:S(2)}) copy-start(bf16[400,128]{1,0:T(8,128)(2,1)S(1)} %collective-permute-done.10.refs_3_) | copy-start | bytes 307204
  122.4 4.9 %collective-permute-start.11 = (bf16[400,128]{1,0:T(8,128)(2,1)}, bf16[400,128]{1,0:T(8,128)(2,1)S(1)}, u32[]{:S(2)}, u32[]{:S(2)}) collective-permute-start(bf16[400,128]{1,0:T(8,128)(2,1)} %mix.1.refs_1_), channel_id=1, source_target_pairs={{0,96},{32,0},{64,32},{96,64},{1,97},{33,1},{65,33},{97,65},{2,98}... | collective-permute-start | bytes 307208 | tf_op jit(solution)/shard_map/ppermute | solution.py:676
  127.2 12.0 %copy-start.6 = (bf16[400,128]{1,0:T(8,128)(2,1)}, bf16[400,128]{1,0:T(8,128)(2,1)S(1)}, u32[]{:S(2)}) copy-start(bf16[400,128]{1,0:T(8,128)(2,1)S(1)} %collective-permute-done.11.refs_4_) | copy-start | bytes 307204
  127.2 12.0 %collective-permute-start.9 = (bf16[400,128]{1,0:T(8,128)(2,1)}, bf16[400,128]{1,0:T(8,128)(2,1)S(1)}, u32[]{:S(2)}, u32[]{:S(2)}) collective-permute-start(bf16[400,128]{1,0:T(8,128)(2,1)} %mix.1.refs_1_), channel_id=1, source_target_pairs={{0,32},{32,64},{64,96},{96,0},{1,33},{33,65},{65,97},{97,1},{2,34}... | collective-permute-start | bytes 307208 | tf_op jit(solution)/shard_map/ppermute | solution.py:676
  139.3 0.7 copy-start.7
  142.2 10.2 %copy-start.4 = (bf16[48,1024]{1,0:T(8,128)(2,1)S(1)}, bf16[48,1024]{1,0:T(8,128)(2,1)}, u32[]{:S(2)}) copy-start(bf16[48,1024]{1,0:T(8,128)(2,1)} %final.1) | copy-start | bytes 294916
  142.2 25.9 %collective-permute-start.16 = (bf16[40,64,128]{2,1,0:T(8,128)(2,1)}, bf16[40,64,128]{2,1,0:T(8,128)(2,1)S(1)}, u32[]{:S(2)}, u32[]{:S(2)}) collective-permute-start(bf16[40,64,128]{2,1,0:T(8,128)(2,1)} %get-tuple-element.194), channel_id=1, source_target_pairs={{0,64},{32,96},{64,0},{96,32},{1,65},{33,97},{65,1},{97,33},{2,66}... | collective-permute-start | bytes 1966088 | tf_op jit(solution)/shard_map/ppermute | solution.py:555
  142.2 29.7 %collective-permute-start.17 = (bf16[40,64,128]{2,1,0:T(8,128)(2,1)}, bf16[40,64,128]{2,1,0:T(8,128)(2,1)}, u32[]{:S(2)}, u32[]{:S(2)}) collective-permute-start(bf16[40,64,128]{2,1,0:T(8,128)(2,1)} %get-tuple-element.195), channel_id=1, source_target_pairs={{0,96},{32,0},{64,32},{96,64},{1,97},{33,1},{65,33},{97,65},{2,98}... | collective-permute-start | bytes 1966088 | tf_op jit(solution)/shard_map/ppermute | solution.py:555
  146.3 28.0 %collective-permute-start.21 = (bf16[40,64,128]{2,1,0:T(8,128)(2,1)}, bf16[40,64,128]{2,1,0:T(8,128)(2,1)}, u32[]{:S(2)}, u32[]{:S(2)}) collective-permute-start(bf16[40,64,128]{2,1,0:T(8,128)(2,1)} %get-tuple-element.201), channel_id=1, source_target_pairs={{0,32},{32,64},{64,96},{96,0},{1,33},{33,65},{65,97},{97,1},{2,34}... | collective-permute-start | bytes 1966088 | tf_op jit(solution)/shard_map/ppermute | solution.py:555
  148.3 26.0 %collective-permute-start.22 = (bf16[40,64,128]{2,1,0:T(8,128)(2,1)}, bf16[40,64,128]{2,1,0:T(8,128)(2,1)}, u32[]{:S(2)}, u32[]{:S(2)}) collective-permute-start(bf16[40,64,128]{2,1,0:T(8,128)(2,1)} %get-tuple-element.202), channel_id=1, source_target_pairs={{0,64},{32,96},{64,0},{96,32},{1,65},{33,97},{65,1},{97,33},{2,66}... | collective-permute-start | bytes 1966088 | tf_op jit(solution)/shard_map/ppermute | solution.py:555
  151.8 34.2 %collective-permute-start.23 = (bf16[40,64,128]{2,1,0:T(8,128)(2,1)}, bf16[40,64,128]{2,1,0:T(8,128)(2,1)}, u32[]{:S(2)}, u32[]{:S(2)}) collective-permute-start(bf16[40,64,128]{2,1,0:T(8,128)(2,1)} %get-tuple-element.203), channel_id=1, source_target_pairs={{0,96},{32,0},{64,32},{96,64},{1,97},{33,1},{65,33},{97,65},{2,98}... | collective-permute-start | bytes 1966088 | tf_op jit(solution)/shard_map/ppermute | solution.py:555
  155.4 30.6 %copy-start.3 = (bf16[40,64,128]{2,1,0:T(8,128)(2,1)S(1)}, bf16[40,64,128]{2,1,0:T(8,128)(2,1)}, u32[]{:S(2)}) copy-start(bf16[40,64,128]{2,1,0:T(8,128)(2,1)} %get-tuple-element.192) | copy-start | bytes 1966084
  155.5 30.6 %copy-start.17 = (s32[4]{0:T(128)S(1)}, s32[4]{0:T(128)}, u32[]{:S(2)}) copy-start(s32[4]{0:T(128)} %copy-done.16) | copy-start | bytes 52
  156.1 11.1 %all-to-all-start.1 = ((bf16[8,48,256]{2,1,0:T(8,128)(2,1)}), bf16[8,48,256]{2,1,0:T(8,128)(2,1)S(1)}, u32[]{:S(2)}, u32[]{:S(2)}) async-start(bf16[8,48,256]{2,1,0:T(8,128)(2,1)} %bitcast.109), calls=%async_computation.1 | async-start | bytes 393216 | tf_op jit(solution)/shard_map/all_to_all | solution.py:684

commit v3 on v2

--- a/solution.py
+++ b/solution.py
@@ -592,9 +592,7 @@
     step_count, request_count, width_here = hidden_in.shape
     ratio = HEADS // KV_HEADS
     heads_here = w_qkv.shape[1] // ((ratio + 2) * HEAD)
-    fits, first_table, second_table, third_table, coming = migration_tables(
-        page_owner, migrate_dest, kv_pool.shape[0]
-    )
+    first_table = migration_tables(page_owner, migrate_dest, kv_pool.shape[0])[1]
     first_table, hidden_in = lax.optimization_barrier((first_table, hidden_in))
     hidden_f = hidden_in.astype(jnp.float32)
     seqs = lax.axis_size("seq")
@@ -610,9 +608,6 @@
         w_qkv,
         preferred_element_type=jnp.float32,
     ).astype(jnp.bfloat16)
-    partial_value, page_fill, group_of_request = lax.optimization_barrier(
-        (partial_value, page_fill, group_of_request)
-    )
     columns = partial_value.shape[1]
     extra = jnp.pad(jnp.stack(pieces(squares), -1), ((0, 0), (0, 0), (0, HEAD - 3)))
     partial_value = jnp.concatenate(
@@ -633,6 +628,12 @@
     rotated = rotate(projected, cosine[:, None], sine[:, None])
     is_value = jnp.arange(heads_here * (ratio + 2)) % (ratio + 2) == ratio + 1
     ready = jnp.where(is_value[None, :, None], projected, rotated).astype(jnp.bfloat16)
+    ready, page_owner, migrate_dest, page_fill, group_of_request = lax.optimization_barrier(
+        (ready, page_owner, migrate_dest, page_fill, group_of_request)
+    )
+    fits, _, second_table, third_table, coming = migration_tables(
+        page_owner, migrate_dest, kv_pool.shape[0]
+    )
     ready = collected(ready, "row")
     ready = ready.reshape(step_count, request_count, heads_here, ratio + 2, HEAD)
     key_lists = resplit(second_table, key_lists)

time: 194 us -> 196 us (1.010)
  the two profiles are of different devices: /device:TPU:0 before, /device:TPU:80 now
where the time goes in v3:
time: 196 us; the launch traced here: 192 us
  starting transfers between devices  57.9 us (30%)
  waiting for transfers between devices  50.8 us (26%)
  Pallas kernels  44.3 us (23%)
  local copies, waits for them, and re-layouts  18.6 us (9%)
  other arithmetic  11 us (6%)
  matrix products  6.7 us (3%)
  between operations  2.66 us (1%)
    ppermute x15, starting transfers between devices, passed(): lax.ppermute(part, axis, ring(axis, k))  38.9 us
    ppermute x15, waiting for transfers between devices, passed(): lax.ppermute(part, axis, ring(axis, k))  32.2 us
    pallas_call x1, Pallas kernels, attend(): pl.pallas_call(functools.partial(attend_kernel, seqs), out_shape=[jax.Sha...  17.4 us
    pallas_call x2, Pallas kernels, resplit(): pl.pallas_call(functools.partial(resplit_kernel, count), out_shape=[jax.S...  8.85 us
    ppermute x3, waiting for transfers between devices, collected(): lax.ppermute(part, axis, ring(axis, size - step))  8.28 us
    unnamed x46, local copies, waits for them, and re-layouts  7.74 us
    ppermute x3, waiting for transfers between devices, block(): lax.ppermute(both, 'row', ring('row', k))  6.38 us
    pallas_call x1, Pallas kernels, settle(): pl.pallas_call(functools.partial(settle_kernel, count), out_shape=jax.Sha...  6.26 us
  transfers between devices with their start and end apart: 25, of which 11 were waited for; matrix products, arithmetic and copies ran while one was open for 13% of the time, Pallas kernels for 20%

profile of v3, /device:TPU:80, one launch (start us, length us, event | category | flops | bytes accessed | tf_op | source)
XLA Modules:
  0.0 192.0 jit_solution(13811079062860199732)
XLA Ops:
  0.7 0.7 broadcast_compare_fusion.2
  1.4 0.7 reshape.556
  2.4 0.7 select_reduce_fusion.2.table
  3.1 0.7 dynamic-slice_convert_fusion
  3.8 1.4 multiply_convert_fusion
  5.4 3.7 %convolution_convert_fusion = bf16[192,1280]{1,0:T(8,128)(2,1)S(1)} fusion(bf16[192,2048]{1,0:T(8,128)(2,1)S(1)} %bitcast.115, bf16[2048,1280]{1,0:T(8,128)(2,1)} %param.14), kind=kOutput, calls=%fused_computation.22 | convolution fusion | flops 1006878720 | bytes 6520832 | tf_op jit(solution)/shard_map/dot_general | solution.py:606
  9.1 0.7 dynamic-slice_bitcast_fusion.2
  10.3 2.9 %collective-permute-start.1 = (bf16[48,1408]{1,0:T(8,128)(2,1)S(1)}, bf16[48,1408]{1,0:T(8,128)(2,1)S(1)}, u32[]{:S(2)}, u32[]{:S(2)}) collective-permute-start(bf16[48,1408]{1,0:T(8,128)(2,1)S(1)} %get-tuple-element.246), channel_id=1, source_target_pairs={{0,64},{32,96},{64,0},{96,32},{1,65},{33,97},{65,1},{97,33},{2,66}... | collective-permute-start | bytes 405512 | tf_op jit(solution)/shard_map/ppermute | solution.py:32
  13.2 5.5 %split_pool.1 = (bf16[44,64,128]{2,1,0:T(8,128)(2,1)}, bf16[44,64,128]{2,1,0:T(8,128)(2,1)}, bf16[44,64,128]{2,1,0:T(8,128)(2,1)}, bf16[44,64,128]{2,1,0:T(8,128...) custom-call(s32[176]{0:T(256)} %select_reduce_fusion.2.table, ...), custom_call_target="tpu_custom_call" | custom-call | bytes 9961472 | tf_op jit(solution)/shard_map/split_pool/pallas_call | solution.py:421
  18.7 1.7 collective-permute-start.12
  20.9 1.6 collective-permute-start.14
  22.5 1.0 collective-permute-start.18
  23.5 1.0 fusion.12
  25.2 0.7 bitcast_dynamic-update-slice_fusion.5
  25.9 1.9 collective-permute-start.3
  28.5 0.8 dynamic_slice.65
  30.2 0.7 concatenate.11.table
  30.9 0.7 collective-permute-done.3
  31.5 1.5 collective-permute-start.4
  33.0 0.7 bitcast_dynamic-update-slice_fusion.3
  33.7 5.1 %collective-permute-done.4 = bf16[48,10,128]{2,1,0:T(8,128)(2,1)S(1)} collective-permute-done((bf16[48,10,128]{2,1,0:T(8,128)(2,1)S(1)}, bf16[48,10,128]{2,1,0:T(8,128)(2,1)S(1)}, u32[]{:S(2)}, u32[]{:S(2)}) %collective-permute-start.4) | collective-permute-done | bytes 122912 | tf_op jit(solution)/shard_map/ppermute | solution.py:42
  38.8 2.8 %collective-permute-start.5 = (bf16[48,10,128]{2,1,0:T(8,128)(2,1)S(1)}, bf16[48,10,128]{2,1,0:T(8,128)(2,1)S(1)}, u32[]{:S(2)}, u32[]{:S(2)}) collective-permute-start(bf16[48,10,128]{2,1,0:T(8,128)(2,1)S(1)} %fusion.10), channel_id=1, source_target_pairs={{0,32},{32,64},{64,96},{96,0},{1,33},{33,65},{65,97},{97,1},{2,34}... | collective-permute-start | bytes 368648 | tf_op jit(solution)/shard_map/ppermute | solution.py:42
  41.6 0.7 bitcast_dynamic-update-slice_fusion.1
  42.3 2.5 %collective-permute-done.5 = bf16[48,10,128]{2,1,0:T(8,128)(2,1)S(1)} collective-permute-done((bf16[48,10,128]{2,1,0:T(8,128)(2,1)S(1)}, bf16[48,10,128]{2,1,0:T(8,128)(2,1)S(1)}, u32[]{:S(2)}, u32[]{:S(2)}) %collective-permute-start.5) | collective-permute-done | bytes 122912 | tf_op jit(solution)/shard_map/ppermute | solution.py:42
  44.8 0.7 bitcast_dynamic-update-slice_fusion
  45.5 0.7 bitcast_dynamic-update-slice_fusion.6
  46.2 0.7 bitcast_dynamic-update-slice_fusion.4
  46.9 0.7 bitcast_dynamic-update-slice_fusion.2
  47.5 1.3 constant_dynamic-slice_fusion.4
  49.0 0.8 copy.57
  49.8 17.4 %attend.1 = (bf16[400,128]{1,0:T(8,128)(2,1)}, bf16[400,128]{1,0:T(8,128)(2,1)}, bf16[400,128]{1,0:T(8,128)(2,1)}, bf16[400,128]{1,0:T(8,128)(2,1)}) custom-call(s32[441]{0:T(512)} %concatenate.11.table, bf16[48,32,128]{2,1,0:T(8,128)(2,1)} %bitcast.110, bf16[256,2,64,128]{3,2,1,0:T(8,128)(2,1)} %pool_ref.3), custom_call_target="tpu_custom_call" | custom-call | flops 2147483648 | bytes 4194304 | tf_op jit(solution)/shard_map/attend/pallas_call | solution.py:161
  67.2 3.1 %collective-permute-start.6 = (bf16[400,128]{1,0:T(8,128)(2,1)}, bf16[400,128]{1,0:T(8,128)(2,1)S(1)}, u32[]{:S(2)}, u32[]{:S(2)}) collective-permute-start(bf16[400,128]{1,0:T(8,128)(2,1)} %get-tuple-element.187), channel_id=1, source_target_pairs={{0,1},{1,2},{2,3},{3,0},{4,5},{5,6},{6,7},{7,4},{8,9},{9,10},{10,1... | collective-permute-start | bytes 307208 | tf_op jit(solution)/shard_map/ppermute | solution.py:555
  71.0 1.5 collective-permute-start.20
  72.5 2.1 %collective-permute-start.7 = (bf16[400,128]{1,0:T(8,128)(2,1)}, bf16[400,128]{1,0:T(8,128)(2,1)}, u32[]{:S(2)}, u32[]{:S(2)}) collective-permute-start(bf16[400,128]{1,0:T(8,128)(2,1)} %get-tuple-element.188), channel_id=1, source_target_pairs={{0,2},{1,3},{2,0},{3,1},{4,6},{5,7},{6,4},{7,5},{8,10},{9,11},{10,... | collective-permute-start | bytes 307208 | tf_op jit(solution)/shard_map/ppermute | solution.py:555
  74.6 4.9 %resplit.2 = (bf16[40,64,128]{2,1,0:T(8,128)(2,1)S(1)}, bf16[40,64,128]{2,1,0:T(8,128)(2,1)}, bf16[40,64,128]{2,1,0:T(8,128)(2,1)}, bf16[40,64,128]{2,1,0:T(8,128)(2,1)}) custom-call(s32[160]{0:T(256)} %select_reduce_fusion.1.table, bf16[44,64,128]{2,1,0:T(8,128)(2,1)} %get-tuple-element.192.refs_0_, bf16[44,64,128]{2,1,0:T(8,128)(2,1)} %collective-permute-done.12.refs_1_, ...), custom_call_target="tpu_custom_call" | custom-call | bytes 5767168 | tf_op jit(solution)/shard_map/resplit/pallas_call | solution.py:472
  79.5 10.2 %collective-permute-done.6.refs_1_ = bf16[400,128]{1,0:T(8,128)(2,1)S(1)} collective-permute-done((bf16[400,128]{1,0:T(8,128)(2,1)}, bf16[400,128]{1,0:T(8,128)(2,1)S(1)}, u32[]{:S(2)}, u32[]{:S(2)}) %collective-permute-start.6) | collective-permute-done | bytes 102432 | tf_op jit(solution)/shard_map/ppermute | solution.py:555
  89.7 0.7 fusion.22
  91.0 13.2 %collective-permute-start.8 = (bf16[400,128]{1,0:T(8,128)(2,1)}, bf16[400,128]{1,0:T(8,128)(2,1)}, u32[]{:S(2)}, u32[]{:S(2)}) collective-permute-start(bf16[400,128]{1,0:T(8,128)(2,1)} %get-tuple-element.189), channel_id=1, source_target_pairs={{0,3},{1,0},{2,1},{3,2},{4,7},{5,4},{6,5},{7,6},{8,11},{9,8},{10,9... | collective-permute-start | bytes 307208 | tf_op jit(solution)/shard_map/ppermute | solution.py:555
  104.6 0.7 reduce_max.18
  105.3 3.7 %collective-permute-done.8.refs_3_ = bf16[400,128]{1,0:T(8,128)(2,1)} collective-permute-done((bf16[400,128]{1,0:T(8,128)(2,1)}, bf16[400,128]{1,0:T(8,128)(2,1)}, u32[]{:S(2)}, u32[]{:S(2)}) %collective-permute-start.8) | collective-permute-done | bytes 102432 | tf_op jit(solution)/shard_map/ppermute | solution.py:555
  109.0 2.1 %mix.1.refs_1_ = bf16[400,128]{1,0:T(8,128)(2,1)} custom-call(bf16[400,128]{1,0:T(8,128)(2,1)} %get-tuple-element.186.refs_0_, bf16[400,128]{1,0:T(8,128)(2,1)} %copy-done.9, bf16[400,128]{1,0:T(8,128)(2,1)} %collective-permute-done.7.refs_2_, bf16[400,128]{1,0:T(8,128)(2,1)} %collective-permute-done.8.refs_3_), custom_call_target="tpu_custom_call" | custom-call | flops 409600 | bytes 512000 | tf_op jit(solution)/shard_map/mix/pallas_call | solution.py:269
  111.1 0.7 slice_bitcast_fusion.1
  111.8 4.2 %collective-permute-done.9.refs_2_ = bf16[400,128]{1,0:T(8,128)(2,1)S(1)} collective-permute-done((bf16[400,128]{1,0:T(8,128)(2,1)}, bf16[400,128]{1,0:T(8,128)(2,1)S(1)}, u32[]{:S(2)}, u32[]{:S(2)}) %collective-permute-start.9) | collective-permute-done | bytes 102432 | tf_op jit(solution)/shard_map/ppermute | solution.py:677
  116.0 4.4 %collective-permute-start.10 = (bf16[400,128]{1,0:T(8,128)(2,1)}, bf16[400,128]{1,0:T(8,128)(2,1)S(1)}, u32[]{:S(2)}, u32[]{:S(2)}) collective-permute-start(bf16[400,128]{1,0:T(8,128)(2,1)} %mix.1.refs_1_), channel_id=1, source_target_pairs={{0,64},{32,96},{64,0},{96,32},{1,65},{33,97},{65,1},{97,33},{2,66}... | collective-permute-start | bytes 307208 | tf_op jit(solution)/shard_map/ppermute | solution.py:677
  121.6 1.6 collective-permute-done.10.refs_3_
  123.2 0.9 collective-permute-start.11
  124.0 1.5 constant_dynamic-slice_fusion.3
  125.6 2.0 %fresh.1.refs_0_ = bf16[400,128]{1,0:T(8,128)(2,1)} custom-call(bf16[384,128]{1,0:T(8,128)(2,1)} %bitcast.117, bf16[48,128]{1,0:T(8,128)(2,1)} %reshape.564.k_ref, bf16[48,128]{1,0:T(8,128)(2,1)} %reshape.565.v_ref), custom_call_target="tpu_custom_call" | custom-call | flops 9437184 | bytes 196608 | tf_op jit(solution)/shard_map/fresh/pallas_call | solution.py:220
  128.8 2.3 %final.1 = bf16[48,1024]{1,0:T(8,128)(2,1)} custom-call(bf16[400,128]{1,0:T(8,128)(2,1)} %fresh.1.refs_0_, bf16[400,128]{1,0:T(8,128)(2,1)} %mix.1.refs_1_, bf16[400,128]{1,0:T(8,128)(2,1)} %copy-done.6, bf16[400,128]{1,0:T(8,128)(2,1)} %copy-done.7, bf16[400,128]{1,0:T(8,128)(2,1)} %copy-done.8), custom_call_target="tpu_custom_call" | custom-call | flops 512000 | bytes 512000 | tf_op jit(solution)/shard_map/final/pallas_call | solution.py:293
  131.0 8.1 %collective-permute-start.16 = (bf16[40,64,128]{2,1,0:T(8,128)(2,1)}, bf16[40,64,128]{2,1,0:T(8,128)(2,1)}, u32[]{:S(2)}, u32[]{:S(2)}) collective-permute-start(bf16[40,64,128]{2,1,0:T(8,128)(2,1)} %get-tuple-element.198), channel_id=1, source_target_pairs={{0,64},{32,96},{64,0},{96,32},{1,65},{33,97},{65,1},{97,33},{2,66}... | collective-permute-start | bytes 1966088 | tf_op jit(solution)/shard_map/ppermute | solution.py:555
  139.2 3.1 %collective-permute-start.17 = (bf16[40,64,128]{2,1,0:T(8,128)(2,1)}, bf16[40,64,128]{2,1,0:T(8,128)(2,1)}, u32[]{:S(2)}, u32[]{:S(2)}) collective-permute-start(bf16[40,64,128]{2,1,0:T(8,128)(2,1)} %get-tuple-element.199), channel_id=1, source_target_pairs={{0,96},{32,0},{64,32},{96,64},{1,97},{33,1},{65,33},{97,65},{2,98}... | collective-permute-start | bytes 1966088 | tf_op jit(solution)/shard_map/ppermute | solution.py:555
  142.3 0.9 copy-done.1
  143.2 4.0 %resplit.3 = (bf16[40,64,128]{2,1,0:T(8,128)(2,1)}, bf16[40,64,128]{2,1,0:T(8,128)(2,1)}, bf16[40,64,128]{2,1,0:T(8,128)(2,1)}, bf16[40,64,128]{2,1,0:T(8,128)(2,1)}) custom-call(s32[160]{0:T(256)} %select_reduce_fusion.1.table, bf16[44,64,128]{2,1,0:T(8,128)(2,1)} %get-tuple-element.200.refs_0_, bf16[44,64,128]{2,1,0:T(8,128)(2,1)} %collective-permute-done.18.refs_1_, ...), custom_call_target="tpu_custom_call" | custom-call | bytes 5767168 | tf_op jit(solution)/shard_map/resplit/pallas_call | solution.py:472
  147.2 1.5 collective-permute-start.22
  148.7 1.9 collective-permute-start.23
  150.6 3.0 %convolution_convert_fusion.1 = bf16[48,2048]{1,0:T(8,128)(2,1)S(1)} fusion(bf16[48,1024]{1,0:T(8,128)(2,1)S(1)} %copy-done.3, bf16[1024,2048]{1,0:T(8,128)(2,1)} %param.15), kind=kOutput, calls=%fused_computation.23 | convolution fusion | flops 201424896 | bytes 4489216 | tf_op jit(solution)/shard_map/dot_general | solution.py:680
  153.7 0.7 copy.58
  154.4 4.3 %all-to-all-start.1 = ((bf16[8,48,256]{2,1,0:T(8,128)(2,1)}), bf16[8,48,256]{2,1,0:T(8,128)(2,1)S(1)}, u32[]{:S(2)}, u32[]{:S(2)}) async-start(bf16[8,48,256]{2,1,0:T(8,128)(2,1)} %bitcast.108), calls=%async_computation.1 | async-start | bytes 393216 | tf_op jit(solution)/shard_map/all_to_all | solution.py:685
  161.5 4.0 %all-to-all-done.1 = bf16[8,48,256]{2,1,0:T(8,128)(2,1)S(1)} async-done(((bf16[8,48,256]{2,1,0:T(8,128)(2,1)}), bf16[8,48,256]{2,1,0:T(8,128)(2,1)S(1)}, u32[]{:S(2)}, u32[]{:S(2)}) %all-to-all-start.1) | async-done | bytes 196640 | tf_op jit(solution)/shard_map/all_to_all | solution.py:685
  166.2 4.1 %collective-permute-done.17 = bf16[40,64,128]{2,1,0:T(8,128)(2,1)} collective-permute-done((bf16[40,64,128]{2,1,0:T(8,128)(2,1)}, bf16[40,64,128]{2,1,0:T(8,128)(2,1)}, u32[]{:S(2)}, u32[]{:S(2)}) %collective-permute-start.17) | collective-permute-done | bytes 655392 | tf_op jit(solution)/shard_map/ppermute | solution.py:555
  170.4 14.1 %collective-permute-done.23 = bf16[40,64,128]{2,1,0:T(8,128)(2,1)} collective-permute-done((bf16[40,64,128]{2,1,0:T(8,128)(2,1)}, bf16[40,64,128]{2,1,0:T(8,128)(2,1)}, u32[]{:S(2)}, u32[]{:S(2)}) %collective-permute-start.23) | collective-permute-done | bytes 655392 | tf_op jit(solution)/shard_map/ppermute | solution.py:555
  184.5 7.4 %conditional.1 = (bf16[256,2,64,128]{3,2,1,0:T(8,128)(2,1)}) conditional(s32[]{:T(128)} %convert_element_type.132, (s32[4,4]{1,0:T(4,128)S(1)}, s32[]{:T(128)}, s32[4096]{0:T(1024)}, bf16[256,2,64,128]{3,2,1,0:T(8,128)(2,1)}) %tuple.53, (s32[4,4]{1,0:T(4,128)S(1)}, s32[4,4,16]{2,1,0:T(4,128)S(1)}, s32[]{:T(128)}, s32[]{:T(128)}, s32[]{:T(128)}, ...), branch_computations={%region_21.23_spmd, %region_23.25_spmd} | conditional | flops 4198404 | bytes 58736920 | solution.py:695
  184.9 0.7 select_n.278.table
  185.6 6.3 %settle.1 = bf16[256,2,64,128]{3,2,1,0:T(8,128)(2,1)} custom-call(s32[256]{0:T(256)} %select_n.278.table, bf16[40,64,128]{2,1,0:T(8,128)(2,1)S(1)} %get-tuple-element.139.refs_0_, bf16[40,64,128]{2,1,0:T(8,128)(2,1)} %get-tuple-element.140.refs_1_, bf16[40,64,128]{2,1,0:T(8,128)(2,1)} %get-tuple-element.141.refs_2_, ...), custom_call_target="tpu_custom_call" | custom-call | bytes 16777216 | tf_op jit(solution)/shard_map/cond/branch_1_fun/settle/pallas_call | solution.py:531
  (125 shorter events, 10.5 us)
Async XLA Ops:
  9.8 11.1 %collective-permute-start.2 = (bf16[48,1408]{1,0:T(8,128)(2,1)}, bf16[48,1408]{1,0:T(8,128)(2,1)S(1)}, u32[]{:S(2)}, u32[]{:S(2)}) collective-permute-start(bf16[48,1408]{1,0:T(8,128)(2,1)} %get-tuple-element.245), channel_id=1, source_target_pairs={{0,96},{32,0},{64,32},{96,64},{1,97},{33,1},{65,33},{97,65},{2,98}... | collective-permute-start | bytes 405512 | tf_op jit(solution)/shard_map/ppermute | solution.py:32
  10.3 12.2 %collective-permute-start.1 = (bf16[48,1408]{1,0:T(8,128)(2,1)S(1)}, bf16[48,1408]{1,0:T(8,128)(2,1)S(1)}, u32[]{:S(2)}, u32[]{:S(2)}) collective-permute-start(bf16[48,1408]{1,0:T(8,128)(2,1)S(1)} %get-tuple-element.246), channel_id=1, source_target_pairs={{0,64},{32,96},{64,0},{96,32},{1,65},{33,97},{65,1},{97,33},{2,66}... | collective-permute-start | bytes 405512 | tf_op jit(solution)/shard_map/ppermute | solution.py:32
  13.2 7.2 %copy-start.14 = (s32[48]{0:T(128)S(1)}, s32[48]{0:T(128)}, u32[]{:S(2)}) copy-start(s32[48]{0:T(128)} %param.19) | copy-start | bytes 580
  13.2 7.5 %copy-start = (bf16[4,48,2048]{2,1,0:T(8,128)(2,1)S(1)}, bf16[4,48,2048]{2,1,0:T(8,128)(2,1)}, u32[]{:S(2)}) copy-start(bf16[4,48,2048]{2,1,0:T(8,128)(2,1)} %param.12) | copy-start | bytes 2359300
  13.2 10.3 %collective-permute-start = (bf16[48,1408]{1,0:T(8,128)(2,1)S(1)}, bf16[48,1408]{1,0:T(8,128)(2,1)}, u32[]{:S(2)}, u32[]{:S(2)}) collective-permute-start(bf16[48,1408]{1,0:T(8,128)(2,1)S(1)} %get-tuple-element.244), channel_id=1, source_target_pairs={{0,32},{32,64},{64,96},{96,0},{1,33},{33,65},{65,97},{97,1},{2,34}... | collective-permute-start | bytes 405512 | tf_op jit(solution)/shard_map/ppermute | solution.py:32
  18.7 52.4 %collective-permute-start.12 = (bf16[44,64,128]{2,1,0:T(8,128)(2,1)}, bf16[44,64,128]{2,1,0:T(8,128)(2,1)}, u32[]{:S(2)}, u32[]{:S(2)}) collective-permute-start(bf16[44,64,128]{2,1,0:T(8,128)(2,1)} %get-tuple-element.193), channel_id=1, source_target_pairs={{0,1},{1,2},{2,3},{3,0},{4,5},{5,6},{6,7},{7,4},{8,9},{9,10},{10,1... | collective-permute-start | bytes 2162696 | tf_op jit(solution)/shard_map/ppermute | solution.py:555
  20.4 50.7 %collective-permute-start.13 = (bf16[44,64,128]{2,1,0:T(8,128)(2,1)}, bf16[44,64,128]{2,1,0:T(8,128)(2,1)}, u32[]{:S(2)}, u32[]{:S(2)}) collective-permute-start(bf16[44,64,128]{2,1,0:T(8,128)(2,1)} %get-tuple-element.194), channel_id=1, source_target_pairs={{0,2},{1,3},{2,0},{3,1},{4,6},{5,7},{6,4},{7,5},{8,10},{9,11},{10,... | collective-permute-start | bytes 2162696 | tf_op jit(solution)/shard_map/ppermute | solution.py:555
  20.4 0.5 copy-start.16
  20.9 51.6 %collective-permute-start.14 = (bf16[44,64,128]{2,1,0:T(8,128)(2,1)}, bf16[44,64,128]{2,1,0:T(8,128)(2,1)}, u32[]{:S(2)}, u32[]{:S(2)}) collective-permute-start(bf16[44,64,128]{2,1,0:T(8,128)(2,1)} %get-tuple-element.195), channel_id=1, source_target_pairs={{0,3},{1,0},{2,1},{3,2},{4,7},{5,4},{6,5},{7,6},{8,11},{9,8},{10,9... | collective-permute-start | bytes 2162696 | tf_op jit(solution)/shard_map/ppermute | solution.py:555
  22.5 116.6 %collective-permute-start.18 = (bf16[44,64,128]{2,1,0:T(8,128)(2,1)}, bf16[44,64,128]{2,1,0:T(8,128)(2,1)}, u32[]{:S(2)}, u32[]{:S(2)}) collective-permute-start(bf16[44,64,128]{2,1,0:T(8,128)(2,1)} %get-tuple-element.201), channel_id=1, source_target_pairs={{0,1},{1,2},{2,3},{3,0},{4,5},{5,6},{6,7},{7,4},{8,9},{9,10},{10,1... | collective-permute-start | bytes 2162696 | tf_op jit(solution)/shard_map/ppermute | solution.py:555
  24.8 3.0 %copy-start.15 = (s32[48]{0:T(128)S(1)}, s32[48]{0:T(128)}, u32[]{:S(2)}) copy-start(s32[48]{0:T(128)} %param.20) | copy-start | bytes 580
  24.8 3.2 %copy-start.10 = (s32[4096]{0:T(1024)S(1)}, s32[4096]{0:T(1024)}, u32[]{:S(2)}) copy-start(s32[4096]{0:T(1024)} %param.17) | copy-start | bytes 49156
  24.8 4.5 %copy-start.11 = (s32[4096]{0:T(1024)S(1)}, s32[4096]{0:T(1024)}, u32[]{:S(2)}) copy-start(s32[4096]{0:T(1024)} %param.21) | copy-start | bytes 49156
  25.9 5.7 %collective-permute-start.3 = (bf16[48,10,128]{2,1,0:T(8,128)(2,1)S(1)}, bf16[48,10,128]{2,1,0:T(8,128)(2,1)S(1)}, u32[]{:S(2)}, u32[]{:S(2)}) collective-permute-start(bf16[48,10,128]{2,1,0:T(8,128)(2,1)S(1)} %fusion.10), channel_id=1, source_target_pairs={{0,96},{32,0},{64,32},{96,64},{1,97},{33,1},{65,33},{97,65},{2,98}... | collective-permute-start | bytes 368648 | tf_op jit(solution)/shard_map/ppermute | solution.py:42
  29.3 1.6 copy-start.13
  31.5 7.3 %collective-permute-start.4 = (bf16[48,10,128]{2,1,0:T(8,128)(2,1)S(1)}, bf16[48,10,128]{2,1,0:T(8,128)(2,1)S(1)}, u32[]{:S(2)}, u32[]{:S(2)}) collective-permute-start(bf16[48,10,128]{2,1,0:T(8,128)(2,1)S(1)} %fusion.10), channel_id=1, source_target_pairs={{0,64},{32,96},{64,0},{96,32},{1,65},{33,97},{65,1},{97,33},{2,66}... | collective-permute-start | bytes 368648 | tf_op jit(solution)/shard_map/ppermute | solution.py:42
  38.8 6.0 %collective-permute-start.5 = (bf16[48,10,128]{2,1,0:T(8,128)(2,1)S(1)}, bf16[48,10,128]{2,1,0:T(8,128)(2,1)S(1)}, u32[]{:S(2)}, u32[]{:S(2)}) collective-permute-start(bf16[48,10,128]{2,1,0:T(8,128)(2,1)S(1)} %fusion.10), channel_id=1, source_target_pairs={{0,32},{32,64},{64,96},{96,0},{1,33},{33,65},{65,97},{97,1},{2,34}... | collective-permute-start | bytes 368648 | tf_op jit(solution)/shard_map/ppermute | solution.py:42
  67.2 22.5 %collective-permute-start.6 = (bf16[400,128]{1,0:T(8,128)(2,1)}, bf16[400,128]{1,0:T(8,128)(2,1)S(1)}, u32[]{:S(2)}, u32[]{:S(2)}) collective-permute-start(bf16[400,128]{1,0:T(8,128)(2,1)} %get-tuple-element.187), channel_id=1, source_target_pairs={{0,1},{1,2},{2,3},{3,0},{4,5},{5,6},{6,7},{7,4},{8,9},{9,10},{10,1... | collective-permute-start | bytes 307208 | tf_op jit(solution)/shard_map/ppermute | solution.py:555
  71.0 71.3 %collective-permute-start.19 = (bf16[44,64,128]{2,1,0:T(8,128)(2,1)}, bf16[44,64,128]{2,1,0:T(8,128)(2,1)S(1)}, u32[]{:S(2)}, u32[]{:S(2)}) collective-permute-start(bf16[44,64,128]{2,1,0:T(8,128)(2,1)} %get-tuple-element.202), channel_id=1, source_target_pairs={{0,2},{1,3},{2,0},{3,1},{4,6},{5,7},{6,4},{7,5},{8,10},{9,11},{10,... | collective-permute-start | bytes 2162696 | tf_op jit(solution)/shard_map/ppermute | solution.py:555
  71.0 71.3 %collective-permute-start.20 = (bf16[44,64,128]{2,1,0:T(8,128)(2,1)}, bf16[44,64,128]{2,1,0:T(8,128)(2,1)}, u32[]{:S(2)}, u32[]{:S(2)}) collective-permute-start(bf16[44,64,128]{2,1,0:T(8,128)(2,1)} %get-tuple-element.203), channel_id=1, source_target_pairs={{0,3},{1,0},{2,1},{3,2},{4,7},{5,4},{6,5},{7,6},{8,11},{9,8},{10,9... | collective-permute-start | bytes 2162696 | tf_op jit(solution)/shard_map/ppermute | solution.py:555
  72.5 18.5 %collective-permute-start.7 = (bf16[400,128]{1,0:T(8,128)(2,1)}, bf16[400,128]{1,0:T(8,128)(2,1)}, u32[]{:S(2)}, u32[]{:S(2)}) collective-permute-start(bf16[400,128]{1,0:T(8,128)(2,1)} %get-tuple-element.188), channel_id=1, source_target_pairs={{0,2},{1,3},{2,0},{3,1},{4,6},{5,7},{6,4},{7,5},{8,10},{9,11},{10,... | collective-permute-start | bytes 307208 | tf_op jit(solution)/shard_map/ppermute | solution.py:555
  89.7 19.3 %copy-start.9 = (bf16[400,128]{1,0:T(8,128)(2,1)}, bf16[400,128]{1,0:T(8,128)(2,1)S(1)}, u32[]{:S(2)}) copy-start(bf16[400,128]{1,0:T(8,128)(2,1)S(1)} %collective-permute-done.6.refs_1_) | copy-start | bytes 307204
  89.7 59.0 %collective-permute-start.15 = (bf16[40,64,128]{2,1,0:T(8,128)(2,1)}, bf16[40,64,128]{2,1,0:T(8,128)(2,1)}, u32[]{:S(2)}, u32[]{:S(2)}) collective-permute-start(bf16[40,64,128]{2,1,0:T(8,128)(2,1)} %get-tuple-element.197), channel_id=1, source_target_pairs={{0,32},{32,64},{64,96},{96,0},{1,33},{33,65},{65,97},{97,1},{2,34}... | collective-permute-start | bytes 1966088 | tf_op jit(solution)/shard_map/ppermute | solution.py:555
  91.0 18.0 %collective-permute-start.8 = (bf16[400,128]{1,0:T(8,128)(2,1)}, bf16[400,128]{1,0:T(8,128)(2,1)}, u32[]{:S(2)}, u32[]{:S(2)}) collective-permute-start(bf16[400,128]{1,0:T(8,128)(2,1)} %get-tuple-element.189), channel_id=1, source_target_pairs={{0,3},{1,0},{2,1},{3,2},{4,7},{5,4},{6,5},{7,6},{8,11},{9,8},{10,9... | collective-permute-start | bytes 307208 | tf_op jit(solution)/shard_map/ppermute | solution.py:555
  111.1 4.9 %collective-permute-start.9 = (bf16[400,128]{1,0:T(8,128)(2,1)}, bf16[400,128]{1,0:T(8,128)(2,1)S(1)}, u32[]{:S(2)}, u32[]{:S(2)}) collective-permute-start(bf16[400,128]{1,0:T(8,128)(2,1)} %mix.1.refs_1_), channel_id=1, source_target_pairs={{0,32},{32,64},{64,96},{96,0},{1,33},{33,65},{65,97},{97,1},{2,34}... | collective-permute-start | bytes 307208 | tf_op jit(solution)/shard_map/ppermute | solution.py:677
  116.0 12.1 %copy-start.6 = (bf16[400,128]{1,0:T(8,128)(2,1)}, bf16[400,128]{1,0:T(8,128)(2,1)S(1)}, u32[]{:S(2)}) copy-start(bf16[400,128]{1,0:T(8,128)(2,1)S(1)} %collective-permute-done.9.refs_2_) | copy-start | bytes 307204
  116.0 7.2 %collective-permute-start.10 = (bf16[400,128]{1,0:T(8,128)(2,1)}, bf16[400,128]{1,0:T(8,128)(2,1)S(1)}, u32[]{:S(2)}, u32[]{:S(2)}) collective-permute-start(bf16[400,128]{1,0:T(8,128)(2,1)} %mix.1.refs_1_), channel_id=1, source_target_pairs={{0,64},{32,96},{64,0},{96,32},{1,65},{33,97},{65,1},{97,33},{2,66}... | collective-permute-start | bytes 307208 | tf_op jit(solution)/shard_map/ppermute | solution.py:677
  123.2 4.9 %copy-start.7 = (bf16[400,128]{1,0:T(8,128)(2,1)}, bf16[400,128]{1,0:T(8,128)(2,1)S(1)}, u32[]{:S(2)}) copy-start(bf16[400,128]{1,0:T(8,128)(2,1)S(1)} %collective-permute-done.10.refs_3_) | copy-start | bytes 307204
  123.2 4.9 %collective-permute-start.11 = (bf16[400,128]{1,0:T(8,128)(2,1)}, bf16[400,128]{1,0:T(8,128)(2,1)S(1)}, u32[]{:S(2)}, u32[]{:S(2)}) collective-permute-start(bf16[400,128]{1,0:T(8,128)(2,1)} %mix.1.refs_1_), channel_id=1, source_target_pairs={{0,96},{32,0},{64,32},{96,64},{1,97},{33,1},{65,33},{97,65},{2,98}... | collective-permute-start | bytes 307208 | tf_op jit(solution)/shard_map/ppermute | solution.py:677
  128.1 0.7 copy-start.8
  131.0 19.6 %copy-start.3 = (bf16[48,1024]{1,0:T(8,128)(2,1)S(1)}, bf16[48,1024]{1,0:T(8,128)(2,1)}, u32[]{:S(2)}) copy-start(bf16[48,1024]{1,0:T(8,128)(2,1)} %final.1) | copy-start | bytes 294916
  131.0 35.2 %collective-permute-start.16 = (bf16[40,64,128]{2,1,0:T(8,128)(2,1)}, bf16[40,64,128]{2,1,0:T(8,128)(2,1)}, u32[]{:S(2)}, u32[]{:S(2)}) collective-permute-start(bf16[40,64,128]{2,1,0:T(8,128)(2,1)} %get-tuple-element.198), channel_id=1, source_target_pairs={{0,64},{32,96},{64,0},{96,32},{1,65},{33,97},{65,1},{97,33},{2,66}... | collective-permute-start | bytes 1966088 | tf_op jit(solution)/shard_map/ppermute | solution.py:555
  139.2 31.2 %collective-permute-start.17 = (bf16[40,64,128]{2,1,0:T(8,128)(2,1)}, bf16[40,64,128]{2,1,0:T(8,128)(2,1)}, u32[]{:S(2)}, u32[]{:S(2)}) collective-permute-start(bf16[40,64,128]{2,1,0:T(8,128)(2,1)} %get-tuple-element.199), channel_id=1, source_target_pairs={{0,96},{32,0},{64,32},{96,64},{1,97},{33,1},{65,33},{97,65},{2,98}... | collective-permute-start | bytes 1966088 | tf_op jit(solution)/shard_map/ppermute | solution.py:555
  142.3 0.9 copy-start.1
  147.2 23.2 %collective-permute-start.21 = (bf16[40,64,128]{2,1,0:T(8,128)(2,1)}, bf16[40,64,128]{2,1,0:T(8,128)(2,1)}, u32[]{:S(2)}, u32[]{:S(2)}) collective-permute-start(bf16[40,64,128]{2,1,0:T(8,128)(2,1)} %get-tuple-element.205), channel_id=1, source_target_pairs={{0,32},{32,64},{64,96},{96,0},{1,33},{33,65},{65,97},{97,1},{2,34}... | collective-permute-start | bytes 1966088 | tf_op jit(solution)/shard_map/ppermute | solution.py:555
  147.2 23.2 %collective-permute-start.22 = (bf16[40,64,128]{2,1,0:T(8,128)(2,1)}, bf16[40,64,128]{2,1,0:T(8,128)(2,1)}, u32[]{:S(2)}, u32[]{:S(2)}) collective-permute-start(bf16[40,64,128]{2,1,0:T(8,128)(2,1)} %get-tuple-element.206), channel_id=1, source_target_pairs={{0,64},{32,96},{64,0},{96,32},{1,65},{33,97},{65,1},{97,33},{2,66}... | collective-permute-start | bytes 1966088 | tf_op jit(solution)/shard_map/ppermute | solution.py:555
  148.7 10.0 %copy-start.12 = (s32[1,4,4,128]{3,1,2,0:T(4,128)S(1)}, s32[1,4,4,128]{3,1,2,0:T(4,128)}, u32[]{:S(2)}) copy-start(s32[1,4,4,128]{3,1,2,0:T(4,128)} %copy.59) | copy-start | bytes 24580
  148.7 12.1 %copy-start.4 = (bf16[4,48,1,128]{3,1,0,2:T(8,128)(2,1)S(1)}, bf16[4,48,1,128]{3,1,0,2:T(8,128)(2,1)}, u32[]{:S(2)}) copy-start(bf16[4,48,1,128]{3,1,0,2:T(8,128)(2,1)} %get-tuple-element.247) | copy-start | bytes 147460
  148.7 12.1 %copy-start.5 = (bf16[4,48,1,128]{3,1,0,2:T(8,128)(2,1)S(1)}, bf16[4,48,1,128]{3,1,0,2:T(8,128)(2,1)}, u32[]{:S(2)}) copy-start(bf16[4,48,1,128]{3,1,0,2:T(8,128)(2,1)} %get-tuple-element.248) | copy-start | bytes 147460
  148.7 35.8 %collective-permute-start.23 = (bf16[40,64,128]{2,1,0:T(8,128)(2,1)}, bf16[40,64,128]{2,1,0:T(8,128)(2,1)}, u32[]{:S(2)}, u32[]{:S(2)}) collective-permute-start(bf16[40,64,128]{2,1,0:T(8,128)(2,1)} %get-tuple-element.207), channel_id=1, source_target_pairs={{0,96},{32,0},{64,32},{96,64},{1,97},{33,1},{65,33},{97,65},{2,98}... | collective-permute-start | bytes 1966088 | tf_op jit(solution)/shard_map/ppermute | solution.py:555
  153.7 30.8 %copy-start.2 = (bf16[40,64,128]{2,1,0:T(8,128)(2,1)S(1)}, bf16[40,64,128]{2,1,0:T(8,128)(2,1)}, u32[]{:S(2)}) copy-start(bf16[40,64,128]{2,1,0:T(8,128)(2,1)} %get-tuple-element.204) | copy-start | bytes 1966084
  153.7 30.8 %copy-start.17 = (s32[4]{0:T(128)S(1)}, s32[4]{0:T(128)}, u32[]{:S(2)}) copy-start(s32[4]{0:T(128)} %copy-done.16) | copy-start | bytes 52
  154.4 11.1 %all-to-all-start.1 = ((bf16[8,48,256]{2,1,0:T(8,128)(2,1)}), bf16[8,48,256]{2,1,0:T(8,128)(2,1)S(1)}, u32[]{:S(2)}, u32[]{:S(2)}) async-start(bf16[8,48,256]{2,1,0:T(8,128)(2,1)} %bitcast.108), calls=%async_computation.1 | async-start | bytes 393216 | tf_op jit(solution)/shard_map/all_to_all | solution.py:685
